TPU v7x, 128 devices: a whole 4x4x4 slice. The times are simulated.
128 devices in a mesh: occi: 8 (over y, z_lo), occj: 16 (over x, z_hi, core).
Axes of the slice: x: 4, y: 4, z: 4 (z_hi: 2, z_lo: 2; z = z_hi * 2 + z_lo), core: 2. Of those that a mesh axis runs over, the one named last changes fastest.
Arguments:
- amplitudes: bfloat16 [16, 16, 512, 512], P('occi', 'occj'), may hold values from -6 to 6
- exch_int: bfloat16 [16, 16, 512, 512], P('occi', 'occj'), may hold values from -6 to 6
- thc_factor: bfloat16 [512, 2048], replicated, may hold values from -0.25 to 0.25
- thc_core: bfloat16 [2048, 2048], replicated, may hold values from -1.5 to 1.5
- fock_vir: bfloat16 [512, 512], replicated, may hold values from -0.25 to 0.25
- eps_vir: float32 [512], replicated, may hold values from 0.5 to 3
- eps_occ: float32 [16], replicated, may hold values from -1.5 to -0.2
- fock_occ: float32 [16, 16], replicated, may hold values from -1.8 to 1.8
- couple_list: int32 [16, 6], replicated, may hold values from 0 to 15, as said below
- couple_count: int32 [16], replicated, may hold values from 1 to 6, as said below
Outputs:
- residual: float32 [16, 16, 512, 512], P('occi', 'occj')
- amplitudes_new: bfloat16 [16, 16, 512, 512], P('occi', 'occj')
Inputs may be any that keep to these rules, and one draw needn't show every extreme that they name: `couple_list`: row j holds 6 distinct orbitals, none of them j. `couple_count`: some row uses all 6 entries.
All inputs are finite; a program needn't handle non-finite values.
Results may differ from a plain program's by a relative error of at most 0.0045.
Values may be sent and summed in bfloat16 or wider, within the bound.
No kernel may reach another device: no remote copies, remote signals or barrier semaphores. Data moves between devices by JAX's collectives and lax.ppermute only.
A program may use at most 128 MiB of HBM per device.

v0:
```python
import jax
import jax.numpy as jnp
from jax import lax
from jax.sharding import PartitionSpec as P


def coupling(fock_occ, couple_list, couple_count):
    n_occ = fock_occ.shape[0]
    slots = jnp.arange(couple_list.shape[1], dtype=jnp.int32)
    active = slots[None, :] < couple_count[:, None]
    target = jnp.arange(n_occ, dtype=jnp.int32)
    hits = (couple_list[:, :, None] == target[None, None, :]) & active[:, :, None]
    return fock_occ * jnp.sum(hits.astype(fock_occ.dtype), axis=1)


def pair_terms(amp_pair, integral, thc_factor, thc_core, fock_vir):
    first = jnp.dot(amp_pair, thc_factor, preferred_element_type=jnp.float32).astype(jnp.bfloat16)
    middle = lax.dot_general(
        thc_factor, first, (((0,), (0,)), ((), ())), preferred_element_type=jnp.float32
    )
    scaled = (thc_core * middle).astype(jnp.bfloat16)
    second = jnp.dot(thc_factor, scaled, preferred_element_type=jnp.float32).astype(jnp.bfloat16)
    ladder = lax.dot_general(
        second, thc_factor, (((1,), (1,)), ((), ())), preferred_element_type=jnp.float32
    )
    virtual = jnp.dot(fock_vir, amp_pair, preferred_element_type=jnp.float32)
    return integral.astype(jnp.float32) + ladder + virtual


def shards(
    amplitudes,
    exch_int,
    thc_factor,
    thc_core,
    fock_vir,
    eps_vir,
    eps_occ,
    fock_occ,
    couple_list,
    couple_count,
):
    rows_i = amplitudes.shape[0]
    virt = amplitudes.shape[2]
    n_first = lax.axis_size("occi")
    n_second = lax.axis_size("occj")
    width = virt // (n_first * n_second)
    first_index = lax.axis_index("occi")
    second_index = lax.axis_index("occj")
    weights = coupling(fock_occ, couple_list, couple_count)
    pairs_here = amplitudes.reshape(rows_i, virt, virt)
    integrals = exch_int.reshape(rows_i, virt, virt)
    row_weights = lax.dynamic_slice_in_dim(weights, second_index, 1, 0)[0]
    empty = jnp.zeros((rows_i, virt, virt), jnp.float32)
    occupied = empty - jnp.einsum(
        "k,skab->sab",
        row_weights,
        lax.all_gather(amplitudes, "occj", axis=1, tiled=True).astype(jnp.float32),
        precision=lax.Precision.HIGHEST,
    )
    half = lax.map(
        lambda pair_in: pair_terms(pair_in[0], pair_in[1], thc_factor, thc_core, fock_vir),
        (pairs_here, integrals),
    )
    half = half + occupied
    spread = lax.all_to_all(
        half.astype(jnp.bfloat16), ("occi", "occj"), split_axis=1, concat_axis=0, tiled=True
    ).astype(half.dtype)
    mirror_part = spread.reshape(n_first, n_second, rows_i, width, virt)
    outgoing = mirror_part.reshape(n_first, n_first, rows_i, rows_i, width, virt)
    outgoing = outgoing.transpose(1, 0, 3, 2, 5, 4).reshape(
        n_first * n_second * rows_i, virt, width
    )
    mirrored = lax.all_to_all(
        outgoing.astype(jnp.bfloat16), ("occi", "occj"), split_axis=0, concat_axis=2, tiled=True
    ).astype(outgoing.dtype)
    residual = half + mirrored
    occ_rows = lax.dynamic_slice_in_dim(eps_occ, first_index * rows_i, rows_i, 0)
    occ_column = lax.dynamic_slice_in_dim(eps_occ, second_index, 1, 0)
    denominator = (
        eps_vir[None, :, None] + eps_vir[None, None, :] - occ_rows[:, None, None] - occ_column[0]
    )
    updated = (pairs_here.astype(jnp.float32) - residual / denominator).astype(jnp.bfloat16)
    return (residual.reshape(rows_i, 1, virt, virt), updated.reshape(rows_i, 1, virt, virt))


def solution(mesh):
    placed = (
        P("occi", "occj", None, None),
        P("occi", "occj", None, None),
        P(),
        P(),
        P(),
        P(),
        P(),
        P(),
        P(),
        P(),
    )
    return jax.shard_map(
        shards,
        mesh=mesh,
        in_specs=placed,
        out_specs=(P("occi", "occj", None, None), P("occi", "occj", None, None)),
        check_vma=False,
    )
```

profile of v0, /device:TPU:1, one launch (start us, length us, event | category | flops | bytes accessed | tf_op | source)
XLA Modules:
  0.0 230.0 jit_solution(6630677729650168291)
XLA Ops:
  7.2 0.7 all-gather.2.cloned.1.call-update
  7.9 2.5 %copy.64 = bf16[2,1,512,512]{2,0,3,1:T(2,128)(2,1)S(1)} copy(bf16[2,1,512,512]{3,2,1,0:T(8,128)(2,1)} %param.12) | data formatting | bytes 2097152 | tf_op args[0]
  10.4 12.6 %copy.66 = bf16[2048,2048]{0,1:T(8,128)(2,1)} copy(bf16[2048,2048]{1,0:T(8,128)(2,1)} %param.15) | data formatting | bytes 16777216 | tf_op jit(solution)/shard_map/while | solution.py:60
  23.1 2.5 %copy.67 = bf16[2,512,512]{2,1,0:T(8,128)(2,1)} copy(bf16[2,512,512]{1,0,2:T(2,128)(2,1)S(1)} %bitcast.100) | data formatting | bytes 2097152 | tf_op jit(solution)/shard_map/while | solution.py:60
  25.7 87.1 %while.11 = (s32[]{:T(128)}, f32[2,512,512]{1,0,2:T(2,128)}, bf16[2,512,512]{2,1,0:T(8,128)(2,1)}, bf16[2048,2048]{0,1:T(8,128)(2,1)}, bf16[2,512,512]{2,1,0:T(8...) while((s32[]{:T(128)}, f32[2,512,512]{1,0,2:T(2,128)}, ...), condition=%wide.region_1.2_spmd.clone, body=%wide.region_0.0_spmd.sunk.clone | while | flops 11021320192 | bytes 47186048 | solution.py:60
  25.7 11.2 %fusion.56 = bf16[2048,2048]{0,1:T(8,128)(2,1)} fusion(bf16[2048,2048]{0,1:T(8,128)(2,1)} %get-tuple-element.178, bf16[512,2048]{1,0:T(8,128)(2,1)} %get-tuple-element.180, bf16[2,512,512]{2,1,0:T(8,128)(2,1)} %get-tuple-element.179, s32[]{:T(128)S(6)} %copy.90), kind=kOutput, calls=%fused_computation.1.clone.1.clone | convolution fusion | flops 5382340608 | bytes 21495812 | tf_op jit(solution)/shard_map/while/body/eval_jaxpr/dot_general | solution.py:18
  37.0 10.3 %convolution_add_fusion.3 = f32[512,512]{1,0:T(8,128)S(1)} fusion(bf16[512,2048]{1,0:T(8,128)(2,1)} %get-tuple-element.180, bf16[2048,2048]{0,1:T(8,128)(2,1)} %fusion.56, bf16[2,512,512]{2,1,0:T(8,128)(2,1)S(1)} %copy-done.7, s32[]{:T(128)S(6)} %copy.90), kind=kOutput, calls=%fused_computation.7.clone.1.clone | convolution fusion | flops 5370281984 | bytes 14155780 | tf_op jit(solution)/shard_map/while/body/eval_jaxpr/dot_general | solution.py:23
  47.3 1.5 fusion.57
  48.8 0.8 copy.86
  49.6 19.6 %dynamic_update_slice.6 = f32[2,512,512]{1,0,2:T(2,128)} dynamic-update-slice(f32[2,512,512]{1,0,2:T(2,128)} %get-tuple-element.169, f32[1,512,512]{1,0,2:T(1,128)S(1)} %copy.86, s32[]{:T(128)S(6)} %copy.90, s32[]{:T(128)} %constant.9.clone.1..sunk.1, s32[]{:T(128)} %constant.9.clone.1..sunk.1) | dynamic-update-slice | bytes 2097156 | tf_op jit(solution)/shard_map/while/body/jit(dynamic_update_index_in_dim)/dynamic_update_slice | solution.py:60
  69.2 11.3 %fusion.56 = bf16[2048,2048]{0,1:T(8,128)(2,1)} fusion(bf16[2048,2048]{0,1:T(8,128)(2,1)} %get-tuple-element.178, bf16[512,2048]{1,0:T(8,128)(2,1)} %get-tuple-element.180, bf16[2,512,512]{2,1,0:T(8,128)(2,1)} %get-tuple-element.179, s32[]{:T(128)S(6)} %copy.90), kind=kOutput, calls=%fused_computation.1.clone.1.clone | convolution fusion | flops 5382340608 | bytes 21495812 | tf_op jit(solution)/shard_map/while/body/eval_jaxpr/dot_general | solution.py:18
  80.5 10.4 %convolution_add_fusion.3 = f32[512,512]{1,0:T(8,128)S(1)} fusion(bf16[512,2048]{1,0:T(8,128)(2,1)} %get-tuple-element.180, bf16[2048,2048]{0,1:T(8,128)(2,1)} %fusion.56, bf16[2,512,512]{2,1,0:T(8,128)(2,1)S(1)} %copy-done.7, s32[]{:T(128)S(6)} %copy.90), kind=kOutput, calls=%fused_computation.7.clone.1.clone | convolution fusion | flops 5370281984 | bytes 14155780 | tf_op jit(solution)/shard_map/while/body/eval_jaxpr/dot_general | solution.py:23
  90.9 1.5 fusion.57
  92.4 0.8 copy.86
  93.2 19.6 %dynamic_update_slice.6 = f32[2,512,512]{1,0,2:T(2,128)} dynamic-update-slice(f32[2,512,512]{1,0,2:T(2,128)} %get-tuple-element.169, f32[1,512,512]{1,0,2:T(1,128)S(1)} %copy.86, s32[]{:T(128)S(6)} %copy.90, s32[]{:T(128)} %constant.9.clone.1..sunk.1, s32[]{:T(128)} %constant.9.clone.1..sunk.1) | dynamic-update-slice | bytes 2097156 | tf_op jit(solution)/shard_map/while/body/jit(dynamic_update_index_in_dim)/dynamic_update_slice | solution.py:60
  112.8 11.6 %all-gather.2.cloned.1.call-done = bf16[2,16,512,512]{3,2,1,0:T(8,128)(2,1)} async-done(((bf16[2,1,512,512]{3,2,1,0:T(8,128)(2,1)}), bf16[2,16,512,512]{3,2,1,0:T(8,128)(2,1)}) %all-gather.2.cloned.1.call-update) | async-done | bytes 16777232 | tf_op jit(solution)/shard_map/all_gather | solution.py:57
  124.4 22.7 %fusion.12 = f32[1,2,512,512]{3,0,2,1:T(1,128)} fusion(bf16[2,16,512,512]{3,2,1,0:T(8,128)(2,1)} %all-gather.2.cloned.1.call-done, f32[16,16]{1,0:T(8,128)S(1)} %convert_reduce_fusion, s32[]{:T(128)S(6)} %select_n.7, f32[16,16]{1,0:T(8,128)} %param.19), kind=kOutput, calls=%fused_computation.14 | convolution fusion | flops 100663312 | bytes 18875396 | tf_op jit(solution)/shard_map/k,skab->sab/dot_general | solution.py:54
  147.1 4.8 %copy.78 = f32[1,2,512,512]{2,1,3,0:T(2,128)S(1)} copy(f32[1,2,512,512]{3,0,2,1:T(1,128)} %fusion.12) | data formatting | bytes 4194304 | tf_op jit(solution)/shard_map/k,skab->sab/dot_general | solution.py:54
  151.9 2.9 %fusion.16 = bf16[2,512,512]{1,0,2:T(2,128)(2,1)S(1)} fusion(f32[2,512,512]{1,0,2:T(2,128)} %get-tuple-element.39, f32[1,2,512,512]{2,1,3,0:T(2,128)S(1)} %copy.78), kind=kLoop, calls=%fused_computation.23 | loop fusion | flops 1572864 | bytes 5242880 | tf_op jit(solution)/shard_map/convert_element_type | solution.py:66
  154.8 3.8 %copy.69 = bf16[2,512,512]{2,0,1:T(2,128)(2,1)} copy(bf16[2,512,512]{1,0,2:T(2,128)(2,1)S(1)} %fusion.16) | data formatting | bytes 2097152 | tf_op jit(solution)/shard_map/convert_element_type | solution.py:66
  158.6 24.4 %all_to_all.8 = bf16[2,512,512]{2,0,1:T(2,128)(2,1)S(1)} all-to-all(bf16[2,512,512]{2,0,1:T(2,128)(2,1)} %copy.69), channel_id=1, replica_groups=mesh['occi'=8,'occj'=16] {'occi','occj'}, dimensions={1} | all-to-all | bytes 2097152 | tf_op jit(solution)/shard_map/all_to_all | solution.py:65
  183.5 1.5 copy.71
  184.9 4.6 %all-to-all-start.1 = ((bf16[256,512,4]{1,2,0:T(4,128)(2,1)}), bf16[256,512,4]{1,2,0:T(4,128)(2,1)S(1)}, u32[]{:S(2)}, u32[]{:S(2)}) async-start(bf16[256,512,4]{1,2,0:T(4,128)(2,1)} %bitcast.103), calls=%async_computation.1 | async-start | bytes 2097152 | tf_op jit(solution)/shard_map/all_to_all | solution.py:73
  189.6 0.6 dynamic_slice.18
  190.3 1.1 broadcast_add_fusion
  191.4 17.3 %all-to-all-done.1 = bf16[256,512,4]{1,2,0:T(4,128)(2,1)S(1)} async-done(((bf16[256,512,4]{1,2,0:T(4,128)(2,1)}), bf16[256,512,4]{1,2,0:T(4,128)(2,1)S(1)}, u32[]{:S(2)}, u32[]{:S(2)}) %all-to-all-start.1) | async-done | bytes 1048608 | tf_op jit(solution)/shard_map/all_to_all | solution.py:73
  208.6 0.6 convert_bitcast_fusion
  209.3 1.1 copy.72
  210.5 0.7 copy-done.3
  211.4 5.2 %fusion.15 = (bf16[2,1,512,512]{2,0,3,1:T(2,128)(2,1)S(1)}, f32[2,512,512]{1,0,2:T(2,128)}) fusion(f32[]{:T(128)} %bitcast.20, f32[2]{0:T(128)S(1)} %dynamic_slice.17, f32[512,512]{0,1:T(8,128)S(1)} %copy-done.4, bf16[2,1,512,512]{2,0,3,1:T(2,128)(2,1)S(1)} %copy-done.2, f32[2,512,128,4]{1,0,3,2:T(2,128)S(1)} %copy.72, f32[2,512,512]{1,0,2:T(2,128)S(1)} %copy-done.3, ...), kind=kLoop, calls=%fused_computation.21 | loop fusion | flops 4718592 | bytes 11534348 | tf_op jit(solution)/shard_map/reshape | solution.py:83
  216.6 4.1 %copy.73 = f32[2,1,512,512]{3,2,1,0:T(8,128)} copy(f32[2,1,512,512]{2,0,3,1:T(2,128)} %bitcast.101) | data formatting | bytes 4194304
  220.7 2.5 %copy.74 = bf16[2,1,512,512]{3,2,1,0:T(8,128)(2,1)} copy(bf16[2,1,512,512]{2,0,3,1:T(2,128)(2,1)S(1)} %get-tuple-element.99) | data formatting | bytes 2097152
  (27 shorter events, 1.0 us)
Async XLA Ops:
  7.2 117.2 %all-gather.2.cloned.1.call-start = ((), (), s32[]{:S(2)}) async-start(), calls=%async_computation.2 | async-start | bytes 17825792 | tf_op jit(solution)/shard_map/all_gather | solution.py:57
  10.4 12.7 %copy-start.1 = (bf16[2,1,512,512]{2,0,3,1:T(2,128)(2,1)}, bf16[2,1,512,512]{2,0,3,1:T(2,128)(2,1)S(1)}, u32[]{:S(2)}) copy-start(bf16[2,1,512,512]{2,0,3,1:T(2,128)(2,1)S(1)} %copy.64) | copy-start | bytes 3145732
  23.1 2.5 %copy-start.8 = (s32[16]{0:T(128)S(1)}, s32[16]{0:T(128)}, u32[]{:S(2)}) copy-start(s32[16]{0:T(128)} %param.21) | copy-start | bytes 196
  23.1 2.5 %copy-start.6 = (s32[16,6]{0,1:T(8,128)S(1)}, s32[16,6]{0,1:T(8,128)}, u32[]{:S(2)}) copy-start(s32[16,6]{0,1:T(8,128)} %param.20) | copy-start | bytes 1156
  23.1 2.6 %copy-start = (bf16[512,512]{1,0:T(8,128)(2,1)S(1)}, bf16[512,512]{1,0:T(8,128)(2,1)}, u32[]{:S(2)}) copy-start(bf16[512,512]{1,0:T(8,128)(2,1)} %param.16) | copy-start | bytes 1572868
  25.7 11.3 %copy-start.7 = (bf16[2,512,512]{2,1,0:T(8,128)(2,1)S(1)}, bf16[2,512,512]{2,1,0:T(8,128)(2,1)}, u32[]{:S(2)}) copy-start(bf16[2,512,512]{2,1,0:T(8,128)(2,1)} %get-tuple-element.177) | copy-start | bytes 3145732 | tf_op jit(solution)/shard_map/while
  69.2 11.3 %copy-start.7 = (bf16[2,512,512]{2,1,0:T(8,128)(2,1)S(1)}, bf16[2,512,512]{2,1,0:T(8,128)(2,1)}, u32[]{:S(2)}) copy-start(bf16[2,512,512]{2,1,0:T(8,128)(2,1)} %get-tuple-element.177) | copy-start | bytes 3145732 | tf_op jit(solution)/shard_map/while
  183.4 6.1 %copy-start.9 = (f32[16]{0:T(128)S(1)}, f32[16]{0:T(128)}, u32[]{:S(2)}) copy-start(f32[16]{0:T(128)} %param.18) | copy-start | bytes 196
  183.4 6.8 %copy-start.5 = (f32[512]{0:T(512)S(1)}, f32[512]{0:T(512)}, u32[]{:S(2)}) copy-start(f32[512]{0:T(512)} %param.17) | copy-start | bytes 6148
  184.9 23.7 %all-to-all-start.1 = ((bf16[256,512,4]{1,2,0:T(4,128)(2,1)}), bf16[256,512,4]{1,2,0:T(4,128)(2,1)S(1)}, u32[]{:S(2)}, u32[]{:S(2)}) async-start(bf16[256,512,4]{1,2,0:T(4,128)(2,1)} %bitcast.103), calls=%async_computation.1 | async-start | bytes 2097152 | tf_op jit(solution)/shard_map/all_to_all | solution.py:73
  209.2 1.2 copy-start.2
  209.2 1.9 copy-start.3
  209.3 2.2 copy-start.4
Sparse Core Ops, SparseCore 0:
  10.5 113.8 all-gather.1
where the time goes:
time: 233 us; the launch traced here: 230 us
  local copies, waits for them, and re-layouts  78.3 us (34%)
  matrix products  69 us (30%)
  waiting for transfers between devices  29.6 us (13%)
  blocking collectives  24.4 us (10%)
  between operations  14.2 us (6%)
  other arithmetic  9.91 us (4%)
  starting transfers between devices  4.64 us (2%)
    dynamic_update_slice x4, local copies, waits for them, and re-layouts, shards(): lax.map(lambda pair_in: pair_terms(pair_in[0], pair_in[1], thc_factor, th...  40.8 us
    all_to_all x1, blocking collectives, shards(): lax.all_to_all(half.astype(jnp.bfloat16), ('occi', 'occj'), split_axis=1,...  24.4 us
    dot_general x1, matrix products, shards(): jnp.einsum('k,skab->sab', row_weights, lax.all_gather(amplitudes, 'occj',...  22.7 us
    dot_general x2, matrix products, pair_terms(): lax.dot_general(thc_factor, first, (((0,), (0,)), ((), ())), preferred_el...  22.5 us
    dot_general x2, matrix products, pair_terms(): lax.dot_general(second, thc_factor, (((1,), (1,)), ((), ())), preferred_e...  20.7 us
    all_to_all x1, waiting for transfers between devices, shards(): lax.all_to_all(outgoing.astype(jnp.bfloat16), ('occi', 'occj'), split_axi...  17.3 us
    while x2, local copies, waits for them, and re-layouts, shards(): lax.map(lambda pair_in: pair_terms(pair_in[0], pair_in[1], thc_factor, th...  15.1 us
    all_gather x1, waiting for transfers between devices, shards(): lax.all_gather(amplitudes, 'occj', axis=1, tiled=True).astype(jnp.float32)  11.6 us
  transfers between devices with their start and end apart: 2, of which 2 were waited for; matrix products, arithmetic and copies ran while one was open for 46% of the time, Pallas kernels for 0%

commit v1 on v0

v1 whole, which is shorter than its diff:
```python
import functools

import jax
import jax.numpy as jnp
from jax import lax
from jax.experimental import pallas as pl
from jax.experimental.pallas import tpu as pltpu
from jax.sharding import PartitionSpec as P

AXES = ("occi", "occj")
F32 = jnp.float32
BF16 = jnp.bfloat16
SUB = 16


def coupling(fock_occ, couple_list, couple_count):
    n_occ = fock_occ.shape[0]
    slots = jnp.arange(couple_list.shape[1], dtype=jnp.int32)
    active = slots[None, :] < couple_count[:, None]
    target = jnp.arange(n_occ, dtype=jnp.int32)
    hits = (couple_list[:, :, None] == target[None, None, :]) & active[:, :, None]
    return fock_occ * jnp.sum(hits.astype(fock_occ.dtype), axis=1)


def params(limit, **kw):
    return pltpu.CompilerParams(vmem_limit_bytes=limit << 20, **kw)


def whole(shape):
    return pl.BlockSpec(shape, lambda *_: (0,) * len(shape))


def pack_kernel(n, place, amp_ref, *outs):
    core, chip = place[0], place[1]
    block = outs[0].shape[0]
    for e in range(n):
        rows = pl.ds(pl.multiple_of((chip ^ (e >> 1)) * block, block), block)
        outs[e][...] = amp_ref[core ^ (e & 1), rows, :]


def pack(place, amps, n):
    _, virt, _ = amps.shape
    block = virt * 2 // n
    return pl.pallas_call(
        functools.partial(pack_kernel, n),
        out_shape=[jax.ShapeDtypeStruct((block, virt), BF16)] * n,
        grid_spec=pltpu.PrefetchScalarGridSpec(
            num_scalar_prefetch=1,
            grid=(1,),
            in_specs=[whole(amps.shape)],
            out_specs=[whole((block, virt))] * n,
        ),
        compiler_params=params(16),
        cost_estimate=pl.CostEstimate(flops=0, bytes_accessed=4 * amps.size, transcendentals=0),
        name="pack",
    )(place, amps)


def mix_kernel(n, w_ref, *refs):
    ins, outs = refs[:n], refs[n:]
    block = ins[0].shape[0]
    w = w_ref[...]
    high = w.astype(BF16)
    rest = w - high.astype(F32)
    mid = rest.astype(BF16)
    low = (rest - mid.astype(F32)).astype(BF16)
    for r in range(0, block, SUB):
        rhs = jnp.concatenate([ref[r : r + SUB, :] for ref in ins], axis=0)
        total = jnp.dot(high, rhs, preferred_element_type=F32)
        total += jnp.dot(mid, rhs, preferred_element_type=F32)
        total += jnp.dot(low, rhs, preferred_element_type=F32)
        for e in range(n):
            outs[e][r : r + SUB, :] = total[e * SUB : (e + 1) * SUB, :].astype(BF16)


def mix(wide, slices):
    n = len(slices)
    shape = slices[0].shape
    return pl.pallas_call(
        functools.partial(mix_kernel, n),
        out_shape=[jax.ShapeDtypeStruct(shape, BF16)] * n,
        grid=(1,),
        in_specs=[whole(wide.shape)] + [whole(shape)] * n,
        out_specs=[whole(shape)] * n,
        compiler_params=params(24),
        cost_estimate=pl.CostEstimate(
            flops=10**9, bytes_accessed=4 * n * shape[0] * shape[1], transcendentals=0
        ),
        name="mix",
    )(wide, *slices)


def ladder_kernel(slot, amp_ref, int_ref, x_ref, xt_ref, core_ref, fock_ref, out_ref, scaled):
    step = pl.program_id(0)
    tile = core_ref.shape[1]
    rank = x_ref.shape[1]
    chunk = min(512, rank)
    amp = amp_ref[...]
    cols = pl.ds(pl.multiple_of(step * tile, tile), tile)
    first = jnp.dot(amp, x_ref[:, cols], preferred_element_type=F32).astype(BF16)
    for p in range(0, rank, chunk):
        middle = jnp.dot(xt_ref[p : p + chunk, :], first, preferred_element_type=F32)
        scaled[p : p + chunk, :] = (core_ref[p : p + chunk, :].astype(F32) * middle).astype(BF16)
    second = jnp.dot(x_ref[...], scaled[...], preferred_element_type=F32).astype(BF16)
    part = jnp.dot(second, xt_ref[cols, :], preferred_element_type=F32)

    @pl.when(step == 0)
    def _():
        virtual = jnp.dot(fock_ref[...], amp, preferred_element_type=F32)
        out_ref[...] = int_ref[...].astype(F32) + virtual + part

    @pl.when(step > 0)
    def _():
        out_ref[...] += part


def ladder(slot, amps, ints, x, xt, core, fock):
    virt, rank = x.shape
    tile = min(512, rank)
    pair = pl.BlockSpec((None, virt, virt), lambda q, s: (s[0], 0, 0))
    return pl.pallas_call(
        ladder_kernel,
        out_shape=jax.ShapeDtypeStruct((virt, virt), F32),
        grid_spec=pltpu.PrefetchScalarGridSpec(
            num_scalar_prefetch=1,
            grid=(rank // tile,),
            in_specs=[
                pair,
                pair,
                whole(x.shape),
                whole(xt.shape),
                pl.BlockSpec((rank, tile), lambda q, s: (0, q)),
                whole(fock.shape),
            ],
            out_specs=whole((virt, virt)),
            scratch_shapes=[pltpu.VMEM((rank, tile), BF16)],
        ),
        compiler_params=params(40, dimension_semantics=("arbitrary",)),
        cost_estimate=pl.CostEstimate(
            flops=4 * virt * rank * (rank + virt) + 2 * virt**3,
            bytes_accessed=2 * rank * rank + 4 * virt * rank,
            transcendentals=0,
        ),
        name="ladder",
    )(slot, amps, ints, x, xt, core, fock)


def half_kernel(n, place, part_ref, *refs):
    slices, (half_ref, send_ref) = refs[:n], refs[n:]
    block = slices[0].shape[0]
    chip = place[1]
    for d in range(n):
        rows = pl.ds(pl.multiple_of((chip ^ d) * block, block), block)
        half = part_ref[rows, :] - slices[d][...].astype(F32)
        half_ref[rows, :] = half
        send_ref[rows, :] = half.astype(BF16)


def half_of(place, part, slices):
    n = len(slices)
    shape = part.shape
    return pl.pallas_call(
        functools.partial(half_kernel, n),
        out_shape=[jax.ShapeDtypeStruct(shape, F32), jax.ShapeDtypeStruct(shape, BF16)],
        grid_spec=pltpu.PrefetchScalarGridSpec(
            num_scalar_prefetch=1,
            grid=(1,),
            in_specs=[whole(shape)] + [whole(slices[0].shape)] * n,
            out_specs=[whole(shape)] * 2,
        ),
        compiler_params=params(16),
        cost_estimate=pl.CostEstimate(flops=0, bytes_accessed=12 * part.size, transcendentals=0),
        name="half",
    )(place, part, *slices)


def finish_kernel(slot, half_ref, mirror_ref, amp_ref, col_ref, row_ref, occ_ref, *refs):
    res_ref, new_ref = refs[-2:]
    residual = half_ref[...] + mirror_ref[...].astype(F32).T
    denominator = col_ref[...] + row_ref[...] - occ_ref[0] - occ_ref[1]
    res_ref[...] = residual
    new_ref[...] = (amp_ref[...].astype(F32) - residual / denominator).astype(BF16)


def finish(slot, half, mirror, amps, eps_col, eps_row, occ, held):
    virt = half.shape[0]
    rows = min(128, virt)
    strip = pl.BlockSpec((None, rows, virt), lambda r, s: (s[0], r, 0))
    held_specs = [pl.BlockSpec(memory_space=pl.ANY)] * len(held)
    return pl.pallas_call(
        finish_kernel,
        out_shape=[
            jax.ShapeDtypeStruct(amps.shape, F32),
            jax.ShapeDtypeStruct(amps.shape, BF16),
        ],
        grid_spec=pltpu.PrefetchScalarGridSpec(
            num_scalar_prefetch=1,
            grid=(virt // rows,),
            in_specs=[
                pl.BlockSpec((rows, virt), lambda r, s: (r, 0)),
                pl.BlockSpec((virt, rows), lambda r, s: (0, r)),
                strip,
                pl.BlockSpec((rows, 1), lambda r, s: (r, 0)),
                whole((1, virt)),
                pl.BlockSpec(memory_space=pltpu.SMEM),
            ]
            + held_specs,
            out_specs=[strip, strip],
        ),
        input_output_aliases={7 + n: n for n in range(len(held))},
        compiler_params=params(16, dimension_semantics=("arbitrary",)),
        cost_estimate=pl.CostEstimate(
            flops=20 * half.size, bytes_accessed=14 * half.size, transcendentals=0
        ),
        name="finish",
    )(slot, half, mirror, amps, eps_col, eps_row, occ, *held)


def shards(
    amplitudes,
    exch_int,
    thc_factor,
    thc_core,
    fock_vir,
    eps_vir,
    eps_occ,
    fock_occ,
    couple_list,
    couple_count,
):
    rows_i, _, virt, _ = amplitudes.shape
    n_first = lax.axis_size("occi")
    n_second = lax.axis_size("occj")
    me_i = lax.axis_index("occi")
    me_j = lax.axis_index("occj")
    core = me_j % 2
    place = jnp.stack([core, me_j // 2]).astype(jnp.int32)
    slot_a = jnp.reshape(core, (1,)).astype(jnp.int32)
    slot_b = 1 - slot_a
    amps = amplitudes.reshape(rows_i, virt, virt)
    ints = exch_int.reshape(rows_i, virt, virt)

    def row_hop(e):
        return [
            (p * n_second + m, p * n_second + (m ^ e))
            for p in range(n_first)
            for m in range(n_second)
        ]

    def mirror_hop(flip):
        return [
            (p * n_second + 2 * q + s, q * n_second + 2 * p + (s ^ flip))
            for p in range(n_first)
            for q in range(n_first)
            for s in range(2)
        ]

    weights = coupling(fock_occ, couple_list, couple_count)
    ids = jnp.arange(n_second, dtype=jnp.int32)
    pick = (ids ^ me_j)[:, None] == ids[None, :]
    weights = jnp.sum(jnp.where(pick[:, :, None], weights[None], 0.0), axis=1)
    weights = jnp.sum(jnp.where(pick[None], weights[:, None, :], 0.0), axis=2)
    tall = jnp.repeat(jnp.repeat(weights, SUB, axis=0), SUB, axis=1)
    lane = jnp.arange(n_second * SUB, dtype=jnp.int32) % SUB
    wide = jnp.where(lane[:, None] == lane[None, :], tall, 0.0)

    slices = pack(place, amps, n_second)
    slices = [slices[0]] + [lax.ppermute(slices[e], AXES, row_hop(e)) for e in range(1, n_second)]
    factor_t = thc_factor.T
    part_a = ladder(slot_a, amps, ints, thc_factor, factor_t, thc_core, fock_vir)
    sums = mix(wide, slices)
    sums = [sums[0]] + [lax.ppermute(sums[e], AXES, row_hop(e)) for e in range(1, n_second)]
    part_b = ladder(slot_b, amps, ints, thc_factor, factor_t, thc_core, fock_vir)
    half_a, send_a = half_of(place, part_a, sums[0::2])
    half_b, send_b = half_of(place, part_b, sums[1::2])
    got_a = lax.ppermute(send_a, AXES, mirror_hop(0))
    got_b = lax.ppermute(send_b, AXES, mirror_hop(1))

    occ_rows = lax.dynamic_slice_in_dim(eps_occ, me_i * rows_i, rows_i, 0)
    occ_column = lax.dynamic_slice_in_dim(eps_occ, me_j, 1, 0)
    occ_a = jnp.stack([jnp.where(core == 0, occ_rows[0], occ_rows[1]), occ_column[0]])
    occ_b = jnp.stack([jnp.where(core == 0, occ_rows[1], occ_rows[0]), occ_column[0]])
    eps_col = eps_vir.reshape(virt, 1)
    eps_row = eps_vir.reshape(1, virt)
    held = finish(slot_a, half_a, got_a, amps, eps_col, eps_row, occ_a, ())
    residual, updated = finish(slot_b, half_b, got_b, amps, eps_col, eps_row, occ_b, held)
    return (
        residual.reshape(rows_i, 1, virt, virt),
        updated.reshape(rows_i, 1, virt, virt),
    )


def solution(mesh):
    pairs = P("occi", "occj", None, None)
    return jax.shard_map(
        shards,
        mesh=mesh,
        in_specs=(pairs, pairs) + (P(),) * 8,
        out_specs=(pairs, pairs),
        check_vma=False,
    )
```

time: 233 us -> 157 us (0.67)
  the two profiles are of different devices: /device:TPU:1 before, /device:TPU:25 now
where the time goes in v1:
time: 157 us; the launch traced here: 156 us
  starting transfers between devices  63 us (40%)
  Pallas kernels  42.2 us (27%)
  waiting for transfers between devices  28.1 us (18%)
  local copies, waits for them, and re-layouts  15.9 us (10%)
  other arithmetic  3.87 us (2%)
  between operations  3.35 us (2%)
    pallas_call x2, Pallas kernels, ladder(): pl.pallas_call(ladder_kernel, out_shape=jax.ShapeDtypeStruct((virt, virt)...  29.1 us
    ppermute x15, starting transfers between devices, shards(): lax.ppermute(slices[e], AXES, row_hop(e))  27.8 us
    ppermute x15, starting transfers between devices, shards(): lax.ppermute(sums[e], AXES, row_hop(e))  27.5 us
    unnamed x51, local copies, waits for them, and re-layouts  14.1 us
    ppermute x1, waiting for transfers between devices, shards(): got_b = lax.ppermute(send_b, AXES, mirror_hop(1))  11.8 us
    ppermute x1, waiting for transfers between devices, shards(): got_a = lax.ppermute(send_a, AXES, mirror_hop(0))  8.84 us
    ppermute x15, waiting for transfers between devices, shards(): lax.ppermute(slices[e], AXES, row_hop(e))  7.43 us
    pallas_call x2, Pallas kernels, finish(): pl.pallas_call(finish_kernel, out_shape=[jax.ShapeDtypeStruct(amps.shape,...  7.07 us
  transfers between devices with their start and end apart: 32, of which 4 were waited for; matrix products, arithmetic and copies ran while one was open for 5% of the time, Pallas kernels for 23%

profile of v1, /device:TPU:25, one launch (start us, length us, event | category | flops | bytes accessed | tf_op | source)
XLA Modules:
  0.0 156.5 jit_solution(5101395919784890376)
XLA Ops:
  0.7 1.2 copy-done
  3.3 3.6 %collective-permute-start.1 = (bf16[64,512]{1,0:T(8,128)(2,1)S(1)}, bf16[64,512]{1,0:T(8,128)(2,1)S(1)}, u32[]{:S(2)}, u32[]{:S(2)}) collective-permute-start(bf16[64,512]{1,0:T(8,128)(2,1)S(1)} %get-tuple-element.44), channel_id=1, source_target_pairs={{0,2},{1,3},{2,0},{3,1},{4,6},{5,7},{6,4},{7,5},{8,10},{9,11},{10,... | collective-permute-start | bytes 196616 | tf_op jit(solution)/shard_map/ppermute | solution.py:268
  11.9 4.0 %collective-permute-start.5 = (bf16[64,512]{1,0:T(8,128)(2,1)S(1)}, bf16[64,512]{1,0:T(8,128)(2,1)S(1)}, u32[]{:S(2)}, u32[]{:S(2)}) collective-permute-start(bf16[64,512]{1,0:T(8,128)(2,1)S(1)} %get-tuple-element.48), channel_id=1, source_target_pairs={{0,6},{1,7},{2,4},{3,5},{4,2},{5,3},{6,0},{7,1},{8,14},{9,15},{10,... | collective-permute-start | bytes 196616 | tf_op jit(solution)/shard_map/ppermute | solution.py:268
  15.9 2.7 %collective-permute-start.7 = (bf16[64,512]{1,0:T(8,128)(2,1)S(1)}, bf16[64,512]{1,0:T(8,128)(2,1)S(1)}, u32[]{:S(2)}, u32[]{:S(2)}) collective-permute-start(bf16[64,512]{1,0:T(8,128)(2,1)S(1)} %get-tuple-element.50), channel_id=1, source_target_pairs={{0,8},{1,9},{2,10},{3,11},{4,12},{5,13},{6,14},{7,15},{8,0},{9,1},... | collective-permute-start | bytes 196616 | tf_op jit(solution)/shard_map/ppermute | solution.py:268
  19.5 5.3 %collective-permute-start.9 = (bf16[64,512]{1,0:T(8,128)(2,1)S(1)}, bf16[64,512]{1,0:T(8,128)(2,1)S(1)}, u32[]{:S(2)}, u32[]{:S(2)}) collective-permute-start(bf16[64,512]{1,0:T(8,128)(2,1)S(1)} %get-tuple-element.52), channel_id=1, source_target_pairs={{0,10},{1,11},{2,8},{3,9},{4,14},{5,15},{6,12},{7,13},{8,2},{9,3},... | collective-permute-start | bytes 196616 | tf_op jit(solution)/shard_map/ppermute | solution.py:268
  24.9 2.4 %collective-permute-start.11 = (bf16[64,512]{1,0:T(8,128)(2,1)S(1)}, bf16[64,512]{1,0:T(8,128)(2,1)S(1)}, u32[]{:S(2)}, u32[]{:S(2)}) collective-permute-start(bf16[64,512]{1,0:T(8,128)(2,1)S(1)} %get-tuple-element.54), channel_id=1, source_target_pairs={{0,12},{1,13},{2,14},{3,15},{4,8},{5,9},{6,10},{7,11},{8,4},{9,5},... | collective-permute-start | bytes 196616 | tf_op jit(solution)/shard_map/ppermute | solution.py:268
  28.2 5.0 %collective-permute-start.13 = (bf16[64,512]{1,0:T(8,128)(2,1)S(1)}, bf16[64,512]{1,0:T(8,128)(2,1)S(1)}, u32[]{:S(2)}, u32[]{:S(2)}) collective-permute-start(bf16[64,512]{1,0:T(8,128)(2,1)S(1)} %get-tuple-element.56), channel_id=1, source_target_pairs={{0,14},{1,15},{2,12},{3,13},{4,10},{5,11},{6,8},{7,9},{8,6},{9,7},... | collective-permute-start | bytes 196616 | tf_op jit(solution)/shard_map/ppermute | solution.py:268
  33.4 3.5 %collective-permute-done.13.refs_14_ = bf16[64,512]{1,0:T(8,128)(2,1)S(1)} collective-permute-done((bf16[64,512]{1,0:T(8,128)(2,1)S(1)}, bf16[64,512]{1,0:T(8,128)(2,1)S(1)}, u32[]{:S(2)}, u32[]{:S(2)}) %collective-permute-start.13) | collective-permute-done | bytes 65568 | tf_op jit(solution)/shard_map/ppermute | solution.py:268
  37.0 3.9 %collective-permute-done.14.refs_15_ = bf16[64,512]{1,0:T(8,128)(2,1)S(1)} collective-permute-done((bf16[64,512]{1,0:T(8,128)(2,1)S(1)}, bf16[64,512]{1,0:T(8,128)(2,1)S(1)}, u32[]{:S(2)}, u32[]{:S(2)}) %collective-permute-start.14) | collective-permute-done | bytes 65568 | tf_op jit(solution)/shard_map/ppermute | solution.py:268
  40.8 1.6 %mix.1 = (bf16[64,512]{1,0:T(8,128)(2,1)S(1)}, bf16[64,512]{1,0:T(8,128)(2,1)S(1)}, bf16[64,512]{1,0:T(8,128)(2,1)S(1)}, bf16[64,512]{1,0:T(8,128)(2,1)S(1)}, bf...) custom-call(f32[256,256]{1,0:T(8,128)S(1)} %compare_select_fusion.w_, ...), custom_call_target="tpu_custom_call" | custom-call | flops 1000000000 | bytes 2097152 | tf_op jit(solution)/shard_map/mix/pallas_call | solution.py:79
  48.1 4.1 %collective-permute-start.26 = (bf16[64,512]{1,0:T(8,128)(2,1)}, bf16[64,512]{1,0:T(8,128)(2,1)S(1)}, u32[]{:S(2)}, u32[]{:S(2)}) collective-permute-start(bf16[64,512]{1,0:T(8,128)(2,1)} %get-tuple-element.71), channel_id=1, source_target_pairs={{0,6},{1,7},{2,4},{3,5},{4,2},{5,3},{6,0},{7,1},{8,14},{9,15},{10,... | collective-permute-start | bytes 196616 | tf_op jit(solution)/shard_map/ppermute | solution.py:272
  52.2 2.7 %collective-permute-start.28 = (bf16[64,512]{1,0:T(8,128)(2,1)}, bf16[64,512]{1,0:T(8,128)(2,1)S(1)}, u32[]{:S(2)}, u32[]{:S(2)}) collective-permute-start(bf16[64,512]{1,0:T(8,128)(2,1)} %get-tuple-element.73), channel_id=1, source_target_pairs={{0,10},{1,11},{2,8},{3,9},{4,14},{5,15},{6,12},{7,13},{8,2},{9,3},... | collective-permute-start | bytes 196616 | tf_op jit(solution)/shard_map/ppermute | solution.py:272
  54.9 1.5 collective-permute-start.29
  56.4 2.5 %copy.25 = bf16[512,2048]{0,1:T(8,128)(2,1)} copy(bf16[512,2048]{1,0:T(8,128)(2,1)S(1)} %copy-done.2) | data formatting | bytes 4194304 | tf_op args[2]
  58.9 1.9 %collective-permute-start.15 = (bf16[64,512]{1,0:T(8,128)(2,1)}, bf16[64,512]{1,0:T(8,128)(2,1)S(1)}, u32[]{:S(2)}, u32[]{:S(2)}) collective-permute-start(bf16[64,512]{1,0:T(8,128)(2,1)} %copy-done.22), channel_id=1, source_target_pairs={{0,1},{1,0},{2,3},{3,2},{4,5},{5,4},{6,7},{7,6},{8,9},{9,8},{10,11... | collective-permute-start | bytes 196616 | tf_op jit(solution)/shard_map/ppermute | solution.py:272
  60.8 1.8 %collective-permute-start.16 = (bf16[64,512]{1,0:T(8,128)(2,1)}, bf16[64,512]{1,0:T(8,128)(2,1)S(1)}, u32[]{:S(2)}, u32[]{:S(2)}) collective-permute-start(bf16[64,512]{1,0:T(8,128)(2,1)} %copy-done.21), channel_id=1, source_target_pairs={{0,3},{1,2},{2,1},{3,0},{4,7},{5,6},{6,5},{7,4},{8,11},{9,10},{10,... | collective-permute-start | bytes 196616 | tf_op jit(solution)/shard_map/ppermute | solution.py:272
  62.6 2.6 %collective-permute-start.18 = (bf16[64,512]{1,0:T(8,128)(2,1)}, bf16[64,512]{1,0:T(8,128)(2,1)S(1)}, u32[]{:S(2)}, u32[]{:S(2)}) collective-permute-start(bf16[64,512]{1,0:T(8,128)(2,1)} %copy-done.19), channel_id=1, source_target_pairs={{0,7},{1,6},{2,5},{3,4},{4,3},{5,2},{6,1},{7,0},{8,15},{9,14},{10,... | collective-permute-start | bytes 196616 | tf_op jit(solution)/shard_map/ppermute | solution.py:272
  65.2 4.0 %collective-permute-start.30 = (bf16[64,512]{1,0:T(8,128)(2,1)}, bf16[64,512]{1,0:T(8,128)(2,1)S(1)}, u32[]{:S(2)}, u32[]{:S(2)}) collective-permute-start(bf16[64,512]{1,0:T(8,128)(2,1)} %copy-done.23), channel_id=1, source_target_pairs={{0,14},{1,15},{2,12},{3,13},{4,10},{5,11},{6,8},{7,9},{8,6},{9,7},... | collective-permute-start | bytes 196616 | tf_op jit(solution)/shard_map/ppermute | solution.py:272
  69.2 1.6 %copy-done.3 = bf16[512,2048]{0,1:T(8,128)(2,1)S(1)} copy-done((bf16[512,2048]{0,1:T(8,128)(2,1)S(1)}, bf16[512,2048]{0,1:T(8,128)(2,1)}, u32[]{:S(2)}) %copy-start.3) | copy-done | bytes 2097176
  73.1 14.6 %ladder.3.part_ref = f32[512,512]{1,0:T(8,128)S(1)} custom-call(s32[1]{0:T(128)} %bitcast.slot, bf16[2,512,512]{2,1,0:T(8,128)(2,1)S(1)} %bitcast.21, bf16[2,512,512]{2,1,0:T(8,128)(2,1)S(1)} %bitcast.30, bf16[512,2048]{1,0:T(8,128)(2,1)S(1)} %copy-done.2, bf16[2048,512]{1,0:T(8,128)(2,1)S(1)} %bitcast.25, bf16[2048,2048]{1,0:T(8,128)(2,1)} %core_ref.3, ...), custom_call_target="tpu_custom_call" | custom-call | flops 11005853696 | bytes 12582912 | tf_op jit(solution)/shard_map/ladder/pallas_call | solution.py:121
  88.0 2.3 %half.3 = (f32[512,512]{1,0:T(8,128)S(1)}, bf16[512,512]{1,0:T(8,128)(2,1)}) custom-call(s32[2]{0:T(128)S(1)} %pad_add_fusion.place, f32[512,512]{1,0:T(8,128)S(1)} %ladder.3.part_ref, bf16[64,512]{1,0:T(8,128)(2,1)S(1)} %get-tuple-element.68.refs_0_, bf16[64,512]{1,0:T(8,128)(2,1)S(1)} %collective-permute-done.24.refs_1_, ...), custom_call_target="tpu_custom_call" | custom-call | bytes 3145728 | tf_op jit(solution)/shard_map/half/pallas_call | solution.py:162
  91.3 3.1 %collective-permute-start.20 = (bf16[64,512]{1,0:T(8,128)(2,1)S(1)}, bf16[64,512]{1,0:T(8,128)(2,1)S(1)}, u32[]{:S(2)}, u32[]{:S(2)}) collective-permute-start(bf16[64,512]{1,0:T(8,128)(2,1)S(1)} %copy-done.16), channel_id=1, source_target_pairs={{0,11},{1,10},{2,9},{3,8},{4,15},{5,14},{6,13},{7,12},{8,3},{9,2},... | collective-permute-start | bytes 196616 | tf_op jit(solution)/shard_map/ppermute | solution.py:272
  94.4 1.8 %collective-permute-start.21 = (bf16[64,512]{1,0:T(8,128)(2,1)S(1)}, bf16[64,512]{1,0:T(8,128)(2,1)S(1)}, u32[]{:S(2)}, u32[]{:S(2)}) collective-permute-start(bf16[64,512]{1,0:T(8,128)(2,1)S(1)} %copy-done.14), channel_id=1, source_target_pairs={{0,13},{1,12},{2,15},{3,14},{4,9},{5,8},{6,11},{7,10},{8,5},{9,4},... | collective-permute-start | bytes 196616 | tf_op jit(solution)/shard_map/ppermute | solution.py:272
  96.2 3.7 %collective-permute-start.22 = (bf16[64,512]{1,0:T(8,128)(2,1)S(1)}, bf16[64,512]{1,0:T(8,128)(2,1)S(1)}, u32[]{:S(2)}, u32[]{:S(2)}) collective-permute-start(bf16[64,512]{1,0:T(8,128)(2,1)S(1)} %copy-done.12), channel_id=1, source_target_pairs={{0,15},{1,14},{2,13},{3,12},{4,11},{5,10},{6,9},{7,8},{8,7},{9,6},... | collective-permute-start | bytes 196616 | tf_op jit(solution)/shard_map/ppermute | solution.py:272
  99.9 2.1 %collective-permute-start.31 = (bf16[512,512]{1,0:T(8,128)(2,1)}, bf16[512,512]{1,0:T(8,128)(2,1)}, u32[]{:S(2)}, u32[]{:S(2)}) collective-permute-start(bf16[512,512]{1,0:T(8,128)(2,1)} %get-tuple-element.77), channel_id=1, source_target_pairs={{0,0},{1,1},{2,16},{3,17},{4,32},{5,33},{6,48},{7,49},{8,64},{9,65... | collective-permute-start | bytes 1572872 | tf_op jit(solution)/shard_map/ppermute | solution.py:276
  102.1 14.5 %ladder.2.part_ref = f32[512,512]{1,0:T(8,128)S(1)} custom-call(s32[1]{0:T(128)S(6)} %sub.7.slot, bf16[2,512,512]{2,1,0:T(8,128)(2,1)S(1)} %bitcast.22, bf16[2,512,512]{2,1,0:T(8,128)(2,1)S(1)} %bitcast.31, bf16[512,2048]{1,0:T(8,128)(2,1)S(1)} %copy-done.2, bf16[2048,512]{1,0:T(8,128)(2,1)S(1)} %bitcast.26, bf16[2048,2048]{1,0:T(8,128)(2,1)} %core_ref.3, ...), custom_call_target="tpu_custom_call" | custom-call | flops 11005853696 | bytes 12582912 | tf_op jit(solution)/shard_map/ladder/pallas_call | solution.py:121
  116.6 1.5 half.2
  118.1 5.6 %collective-permute-start.23 = (bf16[512,512]{1,0:T(8,128)(2,1)}, bf16[512,512]{1,0:T(8,128)(2,1)}, u32[]{:S(2)}, u32[]{:S(2)}) collective-permute-start(bf16[512,512]{1,0:T(8,128)(2,1)} %get-tuple-element.67), channel_id=1, source_target_pairs={{0,1},{1,0},{2,17},{3,16},{4,33},{5,32},{6,49},{7,48},{8,65},{9,64... | collective-permute-start | bytes 1572872 | tf_op jit(solution)/shard_map/ppermute | solution.py:277
  128.7 8.8 %collective-permute-done.31.mirror_ref = bf16[512,512]{1,0:T(8,128)(2,1)} collective-permute-done((bf16[512,512]{1,0:T(8,128)(2,1)}, bf16[512,512]{1,0:T(8,128)(2,1)}, u32[]{:S(2)}, u32[]{:S(2)}) %collective-permute-start.31) | collective-permute-done | bytes 524320 | tf_op jit(solution)/shard_map/ppermute | solution.py:276
  137.6 3.5 %finish.2 = (f32[2,512,512]{2,1,0:T(8,128)}, bf16[2,512,512]{2,1,0:T(8,128)(2,1)}) custom-call(s32[1]{0:T(128)} %bitcast.slot, f32[512,512]{1,0:T(8,128)S(1)} %copy-done.6, bf16[512,512]{1,0:T(8,128)(2,1)} %collective-permute-done.31.mirror_ref, bf16[2,512,512]{2,1,0:T(8,128)(2,1)S(1)} %bitcast.23, f32[512,1]{1,0:T(8,128)S(1)} %copy.29.col_ref, ...), custom_call_target="tpu_custom_call" | custom-call | flops 5242880 | bytes 3670016 | tf_op jit(solution)/shard_map/finish/pallas_call | solution.py:190
  141.1 11.8 %collective-permute-done.23.mirror_ref = bf16[512,512]{1,0:T(8,128)(2,1)} collective-permute-done((bf16[512,512]{1,0:T(8,128)(2,1)}, bf16[512,512]{1,0:T(8,128)(2,1)}, u32[]{:S(2)}, u32[]{:S(2)}) %collective-permute-start.23) | collective-permute-done | bytes 524320 | tf_op jit(solution)/shard_map/ppermute | solution.py:277
  152.9 3.5 %finish.3 = (f32[2,512,512]{2,1,0:T(8,128)}, bf16[2,512,512]{2,1,0:T(8,128)(2,1)}) custom-call(s32[1]{0:T(128)S(6)} %sub.7.slot, f32[512,512]{1,0:T(8,128)S(1)} %get-tuple-element.66.half_ref, bf16[512,512]{1,0:T(8,128)(2,1)} %collective-permute-done.23.mirror_ref, bf16[2,512,512]{2,1,0:T(8,128)(2,1)S(1)} %bitcast.24, ...), custom_call_target="tpu_custom_call", output_to_operand_aliasing={{0}: (7, {}), {1}: (8, {})} | custom-call | flops 5242880 | bytes 3670016 | tf_op jit(solution)/shard_map/finish/pallas_call | solution.py:190
  (111 shorter events, 20.3 us)
Async XLA Ops:
  2.6 9.3 %collective-permute-start = (bf16[64,512]{1,0:T(8,128)(2,1)S(1)}, bf16[64,512]{1,0:T(8,128)(2,1)S(1)}, u32[]{:S(2)}, u32[]{:S(2)}) collective-permute-start(bf16[64,512]{1,0:T(8,128)(2,1)S(1)} %get-tuple-element.43), channel_id=1, source_target_pairs={{0,1},{1,0},{2,3},{3,2},{4,5},{5,4},{6,7},{7,6},{8,9},{9,8},{10,11... | collective-permute-start | bytes 196616 | tf_op jit(solution)/shard_map/ppermute | solution.py:268
  3.3 12.5 %collective-permute-start.1 = (bf16[64,512]{1,0:T(8,128)(2,1)S(1)}, bf16[64,512]{1,0:T(8,128)(2,1)S(1)}, u32[]{:S(2)}, u32[]{:S(2)}) collective-permute-start(bf16[64,512]{1,0:T(8,128)(2,1)S(1)} %get-tuple-element.44), channel_id=1, source_target_pairs={{0,2},{1,3},{2,0},{3,1},{4,6},{5,7},{6,4},{7,5},{8,10},{9,11},{10,... | collective-permute-start | bytes 196616 | tf_op jit(solution)/shard_map/ppermute | solution.py:268
  6.9 9.0 %collective-permute-start.2 = (bf16[64,512]{1,0:T(8,128)(2,1)S(1)}, bf16[64,512]{1,0:T(8,128)(2,1)S(1)}, u32[]{:S(2)}, u32[]{:S(2)}) collective-permute-start(bf16[64,512]{1,0:T(8,128)(2,1)S(1)} %get-tuple-element.45), channel_id=1, source_target_pairs={{0,3},{1,2},{2,1},{3,0},{4,7},{5,6},{6,5},{7,4},{8,11},{9,10},{10,... | collective-permute-start | bytes 196616 | tf_op jit(solution)/shard_map/ppermute | solution.py:268
  7.0 11.6 %collective-permute-start.3 = (bf16[64,512]{1,0:T(8,128)(2,1)S(1)}, bf16[64,512]{1,0:T(8,128)(2,1)S(1)}, u32[]{:S(2)}, u32[]{:S(2)}) collective-permute-start(bf16[64,512]{1,0:T(8,128)(2,1)S(1)} %get-tuple-element.46), channel_id=1, source_target_pairs={{0,4},{1,5},{2,6},{3,7},{4,0},{5,1},{6,2},{7,3},{8,12},{9,13},{10,... | collective-permute-start | bytes 196616 | tf_op jit(solution)/shard_map/ppermute | solution.py:268
  8.2 11.3 %collective-permute-start.4 = (bf16[64,512]{1,0:T(8,128)(2,1)S(1)}, bf16[64,512]{1,0:T(8,128)(2,1)S(1)}, u32[]{:S(2)}, u32[]{:S(2)}) collective-permute-start(bf16[64,512]{1,0:T(8,128)(2,1)S(1)} %get-tuple-element.47), channel_id=1, source_target_pairs={{0,5},{1,4},{2,7},{3,6},{4,1},{5,0},{6,3},{7,2},{8,13},{9,12},{10,... | collective-permute-start | bytes 196616 | tf_op jit(solution)/shard_map/ppermute | solution.py:268
  11.9 12.9 %collective-permute-start.5 = (bf16[64,512]{1,0:T(8,128)(2,1)S(1)}, bf16[64,512]{1,0:T(8,128)(2,1)S(1)}, u32[]{:S(2)}, u32[]{:S(2)}) collective-permute-start(bf16[64,512]{1,0:T(8,128)(2,1)S(1)} %get-tuple-element.48), channel_id=1, source_target_pairs={{0,6},{1,7},{2,4},{3,5},{4,2},{5,3},{6,0},{7,1},{8,14},{9,15},{10,... | collective-permute-start | bytes 196616 | tf_op jit(solution)/shard_map/ppermute | solution.py:268
  15.9 9.0 %collective-permute-start.6 = (bf16[64,512]{1,0:T(8,128)(2,1)S(1)}, bf16[64,512]{1,0:T(8,128)(2,1)S(1)}, u32[]{:S(2)}, u32[]{:S(2)}) collective-permute-start(bf16[64,512]{1,0:T(8,128)(2,1)S(1)} %get-tuple-element.49), channel_id=1, source_target_pairs={{0,7},{1,6},{2,5},{3,4},{4,3},{5,2},{6,1},{7,0},{8,15},{9,14},{10,... | collective-permute-start | bytes 196616 | tf_op jit(solution)/shard_map/ppermute | solution.py:268
  15.9 11.4 %collective-permute-start.7 = (bf16[64,512]{1,0:T(8,128)(2,1)S(1)}, bf16[64,512]{1,0:T(8,128)(2,1)S(1)}, u32[]{:S(2)}, u32[]{:S(2)}) collective-permute-start(bf16[64,512]{1,0:T(8,128)(2,1)S(1)} %get-tuple-element.50), channel_id=1, source_target_pairs={{0,8},{1,9},{2,10},{3,11},{4,12},{5,13},{6,14},{7,15},{8,0},{9,1},... | collective-permute-start | bytes 196616 | tf_op jit(solution)/shard_map/ppermute | solution.py:268
  18.6 9.5 %collective-permute-start.8 = (bf16[64,512]{1,0:T(8,128)(2,1)S(1)}, bf16[64,512]{1,0:T(8,128)(2,1)S(1)}, u32[]{:S(2)}, u32[]{:S(2)}) collective-permute-start(bf16[64,512]{1,0:T(8,128)(2,1)S(1)} %get-tuple-element.51), channel_id=1, source_target_pairs={{0,9},{1,8},{2,11},{3,10},{4,13},{5,12},{6,15},{7,14},{8,1},{9,0},... | collective-permute-start | bytes 196616 | tf_op jit(solution)/shard_map/ppermute | solution.py:268
  19.5 13.7 %collective-permute-start.9 = (bf16[64,512]{1,0:T(8,128)(2,1)S(1)}, bf16[64,512]{1,0:T(8,128)(2,1)S(1)}, u32[]{:S(2)}, u32[]{:S(2)}) collective-permute-start(bf16[64,512]{1,0:T(8,128)(2,1)S(1)} %get-tuple-element.52), channel_id=1, source_target_pairs={{0,10},{1,11},{2,8},{3,9},{4,14},{5,15},{6,12},{7,13},{8,2},{9,3},... | collective-permute-start | bytes 196616 | tf_op jit(solution)/shard_map/ppermute | solution.py:268
  24.8 8.6 %collective-permute-start.10 = (bf16[64,512]{1,0:T(8,128)(2,1)S(1)}, bf16[64,512]{1,0:T(8,128)(2,1)S(1)}, u32[]{:S(2)}, u32[]{:S(2)}) collective-permute-start(bf16[64,512]{1,0:T(8,128)(2,1)S(1)} %get-tuple-element.53), channel_id=1, source_target_pairs={{0,11},{1,10},{2,9},{3,8},{4,15},{5,14},{6,13},{7,12},{8,3},{9,2},... | collective-permute-start | bytes 196616 | tf_op jit(solution)/shard_map/ppermute | solution.py:268
  24.9 8.5 %collective-permute-start.11 = (bf16[64,512]{1,0:T(8,128)(2,1)S(1)}, bf16[64,512]{1,0:T(8,128)(2,1)S(1)}, u32[]{:S(2)}, u32[]{:S(2)}) collective-permute-start(bf16[64,512]{1,0:T(8,128)(2,1)S(1)} %get-tuple-element.54), channel_id=1, source_target_pairs={{0,12},{1,13},{2,14},{3,15},{4,8},{5,9},{6,10},{7,11},{8,4},{9,5},... | collective-permute-start | bytes 196616 | tf_op jit(solution)/shard_map/ppermute | solution.py:268
  27.3 6.1 %collective-permute-start.12 = (bf16[64,512]{1,0:T(8,128)(2,1)S(1)}, bf16[64,512]{1,0:T(8,128)(2,1)S(1)}, u32[]{:S(2)}, u32[]{:S(2)}) collective-permute-start(bf16[64,512]{1,0:T(8,128)(2,1)S(1)} %get-tuple-element.55), channel_id=1, source_target_pairs={{0,13},{1,12},{2,15},{3,14},{4,9},{5,8},{6,11},{7,10},{8,5},{9,4},... | collective-permute-start | bytes 196616 | tf_op jit(solution)/shard_map/ppermute | solution.py:268
  28.2 8.8 %collective-permute-start.13 = (bf16[64,512]{1,0:T(8,128)(2,1)S(1)}, bf16[64,512]{1,0:T(8,128)(2,1)S(1)}, u32[]{:S(2)}, u32[]{:S(2)}) collective-permute-start(bf16[64,512]{1,0:T(8,128)(2,1)S(1)} %get-tuple-element.56), channel_id=1, source_target_pairs={{0,14},{1,15},{2,12},{3,13},{4,10},{5,11},{6,8},{7,9},{8,6},{9,7},... | collective-permute-start | bytes 196616 | tf_op jit(solution)/shard_map/ppermute | solution.py:268
  33.2 7.7 %collective-permute-start.14 = (bf16[64,512]{1,0:T(8,128)(2,1)S(1)}, bf16[64,512]{1,0:T(8,128)(2,1)S(1)}, u32[]{:S(2)}, u32[]{:S(2)}) collective-permute-start(bf16[64,512]{1,0:T(8,128)(2,1)S(1)} %get-tuple-element.57), channel_id=1, source_target_pairs={{0,15},{1,14},{2,13},{3,12},{4,11},{5,10},{6,9},{7,8},{8,7},{9,6},... | collective-permute-start | bytes 196616 | tf_op jit(solution)/shard_map/ppermute | solution.py:268
  48.0 6.8 %collective-permute-start.24 = (bf16[64,512]{1,0:T(8,128)(2,1)S(1)}, bf16[64,512]{1,0:T(8,128)(2,1)S(1)}, u32[]{:S(2)}, u32[]{:S(2)}) collective-permute-start(bf16[64,512]{1,0:T(8,128)(2,1)S(1)} %get-tuple-element.69), channel_id=1, source_target_pairs={{0,2},{1,3},{2,0},{3,1},{4,6},{5,7},{6,4},{7,5},{8,10},{9,11},{10,... | collective-permute-start | bytes 196616 | tf_op jit(solution)/shard_map/ppermute | solution.py:272
  48.1 10.8 %collective-permute-start.25 = (bf16[64,512]{1,0:T(8,128)(2,1)}, bf16[64,512]{1,0:T(8,128)(2,1)S(1)}, u32[]{:S(2)}, u32[]{:S(2)}) collective-permute-start(bf16[64,512]{1,0:T(8,128)(2,1)} %get-tuple-element.70), channel_id=1, source_target_pairs={{0,4},{1,5},{2,6},{3,7},{4,0},{5,1},{6,2},{7,3},{8,12},{9,13},{10,... | collective-permute-start | bytes 196616 | tf_op jit(solution)/shard_map/ppermute | solution.py:272
  48.1 12.7 %collective-permute-start.26 = (bf16[64,512]{1,0:T(8,128)(2,1)}, bf16[64,512]{1,0:T(8,128)(2,1)S(1)}, u32[]{:S(2)}, u32[]{:S(2)}) collective-permute-start(bf16[64,512]{1,0:T(8,128)(2,1)} %get-tuple-element.71), channel_id=1, source_target_pairs={{0,6},{1,7},{2,4},{3,5},{4,2},{5,3},{6,0},{7,1},{8,14},{9,15},{10,... | collective-permute-start | bytes 196616 | tf_op jit(solution)/shard_map/ppermute | solution.py:272
  52.2 10.4 %collective-permute-start.27 = (bf16[64,512]{1,0:T(8,128)(2,1)}, bf16[64,512]{1,0:T(8,128)(2,1)S(1)}, u32[]{:S(2)}, u32[]{:S(2)}) collective-permute-start(bf16[64,512]{1,0:T(8,128)(2,1)} %get-tuple-element.72), channel_id=1, source_target_pairs={{0,8},{1,9},{2,10},{3,11},{4,12},{5,13},{6,14},{7,15},{8,0},{9,1},... | collective-permute-start | bytes 196616 | tf_op jit(solution)/shard_map/ppermute | solution.py:272
  52.2 10.4 %collective-permute-start.28 = (bf16[64,512]{1,0:T(8,128)(2,1)}, bf16[64,512]{1,0:T(8,128)(2,1)S(1)}, u32[]{:S(2)}, u32[]{:S(2)}) collective-permute-start(bf16[64,512]{1,0:T(8,128)(2,1)} %get-tuple-element.73), channel_id=1, source_target_pairs={{0,10},{1,11},{2,8},{3,9},{4,14},{5,15},{6,12},{7,13},{8,2},{9,3},... | collective-permute-start | bytes 196616 | tf_op jit(solution)/shard_map/ppermute | solution.py:272
  54.9 10.3 %collective-permute-start.29 = (bf16[64,512]{1,0:T(8,128)(2,1)}, bf16[64,512]{1,0:T(8,128)(2,1)}, u32[]{:S(2)}, u32[]{:S(2)}) collective-permute-start(bf16[64,512]{1,0:T(8,128)(2,1)} %get-tuple-element.74), channel_id=1, source_target_pairs={{0,12},{1,13},{2,14},{3,15},{4,8},{5,9},{6,10},{7,11},{8,4},{9,5},... | collective-permute-start | bytes 196616 | tf_op jit(solution)/shard_map/ppermute | solution.py:272
  58.9 32.4 %collective-permute-start.15 = (bf16[64,512]{1,0:T(8,128)(2,1)}, bf16[64,512]{1,0:T(8,128)(2,1)S(1)}, u32[]{:S(2)}, u32[]{:S(2)}) collective-permute-start(bf16[64,512]{1,0:T(8,128)(2,1)} %copy-done.22), channel_id=1, source_target_pairs={{0,1},{1,0},{2,3},{3,2},{4,5},{5,4},{6,7},{7,6},{8,9},{9,8},{10,11... | collective-permute-start | bytes 196616 | tf_op jit(solution)/shard_map/ppermute | solution.py:272
  60.8 33.6 %collective-permute-start.16 = (bf16[64,512]{1,0:T(8,128)(2,1)}, bf16[64,512]{1,0:T(8,128)(2,1)S(1)}, u32[]{:S(2)}, u32[]{:S(2)}) collective-permute-start(bf16[64,512]{1,0:T(8,128)(2,1)} %copy-done.21), channel_id=1, source_target_pairs={{0,3},{1,2},{2,1},{3,0},{4,7},{5,6},{6,5},{7,4},{8,11},{9,10},{10,... | collective-permute-start | bytes 196616 | tf_op jit(solution)/shard_map/ppermute | solution.py:272
  62.6 33.6 %collective-permute-start.17 = (bf16[64,512]{1,0:T(8,128)(2,1)}, bf16[64,512]{1,0:T(8,128)(2,1)S(1)}, u32[]{:S(2)}, u32[]{:S(2)}) collective-permute-start(bf16[64,512]{1,0:T(8,128)(2,1)} %copy-done.20), channel_id=1, source_target_pairs={{0,5},{1,4},{2,7},{3,6},{4,1},{5,0},{6,3},{7,2},{8,13},{9,12},{10,... | collective-permute-start | bytes 196616 | tf_op jit(solution)/shard_map/ppermute | solution.py:272
  62.6 37.3 %collective-permute-start.18 = (bf16[64,512]{1,0:T(8,128)(2,1)}, bf16[64,512]{1,0:T(8,128)(2,1)S(1)}, u32[]{:S(2)}, u32[]{:S(2)}) collective-permute-start(bf16[64,512]{1,0:T(8,128)(2,1)} %copy-done.19), channel_id=1, source_target_pairs={{0,7},{1,6},{2,5},{3,4},{4,3},{5,2},{6,1},{7,0},{8,15},{9,14},{10,... | collective-permute-start | bytes 196616 | tf_op jit(solution)/shard_map/ppermute | solution.py:272
  65.2 22.6 %collective-permute-start.30 = (bf16[64,512]{1,0:T(8,128)(2,1)}, bf16[64,512]{1,0:T(8,128)(2,1)S(1)}, u32[]{:S(2)}, u32[]{:S(2)}) collective-permute-start(bf16[64,512]{1,0:T(8,128)(2,1)} %copy-done.23), channel_id=1, source_target_pairs={{0,14},{1,15},{2,12},{3,13},{4,10},{5,11},{6,8},{7,9},{8,6},{9,7},... | collective-permute-start | bytes 196616 | tf_op jit(solution)/shard_map/ppermute | solution.py:272
  87.8 28.8 %collective-permute-start.19 = (bf16[64,512]{1,0:T(8,128)(2,1)S(1)}, bf16[64,512]{1,0:T(8,128)(2,1)S(1)}, u32[]{:S(2)}, u32[]{:S(2)}) collective-permute-start(bf16[64,512]{1,0:T(8,128)(2,1)S(1)} %copy-done.18), channel_id=1, source_target_pairs={{0,9},{1,8},{2,11},{3,10},{4,13},{5,12},{6,15},{7,14},{8,1},{9,0},... | collective-permute-start | bytes 196616 | tf_op jit(solution)/shard_map/ppermute | solution.py:272
  91.3 25.3 %collective-permute-start.20 = (bf16[64,512]{1,0:T(8,128)(2,1)S(1)}, bf16[64,512]{1,0:T(8,128)(2,1)S(1)}, u32[]{:S(2)}, u32[]{:S(2)}) collective-permute-start(bf16[64,512]{1,0:T(8,128)(2,1)S(1)} %copy-done.16), channel_id=1, source_target_pairs={{0,11},{1,10},{2,9},{3,8},{4,15},{5,14},{6,13},{7,12},{8,3},{9,2},... | collective-permute-start | bytes 196616 | tf_op jit(solution)/shard_map/ppermute | solution.py:272
  94.4 22.2 %collective-permute-start.21 = (bf16[64,512]{1,0:T(8,128)(2,1)S(1)}, bf16[64,512]{1,0:T(8,128)(2,1)S(1)}, u32[]{:S(2)}, u32[]{:S(2)}) collective-permute-start(bf16[64,512]{1,0:T(8,128)(2,1)S(1)} %copy-done.14), channel_id=1, source_target_pairs={{0,13},{1,12},{2,15},{3,14},{4,9},{5,8},{6,11},{7,10},{8,5},{9,4},... | collective-permute-start | bytes 196616 | tf_op jit(solution)/shard_map/ppermute | solution.py:272
  96.2 20.4 %collective-permute-start.22 = (bf16[64,512]{1,0:T(8,128)(2,1)S(1)}, bf16[64,512]{1,0:T(8,128)(2,1)S(1)}, u32[]{:S(2)}, u32[]{:S(2)}) collective-permute-start(bf16[64,512]{1,0:T(8,128)(2,1)S(1)} %copy-done.12), channel_id=1, source_target_pairs={{0,15},{1,14},{2,13},{3,12},{4,11},{5,10},{6,9},{7,8},{8,7},{9,6},... | collective-permute-start | bytes 196616 | tf_op jit(solution)/shard_map/ppermute | solution.py:272
  99.9 37.7 %collective-permute-start.31 = (bf16[512,512]{1,0:T(8,128)(2,1)}, bf16[512,512]{1,0:T(8,128)(2,1)}, u32[]{:S(2)}, u32[]{:S(2)}) collective-permute-start(bf16[512,512]{1,0:T(8,128)(2,1)} %get-tuple-element.77), channel_id=1, source_target_pairs={{0,0},{1,1},{2,16},{3,17},{4,32},{5,33},{6,48},{7,49},{8,64},{9,65... | collective-permute-start | bytes 1572872 | tf_op jit(solution)/shard_map/ppermute | solution.py:276
  118.1 34.9 %collective-permute-start.23 = (bf16[512,512]{1,0:T(8,128)(2,1)}, bf16[512,512]{1,0:T(8,128)(2,1)}, u32[]{:S(2)}, u32[]{:S(2)}) collective-permute-start(bf16[512,512]{1,0:T(8,128)(2,1)} %get-tuple-element.67), channel_id=1, source_target_pairs={{0,1},{1,0},{2,17},{3,16},{4,33},{5,32},{6,49},{7,48},{8,65},{9,64... | collective-permute-start | bytes 1572872 | tf_op jit(solution)/shard_map/ppermute | solution.py:277
  (25 other events, 256.6 us)

commit v2 on v1

v2 whole, which is shorter than its diff:
```python
import functools

import jax
import jax.numpy as jnp
from jax import lax
from jax.experimental import pallas as pl
from jax.experimental.pallas import tpu as pltpu
from jax.sharding import PartitionSpec as P

AXES = ("occi", "occj")
F32 = jnp.float32
BF16 = jnp.bfloat16
SUB = 16


def coupling(fock_occ, couple_list, couple_count):
    n_occ = fock_occ.shape[0]
    slots = jnp.arange(couple_list.shape[1], dtype=jnp.int32)
    active = slots[None, :] < couple_count[:, None]
    target = jnp.arange(n_occ, dtype=jnp.int32)
    hits = (couple_list[:, :, None] == target[None, None, :]) & active[:, :, None]
    return fock_occ * jnp.sum(hits.astype(fock_occ.dtype), axis=1)


def params(limit, **kw):
    return pltpu.CompilerParams(vmem_limit_bytes=limit << 20, **kw)


def whole(shape):
    return pl.BlockSpec(shape, lambda *_: (0,) * len(shape))


def mix_kernel(w_ref, in_ref, out_ref):
    n, block, _ = in_ref.shape
    w = w_ref[...]
    high = w.astype(BF16)
    rest = w - high.astype(F32)
    mid = rest.astype(BF16)
    low = (rest - mid.astype(F32)).astype(BF16)
    for r in range(0, block, SUB):
        rhs = jnp.concatenate([in_ref[k, r : r + SUB, :] for k in range(n)], axis=0)
        total = jnp.dot(high, rhs, preferred_element_type=F32)
        total += jnp.dot(mid, rhs, preferred_element_type=F32)
        total += jnp.dot(low, rhs, preferred_element_type=F32)
        for j in range(n):
            out_ref[j, r : r + SUB, :] = total[j * SUB : (j + 1) * SUB, :].astype(BF16)


def mix(wide, slices):
    return pl.pallas_call(
        mix_kernel,
        out_shape=jax.ShapeDtypeStruct(slices.shape, BF16),
        grid=(1,),
        in_specs=[whole(wide.shape), whole(slices.shape)],
        out_specs=whole(slices.shape),
        compiler_params=params(24),
        cost_estimate=pl.CostEstimate(
            flops=10**9, bytes_accessed=4 * slices.size, transcendentals=0
        ),
        name="mix",
    )(wide, slices)


def ladder_kernel(slot, amp_ref, int_ref, x_ref, xt_ref, core_ref, fock_ref, out_ref, scaled):
    step = pl.program_id(0)
    tile = core_ref.shape[1]
    rank = x_ref.shape[1]
    chunk = min(512, rank)
    amp = amp_ref[...]
    cols = pl.ds(pl.multiple_of(step * tile, tile), tile)
    first = jnp.dot(amp, x_ref[:, cols], preferred_element_type=F32).astype(BF16)
    for p in range(0, rank, chunk):
        middle = jnp.dot(xt_ref[p : p + chunk, :], first, preferred_element_type=F32)
        scaled[p : p + chunk, :] = (core_ref[p : p + chunk, :].astype(F32) * middle).astype(BF16)
    second = jnp.dot(x_ref[...], scaled[...], preferred_element_type=F32).astype(BF16)
    part = jnp.dot(second, xt_ref[cols, :], preferred_element_type=F32)

    @pl.when(step == 0)
    def _():
        virtual = jnp.dot(fock_ref[...], amp, preferred_element_type=F32)
        out_ref[...] = int_ref[...].astype(F32) + virtual + part

    @pl.when(step > 0)
    def _():
        out_ref[...] += part


def ladder(slot, amps, ints, x, xt, core, fock):
    virt, rank = x.shape
    tile = min(512, rank)
    pair = pl.BlockSpec((None, virt, virt), lambda q, s: (s[0], 0, 0))
    return pl.pallas_call(
        ladder_kernel,
        out_shape=jax.ShapeDtypeStruct((virt, virt), F32),
        grid_spec=pltpu.PrefetchScalarGridSpec(
            num_scalar_prefetch=1,
            grid=(rank // tile,),
            in_specs=[
                pair,
                pair,
                whole(x.shape),
                whole(xt.shape),
                pl.BlockSpec((rank, tile), lambda q, s: (0, q)),
                whole(fock.shape),
            ],
            out_specs=whole((virt, virt)),
            scratch_shapes=[pltpu.VMEM((rank, tile), BF16)],
        ),
        compiler_params=params(40, dimension_semantics=("arbitrary",)),
        cost_estimate=pl.CostEstimate(
            flops=4 * virt * rank * (rank + virt) + 2 * virt**3,
            bytes_accessed=2 * rank * rank + 4 * virt * rank,
            transcendentals=0,
        ),
        name="ladder",
    )(slot, amps, ints, x, xt, core, fock)


def half_kernel(place, part_a, part_b, sum_ref, send_a, send_b):
    core = place[0]
    send_a[...] = (part_a[...] - sum_ref[core].astype(F32)).astype(BF16)
    send_b[...] = (part_b[...] - sum_ref[1 - core].astype(F32)).astype(BF16)


def half_of(place, part_a, part_b, sums):
    virt = part_a.shape[0]
    rows = min(128, virt)
    strip = pl.BlockSpec((rows, virt), lambda r, s: (r, 0))
    return pl.pallas_call(
        half_kernel,
        out_shape=[jax.ShapeDtypeStruct(part_a.shape, BF16)] * 2,
        grid_spec=pltpu.PrefetchScalarGridSpec(
            num_scalar_prefetch=1,
            grid=(virt // rows,),
            in_specs=[strip, strip, pl.BlockSpec((2, rows, virt), lambda r, s: (0, r, 0))],
            out_specs=[strip, strip],
        ),
        compiler_params=params(16),
        cost_estimate=pl.CostEstimate(
            flops=0, bytes_accessed=16 * part_a.size, transcendentals=0
        ),
        name="half",
    )(place, part_a, part_b, sums)


def finish_kernel(slot, part_ref, sum_ref, mirror_ref, amp_ref, col_ref, row_ref, occ_ref, *refs):
    res_ref, new_ref = refs[-2:]
    half = part_ref[...] - sum_ref[...].astype(F32)
    residual = half + mirror_ref[...].astype(F32).T
    denominator = col_ref[...] + row_ref[...] - occ_ref[0] - occ_ref[1]
    res_ref[...] = residual
    new_ref[...] = (amp_ref[...].astype(F32) - residual / denominator).astype(BF16)


def finish(slot, part, sums, mirror, amps, eps_col, eps_row, occ, held):
    virt = part.shape[0]
    rows = min(128, virt)
    strip = pl.BlockSpec((None, rows, virt), lambda r, s: (s[0], r, 0))
    held_specs = [pl.BlockSpec(memory_space=pl.ANY)] * len(held)
    return pl.pallas_call(
        finish_kernel,
        out_shape=[
            jax.ShapeDtypeStruct(amps.shape, F32),
            jax.ShapeDtypeStruct(amps.shape, BF16),
        ],
        grid_spec=pltpu.PrefetchScalarGridSpec(
            num_scalar_prefetch=1,
            grid=(virt // rows,),
            in_specs=[
                pl.BlockSpec((rows, virt), lambda r, s: (r, 0)),
                strip,
                pl.BlockSpec((virt, rows), lambda r, s: (0, r)),
                strip,
                pl.BlockSpec((rows, 1), lambda r, s: (r, 0)),
                whole((1, virt)),
                pl.BlockSpec(memory_space=pltpu.SMEM),
            ]
            + held_specs,
            out_specs=[strip, strip],
        ),
        input_output_aliases={8 + n: n for n in range(len(held))},
        compiler_params=params(16, dimension_semantics=("arbitrary",)),
        cost_estimate=pl.CostEstimate(
            flops=20 * part.size, bytes_accessed=14 * part.size, transcendentals=0
        ),
        name="finish",
    )(slot, part, sums, mirror, amps, eps_col, eps_row, occ, *held)


def shards(
    amplitudes,
    exch_int,
    thc_factor,
    thc_core,
    fock_vir,
    eps_vir,
    eps_occ,
    fock_occ,
    couple_list,
    couple_count,
):
    rows_i, _, virt, _ = amplitudes.shape
    n_first = lax.axis_size("occi")
    n_second = lax.axis_size("occj")
    me_i = lax.axis_index("occi")
    me_j = lax.axis_index("occj")
    core = me_j % 2
    place = jnp.stack([core, me_j // 2]).astype(jnp.int32)
    slot_a = jnp.reshape(core, (1,)).astype(jnp.int32)
    slot_b = 1 - slot_a
    amps = amplitudes.reshape(rows_i, virt, virt)
    ints = exch_int.reshape(rows_i, virt, virt)

    def mirror_hop(flip):
        return [
            (p * n_second + 2 * q + s, q * n_second + 2 * p + (s ^ flip))
            for p in range(n_first)
            for q in range(n_first)
            for s in range(2)
        ]

    slices = amps.reshape(n_second, rows_i * virt // n_second, virt)
    slices = lax.all_to_all(slices, "occj", 0, 0, tiled=True)
    weights = coupling(fock_occ, couple_list, couple_count)
    tall = jnp.repeat(jnp.repeat(weights, SUB, axis=0), SUB, axis=1)
    lane = jnp.arange(n_second * SUB, dtype=jnp.int32) % SUB
    wide = jnp.where(lane[:, None] == lane[None, :], tall, 0.0)
    factor_t = thc_factor.T
    part_a = ladder(slot_a, amps, ints, thc_factor, factor_t, thc_core, fock_vir)
    slices, part_a = lax.optimization_barrier((slices, part_a))
    sums = mix(wide, slices)
    sums = lax.all_to_all(sums, "occj", 0, 0, tiled=True)
    part_b = ladder(slot_b, amps, ints, thc_factor, factor_t, thc_core, fock_vir)
    sums, part_b = lax.optimization_barrier((sums, part_b))
    sums = sums.reshape(rows_i, virt, virt)
    send_a, send_b = half_of(place, part_a, part_b, sums)
    got_a = lax.ppermute(send_a, AXES, mirror_hop(0))
    got_b = lax.ppermute(send_b, AXES, mirror_hop(1))

    occ_rows = lax.dynamic_slice_in_dim(eps_occ, me_i * rows_i, rows_i, 0)
    occ_column = lax.dynamic_slice_in_dim(eps_occ, me_j, 1, 0)
    occ_a = jnp.stack([jnp.where(core == 0, occ_rows[0], occ_rows[1]), occ_column[0]])
    occ_b = jnp.stack([jnp.where(core == 0, occ_rows[1], occ_rows[0]), occ_column[0]])
    eps_col = eps_vir.reshape(virt, 1)
    eps_row = eps_vir.reshape(1, virt)
    held = finish(slot_a, part_a, sums, got_a, amps, eps_col, eps_row, occ_a, ())
    residual, updated = finish(slot_b, part_b, sums, got_b, amps, eps_col, eps_row, occ_b, held)
    return (
        residual.reshape(rows_i, 1, virt, virt),
        updated.reshape(rows_i, 1, virt, virt),
    )


def solution(mesh):
    pairs = P("occi", "occj", None, None)
    return jax.shard_map(
        shards,
        mesh=mesh,
        in_specs=(pairs, pairs) + (P(),) * 8,
        out_specs=(pairs, pairs),
        check_vma=False,
    )
```

time: 157 us -> 124 us (0.79)
  the two profiles are of different devices: /device:TPU:25 before, /device:TPU:89 now
where the time goes in v2:
time: 124 us; the launch traced here: 123 us
  Pallas kernels  39.9 us (32%)
  waiting for transfers between devices  36.3 us (29%)
  starting transfers between devices  23.1 us (19%)
  local copies, waits for them, and re-layouts  18.6 us (15%)
  between operations  3.53 us (3%)
  other arithmetic  1.87 us (2%)
    pallas_call x2, Pallas kernels, ladder(): pl.pallas_call(ladder_kernel, out_shape=jax.ShapeDtypeStruct((virt, virt)...  28.5 us
    ppermute x1, waiting for transfers between devices, shards(): got_a = lax.ppermute(send_a, AXES, mirror_hop(0))  24.6 us
    unnamed x39, local copies, waits for them, and re-layouts  16.6 us
    ppermute x1, waiting for transfers between devices, shards(): got_b = lax.ppermute(send_b, AXES, mirror_hop(1))  11.7 us
    all_to_all x1, starting transfers between devices, shards(): slices = lax.all_to_all(slices, 'occj', 0, 0, tiled=True)  7.74 us
    all_to_all x1, starting transfers between devices, shards(): sums = lax.all_to_all(sums, 'occj', 0, 0, tiled=True)  7.23 us
    pallas_call x2, Pallas kernels, finish(): pl.pallas_call(finish_kernel, out_shape=[jax.ShapeDtypeStruct(amps.shape,...  7.07 us
    ppermute x1, starting transfers between devices, shards(): got_b = lax.ppermute(send_b, AXES, mirror_hop(1))  4.68 us
  transfers between devices with their start and end apart: 4, of which 2 were waited for; matrix products, arithmetic and copies ran while one was open for 5% of the time, Pallas kernels for 26%

profile of v2, /device:TPU:89, one launch (start us, length us, event | category | flops | bytes accessed | tf_op | source)
XLA Modules:
  0.0 123.3 jit_solution(1778044289796811158)
XLA Ops:
  0.7 7.7 %all-to-all-start = ((bf16[16,64,512]{2,1,0:T(8,128)(2,1)}), bf16[16,64,512]{2,1,0:T(8,128)(2,1)}, u32[]{:S(2)}, u32[]{:S(2)}) async-start(bf16[16,64,512]{2,1,0:T(8,128)(2,1)} %bitcast.25), calls=%async_computation | async-start | bytes 2097152 | tf_op jit(solution)/shard_map/all_to_all | solution.py:223
  8.8 0.1 reshape.75
  9.0 0.1 copy.27
  9.1 2.5 %copy.28 = bf16[512,2048]{0,1:T(8,128)(2,1)} copy(bf16[512,2048]{1,0:T(8,128)(2,1)S(1)} %copy-done.4) | data formatting | bytes 4194304 | tf_op args[2]
  11.6 0.1 compare_select_fusion.w_ref
  11.8 1.6 %copy-done.5 = bf16[512,2048]{1,0:T(8,128)(2,1)S(1)} copy-done((bf16[512,2048]{1,0:T(8,128)(2,1)S(1)}, bf16[512,2048]{1,0:T(8,128)(2,1)}, u32[]{:S(2)}) %copy-start.5) | copy-done | bytes 2097176
  13.3 1.6 %copy-done.7 = bf16[512,2048]{0,1:T(8,128)(2,1)S(1)} copy-done((bf16[512,2048]{0,1:T(8,128)(2,1)S(1)}, bf16[512,2048]{0,1:T(8,128)(2,1)}, u32[]{:S(2)}) %copy-start.7) | copy-done | bytes 2097176
  14.9 1.2 copy-done.11
  16.2 1.0 copy-done.13
  17.2 14.2 %ladder.2.part_a.part_ref = f32[512,512]{1,0:T(8,128)S(1)} custom-call(s32[1]{0:T(128)} %bitcast.slot, bf16[2,512,512]{2,1,0:T(8,128)(2,1)S(1)} %bitcast.26, bf16[2,512,512]{2,1,0:T(8,128)(2,1)S(1)} %bitcast.35, bf16[512,2048]{1,0:T(8,128)(2,1)S(1)} %copy-done.5, bf16[2048,512]{1,0:T(8,128)(2,1)S(1)} %bitcast.30, bf16[2048,2048]{1,0:T(8,128)(2,1)} %core_ref.3, ...), custom_call_target="tpu_custom_call" | custom-call | flops 11005853696 | bytes 12582912 | tf_op jit(solution)/shard_map/ladder/pallas_call | solution.py:92
  31.4 2.2 %mix.1 = bf16[16,64,512]{2,1,0:T(8,128)(2,1)S(1)} custom-call(f32[256,256]{1,0:T(8,128)S(1)} %compare_select_fusion.w_ref, bf16[16,64,512]{2,1,0:T(8,128)(2,1)} %all-to-all-done.in_ref), custom_call_target="tpu_custom_call" | custom-call | flops 1000000000 | bytes 2097152 | tf_op jit(solution)/shard_map/mix/pallas_call | solution.py:50
  33.7 1.0 copy-done.9
  34.6 7.2 %all-to-all-start.1 = ((bf16[16,64,512]{2,1,0:T(8,128)(2,1)}), bf16[16,64,512]{2,1,0:T(8,128)(2,1)S(1)}, u32[]{:S(2)}, u32[]{:S(2)}) async-start(bf16[16,64,512]{2,1,0:T(8,128)(2,1)} %copy-done.9), calls=%async_computation.1 | async-start | bytes 2097152 | tf_op jit(solution)/shard_map/all_to_all | solution.py:232
  41.9 1.6 %copy-done.6 = bf16[512,2048]{1,0:T(8,128)(2,1)S(1)} copy-done((bf16[512,2048]{1,0:T(8,128)(2,1)S(1)}, bf16[512,2048]{1,0:T(8,128)(2,1)}, u32[]{:S(2)}) %copy-start.6) | copy-done | bytes 2097176
  43.5 1.6 %copy-done.8 = bf16[512,2048]{0,1:T(8,128)(2,1)S(1)} copy-done((bf16[512,2048]{0,1:T(8,128)(2,1)S(1)}, bf16[512,2048]{0,1:T(8,128)(2,1)}, u32[]{:S(2)}) %copy-start.8) | copy-done | bytes 2097176
  45.0 1.2 copy-done.12
  46.3 1.0 copy-done.14
  47.3 14.2 %ladder.3.part_b.part_ref = f32[512,512]{1,0:T(8,128)S(1)} custom-call(s32[1]{0:T(128)S(6)} %sub.7.slot, bf16[2,512,512]{2,1,0:T(8,128)(2,1)S(1)} %bitcast.27, bf16[2,512,512]{2,1,0:T(8,128)(2,1)S(1)} %bitcast.36, bf16[512,2048]{1,0:T(8,128)(2,1)S(1)} %copy-done.6, bf16[2048,512]{1,0:T(8,128)(2,1)S(1)} %bitcast.31, bf16[2048,2048]{1,0:T(8,128)(2,1)} %core_ref.3, ...), custom_call_target="tpu_custom_call" | custom-call | flops 11005853696 | bytes 12582912 | tf_op jit(solution)/shard_map/ladder/pallas_call | solution.py:92
  61.6 1.0 copy-done.1
  62.6 1.2 %copy-done.2 = f32[512,512]{1,0:T(8,128)S(1)} copy-done((f32[512,512]{1,0:T(8,128)S(1)}, f32[512,512]{1,0:T(8,128)}, u32[]{:S(2)}) %copy-start.2) | copy-done | bytes 1048600
  63.8 2.2 %half.1 = (bf16[512,512]{1,0:T(8,128)(2,1)}, bf16[512,512]{1,0:T(8,128)(2,1)}) custom-call(s32[2]{0:T(128)S(1)} %pad_add_fusion.place, f32[512,512]{1,0:T(8,128)S(1)} %ladder.2.part_a.part_ref, f32[512,512]{1,0:T(8,128)S(1)} %copy-done.2, bf16[2,512,512]{2,1,0:T(8,128)(2,1)S(1)} %bitcast.22), custom_call_target="tpu_custom_call" | custom-call | bytes 4194304 | tf_op jit(solution)/shard_map/half/pallas_call | solution.py:129
  66.0 3.5 %collective-permute-start.1 = (bf16[512,512]{1,0:T(8,128)(2,1)}, bf16[512,512]{1,0:T(8,128)(2,1)}, u32[]{:S(2)}, u32[]{:S(2)}) collective-permute-start(bf16[512,512]{1,0:T(8,128)(2,1)} %get-tuple-element.17), channel_id=1, source_target_pairs={{0,0},{1,1},{2,16},{3,17},{4,32},{5,33},{6,48},{7,49},{8,64},{9,65... | collective-permute-start | bytes 1572872 | tf_op jit(solution)/shard_map/ppermute | solution.py:237
  69.5 4.7 %collective-permute-start = (bf16[512,512]{1,0:T(8,128)(2,1)}, bf16[512,512]{1,0:T(8,128)(2,1)}, u32[]{:S(2)}, u32[]{:S(2)}) collective-permute-start(bf16[512,512]{1,0:T(8,128)(2,1)} %get-tuple-element.16), channel_id=1, source_target_pairs={{0,1},{1,0},{2,17},{3,16},{4,33},{5,32},{6,49},{7,48},{8,65},{9,64... | collective-permute-start | bytes 1572872 | tf_op jit(solution)/shard_map/ppermute | solution.py:238
  74.2 0.7 fusion.1
  77.6 0.7 dynamic_slice.7
  78.2 0.1 copy.30.col_ref
  78.4 0.8 pad_maximum_fusion.occ_ref
  79.2 0.7 pad_maximum_fusion.1.occ_ref
  80.0 24.6 %collective-permute-done.1.mirror_ref = bf16[512,512]{1,0:T(8,128)(2,1)} collective-permute-done((bf16[512,512]{1,0:T(8,128)(2,1)}, bf16[512,512]{1,0:T(8,128)(2,1)}, u32[]{:S(2)}, u32[]{:S(2)}) %collective-permute-start.1) | collective-permute-done | bytes 524320 | tf_op jit(solution)/shard_map/ppermute | solution.py:237
  104.6 3.5 %finish.2 = (f32[2,512,512]{2,1,0:T(8,128)}, bf16[2,512,512]{2,1,0:T(8,128)(2,1)}) custom-call(s32[1]{0:T(128)} %bitcast.slot, f32[512,512]{1,0:T(8,128)S(1)} %ladder.2.part_a.part_ref, bf16[2,512,512]{2,1,0:T(8,128)(2,1)S(1)} %bitcast.23, bf16[512,512]{1,0:T(8,128)(2,1)} %collective-permute-done.1.mirror_ref, bf16[2,512,512]{2,1,0:T(8,128)(2,1)S(1)} %bitcast.28, ...), custom_call_target="tpu_custom_call" | custom-call | flops 5242880 | bytes 3670016 | tf_op jit(solution)/shard_map/finish/pallas_call | solution.py:160
  108.1 11.7 %collective-permute-done.mirror_ref = bf16[512,512]{1,0:T(8,128)(2,1)} collective-permute-done((bf16[512,512]{1,0:T(8,128)(2,1)}, bf16[512,512]{1,0:T(8,128)(2,1)}, u32[]{:S(2)}, u32[]{:S(2)}) %collective-permute-start) | collective-permute-done | bytes 524320 | tf_op jit(solution)/shard_map/ppermute | solution.py:238
  119.8 3.5 %finish.3 = (f32[2,512,512]{2,1,0:T(8,128)}, bf16[2,512,512]{2,1,0:T(8,128)(2,1)}) custom-call(s32[1]{0:T(128)S(6)} %sub.7.slot, f32[512,512]{1,0:T(8,128)S(1)} %copy-done.3, bf16[2,512,512]{2,1,0:T(8,128)(2,1)S(1)} %bitcast.24, bf16[512,512]{1,0:T(8,128)(2,1)} %collective-permute-done.mirror_ref, ...), custom_call_target="tpu_custom_call", output_to_operand_aliasing={{0}: (8, {}), {1}: (9, {})} | custom-call | flops 5242880 | bytes 3670016 | tf_op jit(solution)/shard_map/finish/pallas_call | solution.py:160
  (38 shorter events, 0.5 us)
Async XLA Ops:
  0.6 7.9 %copy-start.17 = (s32[16]{0:T(128)S(1)}, s32[16]{0:T(128)}, u32[]{:S(2)}) copy-start(s32[16]{0:T(128)} %param.19) | copy-start | bytes 196
  0.6 7.9 %copy-start.16 = (s32[16,6]{0,1:T(8,128)S(1)}, s32[16,6]{0,1:T(8,128)}, u32[]{:S(2)}) copy-start(s32[16,6]{0,1:T(8,128)} %param.18) | copy-start | bytes 1156
  0.7 8.0 %copy-start.15 = (f32[16,16]{1,0:T(8,128)S(1)}, f32[16,16]{1,0:T(8,128)}, u32[]{:S(2)}) copy-start(f32[16,16]{1,0:T(8,128)} %param.17) | copy-start | bytes 3076
  0.7 8.4 %copy-start.4 = (bf16[512,2048]{1,0:T(8,128)(2,1)S(1)}, bf16[512,2048]{1,0:T(8,128)(2,1)}, u32[]{:S(2)}) copy-start(bf16[512,2048]{1,0:T(8,128)(2,1)} %x_ref.3) | copy-start | bytes 6291460
  0.7 30.8 %all-to-all-start = ((bf16[16,64,512]{2,1,0:T(8,128)(2,1)}), bf16[16,64,512]{2,1,0:T(8,128)(2,1)}, u32[]{:S(2)}, u32[]{:S(2)}) async-start(bf16[16,64,512]{2,1,0:T(8,128)(2,1)} %bitcast.25), calls=%async_computation | async-start | bytes 2097152 | tf_op jit(solution)/shard_map/all_to_all | solution.py:223
  9.1 2.6 %copy-start = (bf16[2,1,512,512]{3,2,1,0:T(8,128)(2,1)S(1)}, bf16[2,1,512,512]{3,2,1,0:T(8,128)(2,1)}, u32[]{:S(2)}) copy-start(bf16[2,1,512,512]{3,2,1,0:T(8,128)(2,1)} %param.10) | copy-start | bytes 3145732
  11.7 1.6 %copy-start.5 = (bf16[512,2048]{1,0:T(8,128)(2,1)S(1)}, bf16[512,2048]{1,0:T(8,128)(2,1)}, u32[]{:S(2)}) copy-start(bf16[512,2048]{1,0:T(8,128)(2,1)} %x_ref.3) | copy-start | bytes 6291460
  13.3 1.6 %copy-start.7 = (bf16[512,2048]{0,1:T(8,128)(2,1)S(1)}, bf16[512,2048]{0,1:T(8,128)(2,1)}, u32[]{:S(2)}) copy-start(bf16[512,2048]{0,1:T(8,128)(2,1)} %copy.28) | copy-start | bytes 6291460
  14.9 1.2 copy-start.11
  16.2 1.0 copy-start.13
  33.7 1.0 copy-start.9
  34.6 28.0 %all-to-all-start.1 = ((bf16[16,64,512]{2,1,0:T(8,128)(2,1)}), bf16[16,64,512]{2,1,0:T(8,128)(2,1)S(1)}, u32[]{:S(2)}, u32[]{:S(2)}) async-start(bf16[16,64,512]{2,1,0:T(8,128)(2,1)} %copy-done.9), calls=%async_computation.1 | async-start | bytes 2097152 | tf_op jit(solution)/shard_map/all_to_all | solution.py:232
  41.9 1.6 %copy-start.6 = (bf16[512,2048]{1,0:T(8,128)(2,1)S(1)}, bf16[512,2048]{1,0:T(8,128)(2,1)}, u32[]{:S(2)}) copy-start(bf16[512,2048]{1,0:T(8,128)(2,1)} %x_ref.3) | copy-start | bytes 6291460
  43.5 1.6 %copy-start.8 = (bf16[512,2048]{0,1:T(8,128)(2,1)S(1)}, bf16[512,2048]{0,1:T(8,128)(2,1)}, u32[]{:S(2)}) copy-start(bf16[512,2048]{0,1:T(8,128)(2,1)} %copy.28) | copy-start | bytes 6291460
  45.0 1.2 copy-start.12
  46.3 1.0 copy-start.14
  47.3 30.9 %copy-start.10 = (f32[512]{0:T(512)S(1)}, f32[512]{0:T(512)}, u32[]{:S(2)}) copy-start(f32[512]{0:T(512)} %param.15) | copy-start | bytes 6148
  61.6 1.0 copy-start.1
  62.6 11.6 %copy-start.18 = (f32[16]{0:T(128)S(1)}, f32[16]{0:T(128)}, u32[]{:S(2)}) copy-start(f32[16]{0:T(128)} %param.16) | copy-start | bytes 196
  62.6 1.2 %copy-start.2 = (f32[512,512]{1,0:T(8,128)S(1)}, f32[512,512]{1,0:T(8,128)}, u32[]{:S(2)}) copy-start(f32[512,512]{1,0:T(8,128)} %copy-done.1) | copy-start | bytes 3145732
  66.0 38.6 %collective-permute-start.1 = (bf16[512,512]{1,0:T(8,128)(2,1)}, bf16[512,512]{1,0:T(8,128)(2,1)}, u32[]{:S(2)}, u32[]{:S(2)}) collective-permute-start(bf16[512,512]{1,0:T(8,128)(2,1)} %get-tuple-element.17), channel_id=1, source_target_pairs={{0,0},{1,1},{2,16},{3,17},{4,32},{5,33},{6,48},{7,49},{8,64},{9,65... | collective-permute-start | bytes 1572872 | tf_op jit(solution)/shard_map/ppermute | solution.py:237
  69.5 50.3 %collective-permute-start = (bf16[512,512]{1,0:T(8,128)(2,1)}, bf16[512,512]{1,0:T(8,128)(2,1)}, u32[]{:S(2)}, u32[]{:S(2)}) collective-permute-start(bf16[512,512]{1,0:T(8,128)(2,1)} %get-tuple-element.16), channel_id=1, source_target_pairs={{0,1},{1,0},{2,17},{3,16},{4,33},{5,32},{6,49},{7,48},{8,65},{9,64... | collective-permute-start | bytes 1572872 | tf_op jit(solution)/shard_map/ppermute | solution.py:238
  78.4 41.4 %copy-start.3 = (f32[512,512]{1,0:T(8,128)S(1)}, f32[512,512]{1,0:T(8,128)}, u32[]{:S(2)}) copy-start(f32[512,512]{1,0:T(8,128)} %copy-done.1) | copy-start | bytes 3145732

commit v3 on v2

--- a/solution.py
+++ b/solution.py
@@ -31,29 +31,30 @@
 
 
 def mix_kernel(w_ref, in_ref, out_ref):
-    n, block, _ = in_ref.shape
+    n = in_ref.shape[0]
     w = w_ref[...]
     high = w.astype(BF16)
     rest = w - high.astype(F32)
     mid = rest.astype(BF16)
     low = (rest - mid.astype(F32)).astype(BF16)
-    for r in range(0, block, SUB):
-        rhs = jnp.concatenate([in_ref[k, r : r + SUB, :] for k in range(n)], axis=0)
-        total = jnp.dot(high, rhs, preferred_element_type=F32)
-        total += jnp.dot(mid, rhs, preferred_element_type=F32)
-        total += jnp.dot(low, rhs, preferred_element_type=F32)
-        for j in range(n):
-            out_ref[j, r : r + SUB, :] = total[j * SUB : (j + 1) * SUB, :].astype(BF16)
+    rhs = jnp.concatenate([in_ref[k] for k in range(n)], axis=0)
+    total = jnp.dot(high, rhs, preferred_element_type=F32)
+    total += jnp.dot(mid, rhs, preferred_element_type=F32)
+    total += jnp.dot(low, rhs, preferred_element_type=F32)
+    for j in range(n):
+        out_ref[j] = total[j * SUB : (j + 1) * SUB, :].astype(BF16)
 
 
 def mix(wide, slices):
+    n, block, virt = slices.shape
+    strip = pl.BlockSpec((n, SUB, virt), lambda r: (0, r, 0))
     return pl.pallas_call(
         mix_kernel,
         out_shape=jax.ShapeDtypeStruct(slices.shape, BF16),
-        grid=(1,),
-        in_specs=[whole(wide.shape), whole(slices.shape)],
-        out_specs=whole(slices.shape),
-        compiler_params=params(24),
+        grid=(block // SUB,),
+        in_specs=[whole(wide.shape), strip],
+        out_specs=strip,
+        compiler_params=params(16),
         cost_estimate=pl.CostEstimate(
             flops=10**9, bytes_accessed=4 * slices.size, transcendentals=0
         ),
@@ -61,31 +62,31 @@
     )(wide, slices)
 
 
-def ladder_kernel(slot, amp_ref, int_ref, x_ref, xt_ref, core_ref, fock_ref, out_ref, scaled):
+def ladder_kernel(slot, amp_ref, int_ref, x_ref, core_ref, fock_ref, out_ref, scaled, x_t):
     step = pl.program_id(0)
     tile = core_ref.shape[1]
     rank = x_ref.shape[1]
     chunk = min(512, rank)
     amp = amp_ref[...]
+
+    @pl.when(step == 0)
+    def _():
+        for c in range(0, rank, min(256, rank)):
+            cut = slice(c, c + min(256, rank))
+            x_t[cut, :] = x_ref[:, cut].T
+        virtual = jnp.dot(fock_ref[...], amp, preferred_element_type=F32)
+        out_ref[...] = int_ref[...].astype(F32) + virtual
+
     cols = pl.ds(pl.multiple_of(step * tile, tile), tile)
     first = jnp.dot(amp, x_ref[:, cols], preferred_element_type=F32).astype(BF16)
     for p in range(0, rank, chunk):
-        middle = jnp.dot(xt_ref[p : p + chunk, :], first, preferred_element_type=F32)
+        middle = jnp.dot(x_t[p : p + chunk, :], first, preferred_element_type=F32)
         scaled[p : p + chunk, :] = (core_ref[p : p + chunk, :].astype(F32) * middle).astype(BF16)
     second = jnp.dot(x_ref[...], scaled[...], preferred_element_type=F32).astype(BF16)
-    part = jnp.dot(second, xt_ref[cols, :], preferred_element_type=F32)
-
-    @pl.when(step == 0)
-    def _():
-        virtual = jnp.dot(fock_ref[...], amp, preferred_element_type=F32)
-        out_ref[...] = int_ref[...].astype(F32) + virtual + part
-
-    @pl.when(step > 0)
-    def _():
-        out_ref[...] += part
-
-
-def ladder(slot, amps, ints, x, xt, core, fock):
+    out_ref[...] += jnp.dot(second, x_t[cols, :], preferred_element_type=F32)
+
+
+def ladder(slot, amps, ints, x, core, fock):
     virt, rank = x.shape
     tile = min(512, rank)
     pair = pl.BlockSpec((None, virt, virt), lambda q, s: (s[0], 0, 0))
@@ -99,21 +100,20 @@
                 pair,
                 pair,
                 whole(x.shape),
-                whole(xt.shape),
                 pl.BlockSpec((rank, tile), lambda q, s: (0, q)),
                 whole(fock.shape),
             ],
             out_specs=whole((virt, virt)),
-            scratch_shapes=[pltpu.VMEM((rank, tile), BF16)],
-        ),
-        compiler_params=params(40, dimension_semantics=("arbitrary",)),
+            scratch_shapes=[pltpu.VMEM((rank, tile), BF16), pltpu.VMEM((rank, virt), BF16)],
+        ),
+        compiler_params=params(56, dimension_semantics=("arbitrary",)),
         cost_estimate=pl.CostEstimate(
             flops=4 * virt * rank * (rank + virt) + 2 * virt**3,
             bytes_accessed=2 * rank * rank + 4 * virt * rank,
             transcendentals=0,
         ),
         name="ladder",
-    )(slot, amps, ints, x, xt, core, fock)
+    )(slot, amps, ints, x, core, fock)
 
 
 def half_kernel(place, part_a, part_b, sum_ref, send_a, send_b):
@@ -225,12 +225,11 @@
     tall = jnp.repeat(jnp.repeat(weights, SUB, axis=0), SUB, axis=1)
     lane = jnp.arange(n_second * SUB, dtype=jnp.int32) % SUB
     wide = jnp.where(lane[:, None] == lane[None, :], tall, 0.0)
-    factor_t = thc_factor.T
-    part_a = ladder(slot_a, amps, ints, thc_factor, factor_t, thc_core, fock_vir)
+    part_a = ladder(slot_a, amps, ints, thc_factor, thc_core, fock_vir)
     slices, part_a = lax.optimization_barrier((slices, part_a))
     sums = mix(wide, slices)
     sums = lax.all_to_all(sums, "occj", 0, 0, tiled=True)
-    part_b = ladder(slot_b, amps, ints, thc_factor, factor_t, thc_core, fock_vir)
+    part_b = ladder(slot_b, amps, ints, thc_factor, thc_core, fock_vir)
     sums, part_b = lax.optimization_barrier((sums, part_b))
     sums = sums.reshape(rows_i, virt, virt)
     send_a, send_b = half_of(place, part_a, part_b, sums)

time: 124 us -> 114 us (0.919)
  the two profiles are of different devices: /device:TPU:89 before, /device:TPU:57 now
where the time goes in v3:
time: 114 us; the launch traced here: 113 us
  Pallas kernels  44.6 us (39%)
  waiting for transfers between devices  36.9 us (32%)
  starting transfers between devices  23.3 us (20%)
  between operations  3.36 us (3%)
  local copies, waits for them, and re-layouts  3.11 us (3%)
  other arithmetic  1.78 us (2%)
    pallas_call x2, Pallas kernels, ladder(): pl.pallas_call(ladder_kernel, out_shape=jax.ShapeDtypeStruct((virt, virt)...  32.7 us
    ppermute x1, waiting for transfers between devices, shards(): got_a = lax.ppermute(send_a, AXES, mirror_hop(0))  24.1 us
    ppermute x1, waiting for transfers between devices, shards(): got_b = lax.ppermute(send_b, AXES, mirror_hop(1))  11.9 us
    all_to_all x1, starting transfers between devices, shards(): slices = lax.all_to_all(slices, 'occj', 0, 0, tiled=True)  7.54 us
    all_to_all x1, starting transfers between devices, shards(): sums = lax.all_to_all(sums, 'occj', 0, 0, tiled=True)  7.1 us
    pallas_call x2, Pallas kernels, finish(): pl.pallas_call(finish_kernel, out_shape=[jax.ShapeDtypeStruct(amps.shape,...  7.07 us
    ppermute x1, starting transfers between devices, shards(): got_a = lax.ppermute(send_a, AXES, mirror_hop(0))  4.8 us
    ppermute x1, starting transfers between devices, shards(): got_b = lax.ppermute(send_b, AXES, mirror_hop(1))  3.9 us
  transfers between devices with their start and end apart: 4, of which 4 were waited for; matrix products, arithmetic and copies ran while one was open for 3% of the time, Pallas kernels for 32%

profile of v3, /device:TPU:57, one launch (start us, length us, event | category | flops | bytes accessed | tf_op | source)
XLA Modules:
  0.0 113.1 jit_solution(4272902845781622015)
XLA Ops:
  0.7 7.5 %all-to-all-start = ((bf16[16,64,512]{2,1,0:T(8,128)(2,1)}), bf16[16,64,512]{2,1,0:T(8,128)(2,1)S(1)}, u32[]{:S(2)}, u32[]{:S(2)}) async-start(bf16[16,64,512]{2,1,0:T(8,128)(2,1)} %bitcast.24), calls=%async_computation | async-start | bytes 2097152 | tf_op jit(solution)/shard_map/all_to_all | solution.py:223
  8.2 0.1 pad_add_fusion.place
  8.3 0.0 copy-done.6
  8.3 0.1 convert_reduce_fusion
  8.4 0.1 copy.24
  8.5 0.1 broadcast_in_dim.7
  8.6 0.1 reshape.75
  8.8 0.1 copy.25
  8.9 0.1 compare_select_fusion.w_ref
  9.0 16.3 %ladder.2.part_a.part_ref = f32[512,512]{1,0:T(8,128)} custom-call(s32[1]{0:T(128)} %bitcast.slot, bf16[2,512,512]{2,1,0:T(8,128)(2,1)} %bitcast.25, bf16[2,512,512]{2,1,0:T(8,128)(2,1)} %bitcast.35, bf16[512,2048]{1,0:T(8,128)(2,1)} %x_ref.3, bf16[2048,2048]{1,0:T(8,128)(2,1)} %core_ref.3, bf16[512,512]{1,0:T(8,128)(2,1)} %fock_ref.3), custom_call_target="tpu_custom_call" | custom-call | flops 11005853696 | bytes 12582912 | tf_op jit(solution)/shard_map/ladder/pallas_call | solution.py:93
  25.3 0.1 all-to-all-done.in_ref
  25.4 2.6 %mix.1 = bf16[16,64,512]{2,1,0:T(8,128)(2,1)} custom-call(f32[256,256]{1,0:T(8,128)S(1)} %compare_select_fusion.w_ref, bf16[16,64,512]{2,1,0:T(8,128)(2,1)S(1)} %all-to-all-done.in_ref), custom_call_target="tpu_custom_call" | custom-call | flops 1000000000 | bytes 2097152 | tf_op jit(solution)/shard_map/mix/pallas_call | solution.py:51
  28.1 7.1 %all-to-all-start.1 = ((bf16[16,64,512]{2,1,0:T(8,128)(2,1)}), bf16[16,64,512]{2,1,0:T(8,128)(2,1)S(1)}, u32[]{:S(2)}, u32[]{:S(2)}) async-start(bf16[16,64,512]{2,1,0:T(8,128)(2,1)} %mix.1), calls=%async_computation.1 | async-start | bytes 2097152 | tf_op jit(solution)/shard_map/all_to_all | solution.py:231
  35.2 0.0 copy-start.8
  35.2 0.0 copy-start.4
  35.2 16.4 %ladder.3.part_b.part_ref = f32[512,512]{1,0:T(8,128)} custom-call(s32[1]{0:T(128)S(6)} %sub.7.slot, bf16[2,512,512]{2,1,0:T(8,128)(2,1)} %bitcast.26, bf16[2,512,512]{2,1,0:T(8,128)(2,1)} %bitcast.36, bf16[512,2048]{1,0:T(8,128)(2,1)} %x_ref.3, bf16[2048,2048]{1,0:T(8,128)(2,1)} %core_ref.3, bf16[512,512]{1,0:T(8,128)(2,1)} %fock_ref.3), custom_call_target="tpu_custom_call" | custom-call | flops 11005853696 | bytes 12582912 | tf_op jit(solution)/shard_map/ladder/pallas_call | solution.py:93
  51.6 0.8 all-to-all-done.1
  52.4 1.2 %copy-done.2 = f32[512,512]{1,0:T(8,128)S(1)} copy-done((f32[512,512]{1,0:T(8,128)S(1)}, f32[512,512]{1,0:T(8,128)}, u32[]{:S(2)}) %copy-start.2) | copy-done | bytes 1048600
  53.6 2.2 %half.1 = (bf16[512,512]{1,0:T(8,128)(2,1)}, bf16[512,512]{1,0:T(8,128)(2,1)}) custom-call(s32[2]{0:T(128)S(1)} %pad_add_fusion.place, f32[512,512]{1,0:T(8,128)S(1)} %copy-done.1, f32[512,512]{1,0:T(8,128)S(1)} %copy-done.2, bf16[2,512,512]{2,1,0:T(8,128)(2,1)S(1)} %bitcast.21), custom_call_target="tpu_custom_call" | custom-call | bytes 4194304 | tf_op jit(solution)/shard_map/half/pallas_call | solution.py:129
  55.8 4.8 %collective-permute-start.1 = (bf16[512,512]{1,0:T(8,128)(2,1)}, bf16[512,512]{1,0:T(8,128)(2,1)}, u32[]{:S(2)}, u32[]{:S(2)}) collective-permute-start(bf16[512,512]{1,0:T(8,128)(2,1)} %get-tuple-element.17), channel_id=1, source_target_pairs={{0,0},{1,1},{2,16},{3,17},{4,32},{5,33},{6,48},{7,49},{8,64},{9,65... | collective-permute-start | bytes 1572872 | tf_op jit(solution)/shard_map/ppermute | solution.py:236
  60.6 3.9 %collective-permute-start = (bf16[512,512]{1,0:T(8,128)(2,1)}, bf16[512,512]{1,0:T(8,128)(2,1)}, u32[]{:S(2)}, u32[]{:S(2)}) collective-permute-start(bf16[512,512]{1,0:T(8,128)(2,1)} %get-tuple-element.16), channel_id=1, source_target_pairs={{0,1},{1,0},{2,17},{3,16},{4,33},{5,32},{6,49},{7,48},{8,65},{9,64... | collective-permute-start | bytes 1572872 | tf_op jit(solution)/shard_map/ppermute | solution.py:237
  64.5 0.1 dynamic_slice.6
  64.6 0.6 fusion.1
  67.7 0.6 dynamic_slice.7
  68.3 0.1 copy.27.col_ref
  68.5 0.8 pad_maximum_fusion.occ_ref
  69.3 0.7 pad_maximum_fusion.1.occ_ref
  70.0 24.1 %collective-permute-done.1.mirror_ref = bf16[512,512]{1,0:T(8,128)(2,1)} collective-permute-done((bf16[512,512]{1,0:T(8,128)(2,1)}, bf16[512,512]{1,0:T(8,128)(2,1)}, u32[]{:S(2)}, u32[]{:S(2)}) %collective-permute-start.1) | collective-permute-done | bytes 524320 | tf_op jit(solution)/shard_map/ppermute | solution.py:236
  94.1 3.5 %finish.2 = (f32[2,512,512]{2,1,0:T(8,128)}, bf16[2,512,512]{2,1,0:T(8,128)(2,1)}) custom-call(s32[1]{0:T(128)} %bitcast.slot, f32[512,512]{1,0:T(8,128)S(1)} %copy-done.1, bf16[2,512,512]{2,1,0:T(8,128)(2,1)S(1)} %bitcast.22, bf16[512,512]{1,0:T(8,128)(2,1)} %collective-permute-done.1.mirror_ref, bf16[2,512,512]{2,1,0:T(8,128)(2,1)S(1)} %bitcast.27, ...), custom_call_target="tpu_custom_call" | custom-call | flops 5242880 | bytes 3670016 | tf_op jit(solution)/shard_map/finish/pallas_call | solution.py:160
  97.7 11.9 %collective-permute-done.mirror_ref = bf16[512,512]{1,0:T(8,128)(2,1)} collective-permute-done((bf16[512,512]{1,0:T(8,128)(2,1)}, bf16[512,512]{1,0:T(8,128)(2,1)}, u32[]{:S(2)}, u32[]{:S(2)}) %collective-permute-start) | collective-permute-done | bytes 524320 | tf_op jit(solution)/shard_map/ppermute | solution.py:237
  109.5 0.0 copy-done.3
  109.5 3.5 %finish.3 = (f32[2,512,512]{2,1,0:T(8,128)}, bf16[2,512,512]{2,1,0:T(8,128)(2,1)}) custom-call(s32[1]{0:T(128)S(6)} %sub.7.slot, f32[512,512]{1,0:T(8,128)S(1)} %copy-done.3, bf16[2,512,512]{2,1,0:T(8,128)(2,1)S(1)} %bitcast.23, bf16[512,512]{1,0:T(8,128)(2,1)} %collective-permute-done.mirror_ref, ...), custom_call_target="tpu_custom_call", output_to_operand_aliasing={{0}: (8, {}), {1}: (9, {})} | custom-call | flops 5242880 | bytes 3670016 | tf_op jit(solution)/shard_map/finish/pallas_call | solution.py:160
  (17 shorter events, 0.1 us)
Async XLA Ops:
  0.6 7.7 %copy-start.7 = (s32[16]{0:T(128)S(1)}, s32[16]{0:T(128)}, u32[]{:S(2)}) copy-start(s32[16]{0:T(128)} %param.19) | copy-start | bytes 196
  0.6 7.7 %copy-start.6 = (s32[16,6]{0,1:T(8,128)S(1)}, s32[16,6]{0,1:T(8,128)}, u32[]{:S(2)}) copy-start(s32[16,6]{0,1:T(8,128)} %param.18) | copy-start | bytes 1156
  0.7 7.8 %copy-start.5 = (f32[16,16]{1,0:T(8,128)S(1)}, f32[16,16]{1,0:T(8,128)}, u32[]{:S(2)}) copy-start(f32[16,16]{1,0:T(8,128)} %param.17) | copy-start | bytes 3076
  0.7 24.8 %all-to-all-start = ((bf16[16,64,512]{2,1,0:T(8,128)(2,1)}), bf16[16,64,512]{2,1,0:T(8,128)(2,1)S(1)}, u32[]{:S(2)}, u32[]{:S(2)}) async-start(bf16[16,64,512]{2,1,0:T(8,128)(2,1)} %bitcast.24), calls=%async_computation | async-start | bytes 2097152 | tf_op jit(solution)/shard_map/all_to_all | solution.py:223
  28.1 24.3 %all-to-all-start.1 = ((bf16[16,64,512]{2,1,0:T(8,128)(2,1)}), bf16[16,64,512]{2,1,0:T(8,128)(2,1)S(1)}, u32[]{:S(2)}, u32[]{:S(2)}) async-start(bf16[16,64,512]{2,1,0:T(8,128)(2,1)} %mix.1), calls=%async_computation.1 | async-start | bytes 2097152 | tf_op jit(solution)/shard_map/all_to_all | solution.py:231
  35.2 17.2 %copy-start.1 = (f32[512,512]{1,0:T(8,128)S(1)}, f32[512,512]{1,0:T(8,128)}, u32[]{:S(2)}) copy-start(f32[512,512]{1,0:T(8,128)} %ladder.2.part_a.part_ref) | copy-start | bytes 3145732
  35.2 29.3 %copy-start.8 = (f32[16]{0:T(128)S(1)}, f32[16]{0:T(128)}, u32[]{:S(2)}) copy-start(f32[16]{0:T(128)} %param.16) | copy-start | bytes 196
  35.2 33.2 %copy-start.4 = (f32[512]{0:T(512)S(1)}, f32[512]{0:T(512)}, u32[]{:S(2)}) copy-start(f32[512]{0:T(512)} %param.15) | copy-start | bytes 6148
  51.6 42.6 %copy-start = (bf16[2,1,512,512]{3,2,1,0:T(8,128)(2,1)S(1)}, bf16[2,1,512,512]{3,2,1,0:T(8,128)(2,1)}, u32[]{:S(2)}) copy-start(bf16[2,1,512,512]{3,2,1,0:T(8,128)(2,1)} %param.10) | copy-start | bytes 3145732
  52.4 1.2 %copy-start.2 = (f32[512,512]{1,0:T(8,128)S(1)}, f32[512,512]{1,0:T(8,128)}, u32[]{:S(2)}) copy-start(f32[512,512]{1,0:T(8,128)} %ladder.3.part_b.part_ref) | copy-start | bytes 3145732
  55.8 38.4 %collective-permute-start.1 = (bf16[512,512]{1,0:T(8,128)(2,1)}, bf16[512,512]{1,0:T(8,128)(2,1)}, u32[]{:S(2)}, u32[]{:S(2)}) collective-permute-start(bf16[512,512]{1,0:T(8,128)(2,1)} %get-tuple-element.17), channel_id=1, source_target_pairs={{0,0},{1,1},{2,16},{3,17},{4,32},{5,33},{6,48},{7,49},{8,64},{9,65... | collective-permute-start | bytes 1572872 | tf_op jit(solution)/shard_map/ppermute | solution.py:236
  60.6 49.0 %collective-permute-start = (bf16[512,512]{1,0:T(8,128)(2,1)}, bf16[512,512]{1,0:T(8,128)(2,1)}, u32[]{:S(2)}, u32[]{:S(2)}) collective-permute-start(bf16[512,512]{1,0:T(8,128)(2,1)} %get-tuple-element.16), channel_id=1, source_target_pairs={{0,1},{1,0},{2,17},{3,16},{4,33},{5,32},{6,49},{7,48},{8,65},{9,64... | collective-permute-start | bytes 1572872 | tf_op jit(solution)/shard_map/ppermute | solution.py:237
  68.5 41.1 %copy-start.3 = (f32[512,512]{1,0:T(8,128)S(1)}, f32[512,512]{1,0:T(8,128)}, u32[]{:S(2)}) copy-start(f32[512,512]{1,0:T(8,128)} %ladder.3.part_b.part_ref) | copy-start | bytes 3145732

commit v4 on v3

v4 whole, which is shorter than its diff:
```python
import functools

import jax
import jax.numpy as jnp
from jax import lax
from jax.experimental import pallas as pl
from jax.experimental.pallas import tpu as pltpu
from jax.sharding import PartitionSpec as P

AXES = ("occi", "occj")
F32 = jnp.float32
BF16 = jnp.bfloat16
SUB = 16


def coupling(fock_occ, couple_list, couple_count):
    n_occ = fock_occ.shape[0]
    slots = jnp.arange(couple_list.shape[1], dtype=jnp.int32)
    active = slots[None, :] < couple_count[:, None]
    target = jnp.arange(n_occ, dtype=jnp.int32)
    hits = (couple_list[:, :, None] == target[None, None, :]) & active[:, :, None]
    return fock_occ * jnp.sum(hits.astype(fock_occ.dtype), axis=1)


def params(limit, **kw):
    return pltpu.CompilerParams(vmem_limit_bytes=limit << 20, **kw)


def whole(shape):
    return pl.BlockSpec(shape, lambda *_: (0,) * len(shape))


def mix_kernel(w_ref, in_ref, out_ref):
    n = in_ref.shape[0]
    w = w_ref[...]
    high = w.astype(BF16)
    rest = w - high.astype(F32)
    mid = rest.astype(BF16)
    low = (rest - mid.astype(F32)).astype(BF16)
    for r in range(0, in_ref.shape[1], SUB):
        rhs = jnp.concatenate([in_ref[k, r : r + SUB, :] for k in range(n)], axis=0)
        total = jnp.dot(high, rhs, preferred_element_type=F32)
        total += jnp.dot(mid, rhs, preferred_element_type=F32)
        total += jnp.dot(low, rhs, preferred_element_type=F32)
        for j in range(n):
            out_ref[j, r : r + SUB, :] = total[j * SUB : (j + 1) * SUB, :].astype(BF16)


def mix(wide, slices):
    return pl.pallas_call(
        mix_kernel,
        out_shape=jax.ShapeDtypeStruct(slices.shape, BF16),
        grid=(1,),
        in_specs=[whole(wide.shape), whole(slices.shape)],
        out_specs=whole(slices.shape),
        compiler_params=params(16),
        cost_estimate=pl.CostEstimate(
            flops=10**9, bytes_accessed=4 * slices.size, transcendentals=0
        ),
        name="mix",
    )(wide, slices)


def ladder_kernel(more, close, slot, amp_ref, x_ref, core_ref, *refs):
    scaled, x_t = refs[-2:]
    refs = refs[:-2]
    step = pl.program_id(0)
    tile = core_ref.shape[1]
    rank = x_ref.shape[1]
    chunk = min(512, rank)
    part_ref = refs[-2] if close else refs[-1]
    amp = amp_ref[...]

    @pl.when(step == 0)
    def _():
        for c in range(0, rank, min(256, rank)):
            cut = slice(c, c + min(256, rank))
            x_t[cut, :] = x_ref[:, cut].T
        if more:
            part_ref[...] = refs[0][...]
        else:
            virtual = jnp.dot(refs[1][...], amp, preferred_element_type=F32)
            part_ref[...] = refs[0][...].astype(F32) + virtual

    here = step + more
    cols = pl.ds(pl.multiple_of(here * tile, tile), tile)
    first = jnp.dot(amp, x_ref[:, cols], preferred_element_type=F32).astype(BF16)
    for p in range(0, rank, chunk):
        middle = jnp.dot(x_t[p : p + chunk, :], first, preferred_element_type=F32)
        scaled[p : p + chunk, :] = (core_ref[p : p + chunk, :].astype(F32) * middle).astype(BF16)
    second = jnp.dot(x_ref[...], scaled[...], preferred_element_type=F32).astype(BF16)
    part_ref[...] += jnp.dot(second, x_t[cols, :], preferred_element_type=F32)
    if close:

        @pl.when(step == pl.num_programs(0) - 1)
        def _():
            half = part_ref[...] - refs[-3][...].astype(F32)
            part_ref[...] = half
            refs[-1][...] = half.astype(BF16)


def ladder(slot, amps, x, core, start, tiles, count, ints=None, fock=None, part=None, sums=None):
    virt, rank = x.shape
    tile = rank // count
    pair = pl.BlockSpec((None, virt, virt), lambda q, s: (s[0], 0, 0))
    square = whole((virt, virt))
    extra, specs = ([part], [square]) if start else ([ints, fock], [pair, square])
    outs, out_specs = [jax.ShapeDtypeStruct((virt, virt), F32)], [square]
    if sums is not None:
        extra, specs = extra + [sums], specs + [pair]
        outs, out_specs = outs + [jax.ShapeDtypeStruct((virt, virt), BF16)], [square, square]
    return pl.pallas_call(
        functools.partial(ladder_kernel, start, sums is not None),
        out_shape=outs,
        grid_spec=pltpu.PrefetchScalarGridSpec(
            num_scalar_prefetch=1,
            grid=(tiles,),
            in_specs=[
                pair,
                whole(x.shape),
                pl.BlockSpec((rank, tile), lambda q, s: (0, q + start)),
            ]
            + specs,
            out_specs=out_specs,
            scratch_shapes=[pltpu.VMEM((rank, tile), BF16), pltpu.VMEM((rank, virt), BF16)],
        ),
        compiler_params=params(54, dimension_semantics=("arbitrary",)),
        cost_estimate=pl.CostEstimate(
            flops=4 * virt * rank * (rank + virt) * tiles // count,
            bytes_accessed=2 * rank * rank * tiles // count + 4 * virt * rank,
            transcendentals=0,
        ),
        name="ladder",
    )(slot, amps, x, core, *extra)


def half_kernel(slot, part_ref, sum_ref, half_ref, send_ref):
    half = part_ref[...] - sum_ref[...].astype(F32)
    half_ref[...] = half
    send_ref[...] = half.astype(BF16)


def half_of(slot, part, sums):
    virt = part.shape[0]
    rows = min(256, virt)
    strip = pl.BlockSpec((rows, virt), lambda r, s: (r, 0))
    return pl.pallas_call(
        half_kernel,
        out_shape=[
            jax.ShapeDtypeStruct(part.shape, F32),
            jax.ShapeDtypeStruct(part.shape, BF16),
        ],
        grid_spec=pltpu.PrefetchScalarGridSpec(
            num_scalar_prefetch=1,
            grid=(virt // rows,),
            in_specs=[strip, pl.BlockSpec((None, rows, virt), lambda r, s: (s[0], r, 0))],
            out_specs=[strip, strip],
        ),
        compiler_params=params(16),
        cost_estimate=pl.CostEstimate(
            flops=0, bytes_accessed=12 * part.size, transcendentals=0
        ),
        name="half",
    )(slot, part, sums)


def finish_kernel(slot, half_ref, mirror_ref, amp_ref, col_ref, row_ref, occ_ref, *refs):
    res_ref, new_ref = refs[-2:]
    residual = half_ref[...] + mirror_ref[...].astype(F32).T
    denominator = col_ref[...] + row_ref[...] - occ_ref[0] - occ_ref[1]
    res_ref[...] = residual
    new_ref[...] = (amp_ref[...].astype(F32) - residual / denominator).astype(BF16)


def finish(slot, half, mirror, amps, eps_col, eps_row, occ, held):
    virt = half.shape[0]
    rows = min(256, virt)
    strip = pl.BlockSpec((None, rows, virt), lambda r, s: (s[0], r, 0))
    held_specs = [pl.BlockSpec(memory_space=pl.ANY)] * len(held)
    return pl.pallas_call(
        finish_kernel,
        out_shape=[
            jax.ShapeDtypeStruct(amps.shape, F32),
            jax.ShapeDtypeStruct(amps.shape, BF16),
        ],
        grid_spec=pltpu.PrefetchScalarGridSpec(
            num_scalar_prefetch=1,
            grid=(virt // rows,),
            in_specs=[
                pl.BlockSpec((rows, virt), lambda r, s: (r, 0)),
                pl.BlockSpec((virt, rows), lambda r, s: (0, r)),
                strip,
                pl.BlockSpec((rows, 1), lambda r, s: (r, 0)),
                whole((1, virt)),
                pl.BlockSpec(memory_space=pltpu.SMEM),
            ]
            + held_specs,
            out_specs=[strip, strip],
        ),
        input_output_aliases={7 + n: n for n in range(len(held))},
        compiler_params=params(16, dimension_semantics=("arbitrary",)),
        cost_estimate=pl.CostEstimate(
            flops=20 * half.size, bytes_accessed=14 * half.size, transcendentals=0
        ),
        name="finish",
    )(slot, half, mirror, amps, eps_col, eps_row, occ, *held)


def shards(
    amplitudes,
    exch_int,
    thc_factor,
    thc_core,
    fock_vir,
    eps_vir,
    eps_occ,
    fock_occ,
    couple_list,
    couple_count,
):
    rows_i, _, virt, _ = amplitudes.shape
    n_first = lax.axis_size("occi")
    n_second = lax.axis_size("occj")
    me_i = lax.axis_index("occi")
    me_j = lax.axis_index("occj")
    core = me_j % 2
    place = jnp.stack([core, me_j // 2]).astype(jnp.int32)
    slot_a = jnp.reshape(core, (1,)).astype(jnp.int32)
    slot_b = 1 - slot_a
    amps = amplitudes.reshape(rows_i, virt, virt)
    ints = exch_int.reshape(rows_i, virt, virt)

    def mirror_hop(flip):
        return [
            (p * n_second + 2 * q + s, q * n_second + 2 * p + (s ^ flip))
            for p in range(n_first)
            for q in range(n_first)
            for s in range(2)
        ]

    slices = amps.reshape(n_second, rows_i * virt // n_second, virt)
    slices = lax.all_to_all(slices, "occj", 0, 0, tiled=True)
    weights = coupling(fock_occ, couple_list, couple_count)
    tall = jnp.repeat(jnp.repeat(weights, SUB, axis=0), SUB, axis=1)
    lane = jnp.arange(n_second * SUB, dtype=jnp.int32) % SUB
    wide = jnp.where(lane[:, None] == lane[None, :], tall, 0.0)
    count = 4
    early = count // 2
    (part_a,) = ladder(
        slot_a, amps, thc_factor, thc_core, 0, early, count, ints=ints, fock=fock_vir
    )
    slices, part_a = lax.optimization_barrier((slices, part_a))
    sums = mix(wide, slices)
    sums, part_a = lax.optimization_barrier((sums, part_a))
    sums = lax.all_to_all(sums, "occj", 0, 0, tiled=True)
    (part_a,) = ladder(
        slot_a, amps, thc_factor, thc_core, early, count - early, count, part=part_a
    )
    sums, part_a = lax.optimization_barrier((sums, part_a))
    sums = sums.reshape(rows_i, virt, virt)
    half_a, send_a = half_of(slot_a, part_a, sums)
    send_a, sums = lax.optimization_barrier((send_a, sums))
    got_a = lax.ppermute(send_a, AXES, mirror_hop(0))
    half_b, send_b = ladder(
        slot_b, amps, thc_factor, thc_core, 0, count, count, ints=ints, fock=fock_vir, sums=sums
    )
    got_b = lax.ppermute(send_b, AXES, mirror_hop(1))

    occ_rows = lax.dynamic_slice_in_dim(eps_occ, me_i * rows_i, rows_i, 0)
    occ_column = lax.dynamic_slice_in_dim(eps_occ, me_j, 1, 0)
    occ_a = jnp.stack([jnp.where(core == 0, occ_rows[0], occ_rows[1]), occ_column[0]])
    occ_b = jnp.stack([jnp.where(core == 0, occ_rows[1], occ_rows[0]), occ_column[0]])
    eps_col = eps_vir.reshape(virt, 1)
    eps_row = eps_vir.reshape(1, virt)
    held = finish(slot_a, half_a, got_a, amps, eps_col, eps_row, occ_a, ())
    residual, updated = finish(slot_b, half_b, got_b, amps, eps_col, eps_row, occ_b, held)
    return (
        residual.reshape(rows_i, 1, virt, virt),
        updated.reshape(rows_i, 1, virt, virt),
    )


def solution(mesh):
    pairs = P("occi", "occj", None, None)
    return jax.shard_map(
        shards,
        mesh=mesh,
        in_specs=(pairs, pairs) + (P(),) * 8,
        out_specs=(pairs, pairs),
        check_vma=False,
    )
```

time: 114 us -> 108 us (0.947)
  the two profiles are of different devices: /device:TPU:57 before, /device:TPU:25 now
where the time goes in v4:
time: 108 us; the launch traced here: 107 us
  Pallas kernels  44.4 us (41%)
  waiting for transfers between devices  33.3 us (31%)
  starting transfers between devices  20.6 us (19%)
  local copies, waits for them, and re-layouts  3.59 us (3%)
  between operations  3.45 us (3%)
  other arithmetic  1.79 us (2%)
    pallas_call x3, Pallas kernels, ladder(): pl.pallas_call(functools.partial(ladder_kernel, start, sums is not None),...  37.4 us
    ppermute x1, waiting for transfers between devices, shards(): got_b = lax.ppermute(send_b, AXES, mirror_hop(1))  13.8 us
    all_to_all x1, starting transfers between devices, shards(): slices = lax.all_to_all(slices, 'occj', 0, 0, tiled=True)  8.44 us
    all_to_all x1, waiting for transfers between devices, shards(): sums = lax.all_to_all(sums, 'occj', 0, 0, tiled=True)  7.01 us
    ppermute x1, waiting for transfers between devices, shards(): got_a = lax.ppermute(send_a, AXES, mirror_hop(0))  6.35 us
    all_to_all x1, waiting for transfers between devices, shards(): slices = lax.all_to_all(slices, 'occj', 0, 0, tiled=True)  6.21 us
    ppermute x1, starting transfers between devices, shards(): got_b = lax.ppermute(send_b, AXES, mirror_hop(1))  5.52 us
    all_to_all x1, starting transfers between devices, shards(): sums = lax.all_to_all(sums, 'occj', 0, 0, tiled=True)  4.31 us
  transfers between devices with their start and end apart: 4, of which 4 were waited for; matrix products, arithmetic and copies ran while one was open for 3% of the time, Pallas kernels for 37%

profile of v4, /device:TPU:25, one launch (start us, length us, event | category | flops | bytes accessed | tf_op | source)
XLA Modules:
  0.0 107.2 jit_solution(2998059364630483398)
XLA Ops:
  0.6 0.0 copy-start.7
  0.6 0.0 copy-start.6
  0.7 8.4 %all-to-all-start = ((bf16[16,64,512]{2,1,0:T(8,128)(2,1)}), bf16[16,64,512]{2,1,0:T(8,128)(2,1)S(1)}, u32[]{:S(2)}, u32[]{:S(2)}) async-start(bf16[16,64,512]{2,1,0:T(8,128)(2,1)} %bitcast.20), calls=%async_computation | async-start | bytes 2097152 | tf_op jit(solution)/shard_map/all_to_all | solution.py:242
  9.1 0.0 copy-done.7
  9.1 0.1 convert_reduce_fusion
  9.3 0.1 copy.24
  9.3 0.1 broadcast_in_dim.7
  9.4 0.1 reshape.77
  9.6 0.1 copy.25
  9.7 0.1 compare_select_fusion.w_ref
  9.8 10.3 %ladder.3.refs_0_ = f32[512,512]{1,0:T(8,128)} custom-call(s32[1]{0:T(128)} %bitcast.slot, bf16[2,512,512]{2,1,0:T(8,128)(2,1)} %bitcast.21, bf16[512,2048]{1,0:T(8,128)(2,1)} %x_ref.5, bf16[2048,2048]{1,0:T(8,128)(2,1)} %core_ref.5, bf16[2,512,512]{2,1,0:T(8,128)(2,1)} %bitcast.34, bf16[512,512]{1,0:T(8,128)(2,1)} %refs_1_.3), custom_call_target="tpu_custom_call" | custom-call | flops 5368709120 | bytes 8388608 | tf_op jit(solution)/shard_map/ladder/pallas_call | solution.py:112
  20.1 6.2 %all-to-all-done.in_ref = bf16[16,64,512]{2,1,0:T(8,128)(2,1)S(1)} async-done(((bf16[16,64,512]{2,1,0:T(8,128)(2,1)}), bf16[16,64,512]{2,1,0:T(8,128)(2,1)S(1)}, u32[]{:S(2)}, u32[]{:S(2)}) %all-to-all-start) | async-done | bytes 1048608 | tf_op jit(solution)/shard_map/all_to_all | solution.py:242
  26.3 2.0 %mix.1 = bf16[16,64,512]{2,1,0:T(8,128)(2,1)} custom-call(f32[256,256]{1,0:T(8,128)S(1)} %compare_select_fusion.w_ref, bf16[16,64,512]{2,1,0:T(8,128)(2,1)S(1)} %all-to-all-done.in_ref), custom_call_target="tpu_custom_call" | custom-call | flops 1000000000 | bytes 2097152 | tf_op jit(solution)/shard_map/mix/pallas_call | solution.py:50
  28.3 4.3 %all-to-all-start.1 = ((bf16[16,64,512]{2,1,0:T(8,128)(2,1)}), bf16[16,64,512]{2,1,0:T(8,128)(2,1)S(1)}, u32[]{:S(2)}, u32[]{:S(2)}) async-start(bf16[16,64,512]{2,1,0:T(8,128)(2,1)} %mix.1), calls=%async_computation.1 | async-start | bytes 2097152 | tf_op jit(solution)/shard_map/all_to_all | solution.py:255
  32.6 10.3 %ladder.4.part_ref = f32[512,512]{1,0:T(8,128)} custom-call(s32[1]{0:T(128)} %bitcast.slot, bf16[2,512,512]{2,1,0:T(8,128)(2,1)} %bitcast.22, bf16[512,2048]{1,0:T(8,128)(2,1)} %x_ref.5, bf16[2048,2048]{1,0:T(8,128)(2,1)} %core_ref.5, f32[512,512]{1,0:T(8,128)} %ladder.3.refs_0_), custom_call_target="tpu_custom_call" | custom-call | flops 5368709120 | bytes 8388608 | tf_op jit(solution)/shard_map/ladder/pallas_call | solution.py:112
  42.9 7.0 %all-to-all-done.1 = bf16[16,64,512]{2,1,0:T(8,128)(2,1)S(1)} async-done(((bf16[16,64,512]{2,1,0:T(8,128)(2,1)}), bf16[16,64,512]{2,1,0:T(8,128)(2,1)S(1)}, u32[]{:S(2)}, u32[]{:S(2)}) %all-to-all-start.1) | async-done | bytes 1048608 | tf_op jit(solution)/shard_map/all_to_all | solution.py:255
  49.9 1.6 %copy-done.2 = f32[512,512]{1,0:T(8,128)S(1)} copy-done((f32[512,512]{1,0:T(8,128)S(1)}, f32[512,512]{1,0:T(8,128)}, u32[]{:S(2)}) %copy-start.2) | copy-done | bytes 1048600
  51.5 0.8 half.1
  52.3 2.3 %collective-permute-start.1 = (bf16[512,512]{1,0:T(8,128)(2,1)}, bf16[512,512]{1,0:T(8,128)(2,1)}, u32[]{:S(2)}, u32[]{:S(2)}) collective-permute-start(bf16[512,512]{1,0:T(8,128)(2,1)} %get-tuple-element.29), channel_id=1, source_target_pairs={{0,0},{1,1},{2,16},{3,17},{4,32},{5,33},{6,48},{7,49},{8,64},{9,65... | collective-permute-start | bytes 1572872 | tf_op jit(solution)/shard_map/ppermute | solution.py:263
  54.7 16.8 %ladder.5 = (f32[512,512]{1,0:T(8,128)}, bf16[512,512]{1,0:T(8,128)(2,1)}) custom-call(s32[1]{0:T(128)S(6)} %sub.3.slot, bf16[2,512,512]{2,1,0:T(8,128)(2,1)} %bitcast.23, bf16[512,2048]{1,0:T(8,128)(2,1)} %x_ref.5, bf16[2048,2048]{1,0:T(8,128)(2,1)} %core_ref.5, bf16[2,512,512]{2,1,0:T(8,128)(2,1)} %bitcast.35, bf16[512,512]{1,0:T(8,128)(2,1)} %refs_1_.3, ...), custom_call_target="tpu_custom_call" | custom-call | flops 10737418240 | bytes 12582912 | tf_op jit(solution)/shard_map/ladder/pallas_call | solution.py:112
  71.5 5.5 %collective-permute-start = (bf16[512,512]{1,0:T(8,128)(2,1)}, bf16[512,512]{1,0:T(8,128)(2,1)S(1)}, u32[]{:S(2)}, u32[]{:S(2)}) collective-permute-start(bf16[512,512]{1,0:T(8,128)(2,1)} %get-tuple-element.27), channel_id=1, source_target_pairs={{0,1},{1,0},{2,17},{3,16},{4,33},{5,32},{6,49},{7,48},{8,65},{9,64... | collective-permute-start | bytes 1572872 | tf_op jit(solution)/shard_map/ppermute | solution.py:267
  77.0 0.1 dynamic_slice.6
  77.1 0.7 fusion.1
  80.4 0.7 dynamic_slice.7
  81.1 0.0 copy-done.4
  81.1 0.1 copy.27.col_ref
  81.2 0.8 pad_maximum_fusion.occ_ref
  82.1 0.7 pad_maximum_fusion.1.occ_ref
  82.8 6.3 %collective-permute-done.1.mirror_ref = bf16[512,512]{1,0:T(8,128)(2,1)} collective-permute-done((bf16[512,512]{1,0:T(8,128)(2,1)}, bf16[512,512]{1,0:T(8,128)(2,1)}, u32[]{:S(2)}, u32[]{:S(2)}) %collective-permute-start.1) | collective-permute-done | bytes 524320 | tf_op jit(solution)/shard_map/ppermute | solution.py:263
  89.2 2.3 %finish.2 = (f32[2,512,512]{2,1,0:T(8,128)}, bf16[2,512,512]{2,1,0:T(8,128)(2,1)}) custom-call(s32[1]{0:T(128)} %bitcast.slot, f32[512,512]{1,0:T(8,128)S(1)} %get-tuple-element.28.half_ref, bf16[512,512]{1,0:T(8,128)(2,1)} %collective-permute-done.1.mirror_ref, bf16[2,512,512]{2,1,0:T(8,128)(2,1)S(1)} %bitcast.24, f32[512,1]{1,0:T(8,128)S(1)} %copy.27.col_ref, ...), custom_call_target="tpu_custom_call" | custom-call | flops 5242880 | bytes 3670016 | tf_op jit(solution)/shard_map/finish/pallas_call | solution.py:180
  91.5 13.8 %collective-permute-done.mirror_ref = bf16[512,512]{1,0:T(8,128)(2,1)S(1)} collective-permute-done((bf16[512,512]{1,0:T(8,128)(2,1)}, bf16[512,512]{1,0:T(8,128)(2,1)S(1)}, u32[]{:S(2)}, u32[]{:S(2)}) %collective-permute-start) | collective-permute-done | bytes 524320 | tf_op jit(solution)/shard_map/ppermute | solution.py:267
  105.2 1.9 %finish.3 = (f32[2,512,512]{2,1,0:T(8,128)}, bf16[2,512,512]{2,1,0:T(8,128)(2,1)}) custom-call(s32[1]{0:T(128)S(6)} %sub.3.slot, f32[512,512]{1,0:T(8,128)S(1)} %copy-done.3, bf16[512,512]{1,0:T(8,128)(2,1)S(1)} %collective-permute-done.mirror_ref, bf16[2,512,512]{2,1,0:T(8,128)(2,1)S(1)} %bitcast.25, ...), custom_call_target="tpu_custom_call", output_to_operand_aliasing={{0}: (7, {}), {1}: (8, {})} | custom-call | flops 5242880 | bytes 3670016 | tf_op jit(solution)/shard_map/finish/pallas_call | solution.py:180
  (17 shorter events, 0.1 us)
Async XLA Ops:
  0.6 8.5 %copy-start.7 = (s32[16]{0:T(128)S(1)}, s32[16]{0:T(128)}, u32[]{:S(2)}) copy-start(s32[16]{0:T(128)} %param.19) | copy-start | bytes 196
  0.6 8.5 %copy-start.6 = (s32[16,6]{0,1:T(8,128)S(1)}, s32[16,6]{0,1:T(8,128)}, u32[]{:S(2)}) copy-start(s32[16,6]{0,1:T(8,128)} %param.18) | copy-start | bytes 1156
  0.7 8.6 %copy-start.5 = (f32[16,16]{1,0:T(8,128)S(1)}, f32[16,16]{1,0:T(8,128)}, u32[]{:S(2)}) copy-start(f32[16,16]{1,0:T(8,128)} %param.17) | copy-start | bytes 3076
  0.7 25.7 %all-to-all-start = ((bf16[16,64,512]{2,1,0:T(8,128)(2,1)}), bf16[16,64,512]{2,1,0:T(8,128)(2,1)S(1)}, u32[]{:S(2)}, u32[]{:S(2)}) async-start(bf16[16,64,512]{2,1,0:T(8,128)(2,1)} %bitcast.20), calls=%async_computation | async-start | bytes 2097152 | tf_op jit(solution)/shard_map/all_to_all | solution.py:242
  28.3 21.6 %all-to-all-start.1 = ((bf16[16,64,512]{2,1,0:T(8,128)(2,1)}), bf16[16,64,512]{2,1,0:T(8,128)(2,1)S(1)}, u32[]{:S(2)}, u32[]{:S(2)}) async-start(bf16[16,64,512]{2,1,0:T(8,128)(2,1)} %mix.1), calls=%async_computation.1 | async-start | bytes 2097152 | tf_op jit(solution)/shard_map/all_to_all | solution.py:255
  49.9 4.8 %copy-start.1 = (bf16[16,64,512]{2,1,0:T(8,128)(2,1)}, bf16[16,64,512]{2,1,0:T(8,128)(2,1)S(1)}, u32[]{:S(2)}) copy-start(bf16[16,64,512]{2,1,0:T(8,128)(2,1)S(1)} %all-to-all-done.1) | copy-start | bytes 3145732
  49.9 1.6 %copy-start.2 = (f32[512,512]{1,0:T(8,128)S(1)}, f32[512,512]{1,0:T(8,128)}, u32[]{:S(2)}) copy-start(f32[512,512]{1,0:T(8,128)} %ladder.4.part_ref) | copy-start | bytes 3145732
  52.3 24.7 %copy-start.8 = (f32[16]{0:T(128)S(1)}, f32[16]{0:T(128)}, u32[]{:S(2)}) copy-start(f32[16]{0:T(128)} %param.16) | copy-start | bytes 196
  52.3 28.7 %copy-start.4 = (f32[512]{0:T(512)S(1)}, f32[512]{0:T(512)}, u32[]{:S(2)}) copy-start(f32[512]{0:T(512)} %param.15) | copy-start | bytes 6148
  52.3 36.8 %copy-start = (bf16[2,1,512,512]{3,2,1,0:T(8,128)(2,1)S(1)}, bf16[2,1,512,512]{3,2,1,0:T(8,128)(2,1)}, u32[]{:S(2)}) copy-start(bf16[2,1,512,512]{3,2,1,0:T(8,128)(2,1)} %param.10) | copy-start | bytes 3145732
  52.3 36.8 %collective-permute-start.1 = (bf16[512,512]{1,0:T(8,128)(2,1)}, bf16[512,512]{1,0:T(8,128)(2,1)}, u32[]{:S(2)}, u32[]{:S(2)}) collective-permute-start(bf16[512,512]{1,0:T(8,128)(2,1)} %get-tuple-element.29), channel_id=1, source_target_pairs={{0,0},{1,1},{2,16},{3,17},{4,32},{5,33},{6,48},{7,49},{8,64},{9,65... | collective-permute-start | bytes 1572872 | tf_op jit(solution)/shard_map/ppermute | solution.py:263
  71.5 33.7 %collective-permute-start = (bf16[512,512]{1,0:T(8,128)(2,1)}, bf16[512,512]{1,0:T(8,128)(2,1)S(1)}, u32[]{:S(2)}, u32[]{:S(2)}) collective-permute-start(bf16[512,512]{1,0:T(8,128)(2,1)} %get-tuple-element.27), channel_id=1, source_target_pairs={{0,1},{1,0},{2,17},{3,16},{4,33},{5,32},{6,49},{7,48},{8,65},{9,64... | collective-permute-start | bytes 1572872 | tf_op jit(solution)/shard_map/ppermute | solution.py:267
  81.2 24.0 %copy-start.3 = (f32[512,512]{1,0:T(8,128)S(1)}, f32[512,512]{1,0:T(8,128)}, u32[]{:S(2)}) copy-start(f32[512,512]{1,0:T(8,128)} %get-tuple-element.26.half_ref) | copy-start | bytes 3145732

commit v5 on v4

--- a/solution.py
+++ b/solution.py
@@ -156,7 +156,7 @@
             in_specs=[strip, pl.BlockSpec((None, rows, virt), lambda r, s: (s[0], r, 0))],
             out_specs=[strip, strip],
         ),
-        compiler_params=params(16),
+        compiler_params=params(56),
         cost_estimate=pl.CostEstimate(
             flops=0, bytes_accessed=12 * part.size, transcendentals=0
         ),
@@ -164,21 +164,24 @@
     )(slot, part, sums)
 
 
-def finish_kernel(slot, half_ref, mirror_ref, amp_ref, col_ref, row_ref, occ_ref, *refs):
+def finish_kernel(n, ids, half_ref, amp_ref, col_ref, row_ref, occ_ref, *refs):
     res_ref, new_ref = refs[-2:]
-    residual = half_ref[...] + mirror_ref[...].astype(F32).T
-    denominator = col_ref[...] + row_ref[...] - occ_ref[0] - occ_ref[1]
+    mirror = refs[0][...]
+    if n == 2:
+        mirror = jnp.where(ids[3] == 1, refs[1][...], mirror)
+    residual = half_ref[...] + mirror.astype(F32).T
+    denominator = col_ref[...] + row_ref[...] - occ_ref[ids[1]] - occ_ref[ids[2]]
     res_ref[...] = residual
     new_ref[...] = (amp_ref[...].astype(F32) - residual / denominator).astype(BF16)
 
 
-def finish(slot, half, mirror, amps, eps_col, eps_row, occ, held):
+def finish(ids, half, mirrors, amps, eps_col, eps_row, eps_occ, held):
     virt = half.shape[0]
     rows = min(256, virt)
     strip = pl.BlockSpec((None, rows, virt), lambda r, s: (s[0], r, 0))
-    held_specs = [pl.BlockSpec(memory_space=pl.ANY)] * len(held)
+    n = len(mirrors)
     return pl.pallas_call(
-        finish_kernel,
+        functools.partial(finish_kernel, n),
         out_shape=[
             jax.ShapeDtypeStruct(amps.shape, F32),
             jax.ShapeDtypeStruct(amps.shape, BF16),
@@ -188,22 +191,22 @@
             grid=(virt // rows,),
             in_specs=[
                 pl.BlockSpec((rows, virt), lambda r, s: (r, 0)),
-                pl.BlockSpec((virt, rows), lambda r, s: (0, r)),
                 strip,
                 pl.BlockSpec((rows, 1), lambda r, s: (r, 0)),
                 whole((1, virt)),
                 pl.BlockSpec(memory_space=pltpu.SMEM),
             ]
-            + held_specs,
+            + [pl.BlockSpec((virt, rows), lambda r, s: (0, r))] * n
+            + [pl.BlockSpec(memory_space=pl.ANY)] * len(held),
             out_specs=[strip, strip],
         ),
-        input_output_aliases={7 + n: n for n in range(len(held))},
+        input_output_aliases={6 + n + m: m for m in range(len(held))},
         compiler_params=params(16, dimension_semantics=("arbitrary",)),
         cost_estimate=pl.CostEstimate(
             flops=20 * half.size, bytes_accessed=14 * half.size, transcendentals=0
         ),
         name="finish",
-    )(slot, half, mirror, amps, eps_col, eps_row, occ, *held)
+    )(ids, half, amps, eps_col, eps_row, eps_occ, *mirrors, *held)
 
 
 def shards(
@@ -224,19 +227,47 @@
     me_i = lax.axis_index("occi")
     me_j = lax.axis_index("occj")
     core = me_j % 2
-    place = jnp.stack([core, me_j // 2]).astype(jnp.int32)
     slot_a = jnp.reshape(core, (1,)).astype(jnp.int32)
     slot_b = 1 - slot_a
     amps = amplitudes.reshape(rows_i, virt, virt)
     ints = exch_int.reshape(rows_i, virt, virt)
 
-    def mirror_hop(flip):
-        return [
-            (p * n_second + 2 * q + s, q * n_second + 2 * p + (s ^ flip))
-            for p in range(n_first)
-            for q in range(n_first)
-            for s in range(2)
-        ]
+    def hop(kind, flip):
+        pairs = []
+        for y in range(n_first // 2):
+            for x in range(n_first // 2):
+                far = (x - y) % (n_first // 2) == n_first // 4
+                if kind != "all" and far == (kind == "near"):
+                    continue
+                for low in range(2):
+                    for high in range(2):
+                        here, over = (y, low, x, high), (x, high, y, low)
+                        relay = (x, low, x, high)
+                        one, two = {
+                            "near": (here, over),
+                            "all": (here, over),
+                            "to": (here, relay),
+                            "from": (relay, over),
+                        }[kind]
+                        for c in range(2):
+                            pairs.append((spot(one, c), spot(two, c ^ flip)))
+        return pairs
+
+    def spot(chip, c):
+        y, low, x, high = chip
+        return (2 * y + low) * n_second + 2 * (2 * x + high) + c
+
+    def send(array, kind, flip):
+        return lax.ppermute(array, AXES, hop(kind, flip))
+
+    far_here = ((me_j // 4 - me_i // 2) % (n_first // 2) == n_first // 4).astype(jnp.int32)
+    eps_col = eps_vir.reshape(virt, 1)
+    eps_row = eps_vir.reshape(1, virt)
+
+    def ids_of(slot):
+        return jnp.stack([slot[0], me_i * rows_i + slot[0], me_j, far_here]).astype(jnp.int32)
+
+    ids_a, ids_b = ids_of(slot_a), ids_of(slot_b)
 
     slices = amps.reshape(n_second, rows_i * virt // n_second, virt)
     slices = lax.all_to_all(slices, "occj", 0, 0, tiled=True)
@@ -245,35 +276,34 @@
     lane = jnp.arange(n_second * SUB, dtype=jnp.int32) % SUB
     wide = jnp.where(lane[:, None] == lane[None, :], tall, 0.0)
     count = 4
-    early = count // 2
-    (part_a,) = ladder(
-        slot_a, amps, thc_factor, thc_core, 0, early, count, ints=ints, fock=fock_vir
-    )
-    slices, part_a = lax.optimization_barrier((slices, part_a))
+    early = count - 1
+    tables = (thc_factor, thc_core)
+    origin = dict(ints=ints, fock=fock_vir)
+    (part_a,) = ladder(slot_a, amps, *tables, 0, count, count, **origin)
+    slices, part_a, ids_a, ids_b, eps_col = lax.optimization_barrier(
+        (slices, part_a, ids_a, ids_b, eps_col)
+    )
     sums = mix(wide, slices)
-    sums, part_a = lax.optimization_barrier((sums, part_a))
+    sums, part_a, slot_b = lax.optimization_barrier((sums, part_a, slot_b))
     sums = lax.all_to_all(sums, "occj", 0, 0, tiled=True)
-    (part_a,) = ladder(
-        slot_a, amps, thc_factor, thc_core, early, count - early, count, part=part_a
-    )
-    sums, part_a = lax.optimization_barrier((sums, part_a))
+    (part_b,) = ladder(slot_b, amps, *tables, 0, early, count, **origin)
+    sums, part_a, part_b = lax.optimization_barrier((sums, part_a, part_b))
     sums = sums.reshape(rows_i, virt, virt)
     half_a, send_a = half_of(slot_a, part_a, sums)
-    send_a, sums = lax.optimization_barrier((send_a, sums))
-    got_a = lax.ppermute(send_a, AXES, mirror_hop(0))
+    send_a, sums, part_b = lax.optimization_barrier((send_a, sums, part_b))
+    near_a = send(send_a, "near", 0)
+    relay_a = send(send_a, "to", 0)
     half_b, send_b = ladder(
-        slot_b, amps, thc_factor, thc_core, 0, count, count, ints=ints, fock=fock_vir, sums=sums
-    )
-    got_b = lax.ppermute(send_b, AXES, mirror_hop(1))
-
-    occ_rows = lax.dynamic_slice_in_dim(eps_occ, me_i * rows_i, rows_i, 0)
-    occ_column = lax.dynamic_slice_in_dim(eps_occ, me_j, 1, 0)
-    occ_a = jnp.stack([jnp.where(core == 0, occ_rows[0], occ_rows[1]), occ_column[0]])
-    occ_b = jnp.stack([jnp.where(core == 0, occ_rows[1], occ_rows[0]), occ_column[0]])
-    eps_col = eps_vir.reshape(virt, 1)
-    eps_row = eps_vir.reshape(1, virt)
-    held = finish(slot_a, half_a, got_a, amps, eps_col, eps_row, occ_a, ())
-    residual, updated = finish(slot_b, half_b, got_b, amps, eps_col, eps_row, occ_b, held)
+        slot_b, amps, *tables, early, count - early, count, part=part_b, sums=sums
+    )
+    got_b = send(send_b, "all", 1)
+    relay_a, _ = lax.optimization_barrier((relay_a, send_b))
+    far_a = send(relay_a, "from", 0)
+
+    held = finish(ids_a, half_a, (near_a, far_a), amps, eps_col, eps_row, eps_occ, ())
+    residual, updated = finish(
+        ids_b, half_b, (got_b,), amps, eps_col, eps_row, eps_occ, held
+    )
     return (
         residual.reshape(rows_i, 1, virt, virt),
         updated.reshape(rows_i, 1, virt, virt),

time: 108 us -> 103 us (0.954)
  the two profiles are of different devices: /device:TPU:25 before, /device:TPU:36 now
where the time goes in v5:
time: 103 us; the launch traced here: 102 us
  Pallas kernels  46.6 us (45%)
  waiting for transfers between devices  28.9 us (28%)
  starting transfers between devices  24.1 us (23%)
  local copies, waits for them, and re-layouts  1.56 us (2%)
    pallas_call x3, Pallas kernels, ladder(): pl.pallas_call(functools.partial(ladder_kernel, start, sums is not None),...  36.5 us
    ppermute x4, waiting for transfers between devices, send(): return lax.ppermute(array, AXES, hop(kind, flip))  26.4 us
    ppermute x4, starting transfers between devices, send(): return lax.ppermute(array, AXES, hop(kind, flip))  9.53 us
    all_to_all x1, starting transfers between devices, shards(): slices = lax.all_to_all(slices, 'occj', 0, 0, tiled=True)  7.38 us
    all_to_all x1, starting transfers between devices, shards(): sums = lax.all_to_all(sums, 'occj', 0, 0, tiled=True)  7.21 us
    pallas_call x2, Pallas kernels, finish(): pl.pallas_call(functools.partial(finish_kernel, n), out_shape=[jax.ShapeD...  5.84 us
    all_to_all x1, waiting for transfers between devices, shards(): sums = lax.all_to_all(sums, 'occj', 0, 0, tiled=True)  2.51 us
    pallas_call x1, Pallas kernels, half_of(): pl.pallas_call(half_kernel, out_shape=[jax.ShapeDtypeStruct(part.shape, F...  2.36 us
  transfers between devices with their start and end apart: 6, of which 3 were waited for; matrix products, arithmetic and copies ran while one was open for 1% of the time, Pallas kernels for 39%

profile of v5, /device:TPU:36, one launch (start us, length us, event | category | flops | bytes accessed | tf_op | source)
XLA Modules:
  0.0 102.3 jit_solution(1800049155558918071)
XLA Ops:
  0.7 7.4 %all-to-all-start = ((bf16[16,64,512]{2,1,0:T(8,128)(2,1)}), bf16[16,64,512]{2,1,0:T(8,128)(2,1)S(1)}, u32[]{:S(2)}, u32[]{:S(2)}) async-start(bf16[16,64,512]{2,1,0:T(8,128)(2,1)} %bitcast.21), calls=%async_computation | async-start | bytes 2097152 | tf_op jit(solution)/shard_map/all_to_all | solution.py:273
  8.1 0.1 convert_reduce_fusion
  8.2 0.1 copy.24
  8.3 0.1 broadcast_in_dim.7
  8.4 0.1 reshape.78
  8.5 0.1 copy.25
  8.7 0.1 compare_select_fusion.w_ref
  8.8 0.1 add_add_fusion
  8.9 16.3 %ladder.3.part_ref = f32[512,512]{1,0:T(8,128)} custom-call(s32[1]{0:T(128)} %bitcast.1.slot, bf16[2,512,512]{2,1,0:T(8,128)(2,1)} %bitcast.22, bf16[512,2048]{1,0:T(8,128)(2,1)} %x_ref.5, bf16[2048,2048]{1,0:T(8,128)(2,1)} %core_ref.5, bf16[2,512,512]{2,1,0:T(8,128)(2,1)} %bitcast.35, bf16[512,512]{1,0:T(8,128)(2,1)} %refs_1_.3), custom_call_target="tpu_custom_call" | custom-call | flops 10737418240 | bytes 12582912 | tf_op jit(solution)/shard_map/ladder/pallas_call | solution.py:112
  25.2 0.0 all-to-all-done.in_ref
  25.2 2.0 %mix.1 = bf16[16,64,512]{2,1,0:T(8,128)(2,1)} custom-call(f32[256,256]{1,0:T(8,128)S(1)} %compare_select_fusion.w_ref, bf16[16,64,512]{2,1,0:T(8,128)(2,1)S(1)} %all-to-all-done.in_ref), custom_call_target="tpu_custom_call" | custom-call | flops 1000000000 | bytes 2097152 | tf_op jit(solution)/shard_map/mix/pallas_call | solution.py:50
  27.1 7.2 %all-to-all-start.1 = ((bf16[16,64,512]{2,1,0:T(8,128)(2,1)}), bf16[16,64,512]{2,1,0:T(8,128)(2,1)S(1)}, u32[]{:S(2)}, u32[]{:S(2)}) async-start(bf16[16,64,512]{2,1,0:T(8,128)(2,1)} %mix.1), calls=%async_computation.1 | async-start | bytes 2097152 | tf_op jit(solution)/shard_map/all_to_all | solution.py:288
  34.3 13.3 %ladder.4.refs_0_ = f32[512,512]{1,0:T(8,128)} custom-call(s32[1]{0:T(128)} %sub.16.slot, bf16[2,512,512]{2,1,0:T(8,128)(2,1)} %bitcast.23, bf16[512,2048]{1,0:T(8,128)(2,1)} %x_ref.5, bf16[2048,2048]{1,0:T(8,128)(2,1)} %core_ref.5, bf16[2,512,512]{2,1,0:T(8,128)(2,1)} %bitcast.36, bf16[512,512]{1,0:T(8,128)(2,1)} %refs_1_.3), custom_call_target="tpu_custom_call" | custom-call | flops 8053063680 | bytes 10485760 | tf_op jit(solution)/shard_map/ladder/pallas_call | solution.py:112
  47.6 2.5 %all-to-all-done.1 = bf16[16,64,512]{2,1,0:T(8,128)(2,1)S(1)} async-done(((bf16[16,64,512]{2,1,0:T(8,128)(2,1)}), bf16[16,64,512]{2,1,0:T(8,128)(2,1)S(1)}, u32[]{:S(2)}, u32[]{:S(2)}) %all-to-all-start.1) | async-done | bytes 1048608 | tf_op jit(solution)/shard_map/all_to_all | solution.py:288
  50.1 1.0 copy-done.5
  51.1 2.4 %half.1 = (f32[512,512]{1,0:T(8,128)}, bf16[512,512]{1,0:T(8,128)(2,1)}) custom-call(s32[1]{0:T(128)} %bitcast.1.slot, f32[512,512]{1,0:T(8,128)} %ladder.3.part_ref, bf16[2,512,512]{2,1,0:T(8,128)(2,1)} %bitcast.30), custom_call_target="tpu_custom_call" | custom-call | bytes 3145728 | tf_op jit(solution)/shard_map/half/pallas_call | solution.py:147
  53.5 0.0 copy-start.4
  53.5 6.0 %collective-permute-start.2 = (bf16[512,512]{1,0:T(8,128)(2,1)}, bf16[512,512]{1,0:T(8,128)(2,1)}, u32[]{:S(2)}, u32[]{:S(2)}) collective-permute-start(bf16[512,512]{1,0:T(8,128)(2,1)} %get-tuple-element.42), channel_id=1, source_target_pairs={{8,72},{9,73},{10,74},{11,75},{24,88},{25,89},{26,90},{27,91},{44,... | collective-permute-start | bytes 1572872 | tf_op jit(solution)/shard_map/ppermute | solution.py:261
  59.5 1.4 %collective-permute-start.1 = (bf16[512,512]{1,0:T(8,128)(2,1)}, bf16[512,512]{1,0:T(8,128)(2,1)}, u32[]{:S(2)}, u32[]{:S(2)}) collective-permute-start(bf16[512,512]{1,0:T(8,128)(2,1)} %get-tuple-element.42), channel_id=1, source_target_pairs={{0,0},{1,1},{2,16},{3,17},{16,2},{17,3},{18,18},{19,19},{4,32},{5,... | collective-permute-start | bytes 1572872 | tf_op jit(solution)/shard_map/ppermute | solution.py:261
  61.0 6.9 %ladder.5 = (f32[512,512]{1,0:T(8,128)}, bf16[512,512]{1,0:T(8,128)(2,1)}) custom-call(s32[1]{0:T(128)} %sub.16.slot, bf16[2,512,512]{2,1,0:T(8,128)(2,1)} %bitcast.24, bf16[512,2048]{1,0:T(8,128)(2,1)} %x_ref.5, bf16[2048,2048]{1,0:T(8,128)(2,1)} %core_ref.5, f32[512,512]{1,0:T(8,128)} %ladder.4.refs_0_, bf16[2,512,512]{2,1,0:T(8,128)(2,1)} %bitcast.31), custom_call_target="tpu_custom_call" | custom-call | flops 2684354560 | bytes 6291456 | tf_op jit(solution)/shard_map/ladder/pallas_call | solution.py:112
  67.8 2.1 %collective-permute-done.2 = bf16[512,512]{1,0:T(8,128)(2,1)} collective-permute-done((bf16[512,512]{1,0:T(8,128)(2,1)}, bf16[512,512]{1,0:T(8,128)(2,1)}, u32[]{:S(2)}, u32[]{:S(2)}) %collective-permute-start.2) | collective-permute-done | bytes 524320 | tf_op jit(solution)/shard_map/ppermute | solution.py:261
  69.9 1.3 %collective-permute-start.3 = (bf16[512,512]{1,0:T(8,128)(2,1)}, bf16[512,512]{1,0:T(8,128)(2,1)}, u32[]{:S(2)}, u32[]{:S(2)}) collective-permute-start(bf16[512,512]{1,0:T(8,128)(2,1)} %collective-permute-done.2), channel_id=1, source_target_pairs={{72,64},{73,65},{74,80},{75,81},{88,66},{89,67},{90,82},{91,83},{1... | collective-permute-start | bytes 1572872 | tf_op jit(solution)/shard_map/ppermute | solution.py:261
  71.2 0.8 collective-permute-start
  72.0 0.0 copy-done.3
  72.0 0.1 copy.27.col_ref
  72.2 0.0 collective-permute-done.1.refs_0_
  72.2 24.3 %collective-permute-done.3.refs_1_ = bf16[512,512]{1,0:T(8,128)(2,1)} collective-permute-done((bf16[512,512]{1,0:T(8,128)(2,1)}, bf16[512,512]{1,0:T(8,128)(2,1)}, u32[]{:S(2)}, u32[]{:S(2)}) %collective-permute-start.3) | collective-permute-done | bytes 524320 | tf_op jit(solution)/shard_map/ppermute | solution.py:261
  96.4 0.0 copy-done
  96.4 0.0 copy-done.4
  96.4 3.0 %finish.2 = (f32[2,512,512]{2,1,0:T(8,128)}, bf16[2,512,512]{2,1,0:T(8,128)(2,1)}) custom-call(s32[4]{0:T(128)S(1)} %get-tuple-element.40.ids, f32[512,512]{1,0:T(8,128)S(1)} %copy-done.1, bf16[2,512,512]{2,1,0:T(8,128)(2,1)S(1)} %bitcast.25, f32[512,1]{1,0:T(8,128)S(1)} %copy.27.col_ref, f32[1,512]{1,0:T(1,128)S(1)} %bitcast.28, f32[16]{0:T(128)S(1)} %copy-done.4, ...), custom_call_target="tpu_custom_call" | custom-call | flops 5242880 | bytes 3670016 | tf_op jit(solution)/shard_map/finish/pallas_call | solution.py:183
  99.4 0.0 collective-permute-done.refs_0_
  99.4 2.9 %finish.3 = (f32[2,512,512]{2,1,0:T(8,128)}, bf16[2,512,512]{2,1,0:T(8,128)(2,1)}) custom-call(s32[4]{0:T(128)S(1)} %get-tuple-element.25.ids, f32[512,512]{1,0:T(8,128)S(1)} %copy-done.2, bf16[2,512,512]{2,1,0:T(8,128)(2,1)S(1)} %bitcast.26, f32[512,1]{1,0:T(8,128)S(1)} %copy.27.col_ref, ...), custom_call_target="tpu_custom_call", output_to_operand_aliasing={{0}: (7, {}), {1}: (8, {})} | custom-call | flops 5242880 | bytes 3670016 | tf_op jit(solution)/shard_map/finish/pallas_call | solution.py:183
  (17 shorter events, 0.1 us)
Async XLA Ops:
  0.6 7.4 %copy-start.8 = (s32[16]{0:T(128)S(1)}, s32[16]{0:T(128)}, u32[]{:S(2)}) copy-start(s32[16]{0:T(128)} %param.19) | copy-start | bytes 196
  0.6 7.5 %copy-start.7 = (s32[16,6]{0,1:T(8,128)S(1)}, s32[16,6]{0,1:T(8,128)}, u32[]{:S(2)}) copy-start(s32[16,6]{0,1:T(8,128)} %param.18) | copy-start | bytes 1156
  0.7 7.6 %copy-start.6 = (f32[16,16]{1,0:T(8,128)S(1)}, f32[16,16]{1,0:T(8,128)}, u32[]{:S(2)}) copy-start(f32[16,16]{1,0:T(8,128)} %param.17) | copy-start | bytes 3076
  0.7 24.5 %all-to-all-start = ((bf16[16,64,512]{2,1,0:T(8,128)(2,1)}), bf16[16,64,512]{2,1,0:T(8,128)(2,1)S(1)}, u32[]{:S(2)}, u32[]{:S(2)}) async-start(bf16[16,64,512]{2,1,0:T(8,128)(2,1)} %bitcast.21), calls=%async_computation | async-start | bytes 2097152 | tf_op jit(solution)/shard_map/all_to_all | solution.py:273
  27.1 23.0 %all-to-all-start.1 = ((bf16[16,64,512]{2,1,0:T(8,128)(2,1)}), bf16[16,64,512]{2,1,0:T(8,128)(2,1)S(1)}, u32[]{:S(2)}, u32[]{:S(2)}) async-start(bf16[16,64,512]{2,1,0:T(8,128)(2,1)} %mix.1), calls=%async_computation.1 | async-start | bytes 2097152 | tf_op jit(solution)/shard_map/all_to_all | solution.py:288
  50.1 1.0 copy-start.5
  53.5 18.6 %copy-start.3 = (f32[512]{0:T(512)S(1)}, f32[512]{0:T(512)}, u32[]{:S(2)}) copy-start(f32[512]{0:T(512)} %param.15) | copy-start | bytes 6148
  53.5 43.0 %copy-start = (bf16[2,1,512,512]{3,2,1,0:T(8,128)(2,1)S(1)}, bf16[2,1,512,512]{3,2,1,0:T(8,128)(2,1)}, u32[]{:S(2)}) copy-start(bf16[2,1,512,512]{3,2,1,0:T(8,128)(2,1)} %param.10) | copy-start | bytes 3145732
  53.5 43.0 %copy-start.1 = (f32[512,512]{1,0:T(8,128)S(1)}, f32[512,512]{1,0:T(8,128)}, u32[]{:S(2)}) copy-start(f32[512,512]{1,0:T(8,128)} %get-tuple-element.41.half_ref) | copy-start | bytes 3145732
  53.5 43.0 %copy-start.4 = (f32[16]{0:T(128)S(1)}, f32[16]{0:T(128)}, u32[]{:S(2)}) copy-start(f32[16]{0:T(128)} %occ_ref.3) | copy-start | bytes 196
  53.5 16.5 %collective-permute-start.2 = (bf16[512,512]{1,0:T(8,128)(2,1)}, bf16[512,512]{1,0:T(8,128)(2,1)}, u32[]{:S(2)}, u32[]{:S(2)}) collective-permute-start(bf16[512,512]{1,0:T(8,128)(2,1)} %get-tuple-element.42), channel_id=1, source_target_pairs={{8,72},{9,73},{10,74},{11,75},{24,88},{25,89},{26,90},{27,91},{44,... | collective-permute-start | bytes 1572872 | tf_op jit(solution)/shard_map/ppermute | solution.py:261
  59.5 12.7 %collective-permute-start.1 = (bf16[512,512]{1,0:T(8,128)(2,1)}, bf16[512,512]{1,0:T(8,128)(2,1)}, u32[]{:S(2)}, u32[]{:S(2)}) collective-permute-start(bf16[512,512]{1,0:T(8,128)(2,1)} %get-tuple-element.42), channel_id=1, source_target_pairs={{0,0},{1,1},{2,16},{3,17},{16,2},{17,3},{18,18},{19,19},{4,32},{5,... | collective-permute-start | bytes 1572872 | tf_op jit(solution)/shard_map/ppermute | solution.py:261
  67.8 31.6 %copy-start.2 = (f32[512,512]{1,0:T(8,128)S(1)}, f32[512,512]{1,0:T(8,128)}, u32[]{:S(2)}) copy-start(f32[512,512]{1,0:T(8,128)} %get-tuple-element.37.half_ref) | copy-start | bytes 3145732
  69.9 26.5 %collective-permute-start.3 = (bf16[512,512]{1,0:T(8,128)(2,1)}, bf16[512,512]{1,0:T(8,128)(2,1)}, u32[]{:S(2)}, u32[]{:S(2)}) collective-permute-start(bf16[512,512]{1,0:T(8,128)(2,1)} %collective-permute-done.2), channel_id=1, source_target_pairs={{72,64},{73,65},{74,80},{75,81},{88,66},{89,67},{90,82},{91,83},{1... | collective-permute-start | bytes 1572872 | tf_op jit(solution)/shard_map/ppermute | solution.py:261
  71.2 28.2 %collective-permute-start = (bf16[512,512]{1,0:T(8,128)(2,1)}, bf16[512,512]{1,0:T(8,128)(2,1)}, u32[]{:S(2)}, u32[]{:S(2)}) collective-permute-start(bf16[512,512]{1,0:T(8,128)(2,1)} %get-tuple-element.39), channel_id=1, source_target_pairs={{0,1},{1,0},{2,17},{3,16},{16,3},{17,2},{18,19},{19,18},{4,33},{5,... | collective-permute-start | bytes 1572872 | tf_op jit(solution)/shard_map/ppermute | solution.py:261

commit v6 on v3

--- a/solution.py
+++ b/solution.py
@@ -37,23 +37,22 @@
     rest = w - high.astype(F32)
     mid = rest.astype(BF16)
     low = (rest - mid.astype(F32)).astype(BF16)
-    rhs = jnp.concatenate([in_ref[k] for k in range(n)], axis=0)
-    total = jnp.dot(high, rhs, preferred_element_type=F32)
-    total += jnp.dot(mid, rhs, preferred_element_type=F32)
-    total += jnp.dot(low, rhs, preferred_element_type=F32)
-    for j in range(n):
-        out_ref[j] = total[j * SUB : (j + 1) * SUB, :].astype(BF16)
+    for r in range(0, in_ref.shape[1], SUB):
+        rhs = jnp.concatenate([in_ref[k, r : r + SUB, :] for k in range(n)], axis=0)
+        total = jnp.dot(high, rhs, preferred_element_type=F32)
+        total += jnp.dot(mid, rhs, preferred_element_type=F32)
+        total += jnp.dot(low, rhs, preferred_element_type=F32)
+        for j in range(n):
+            out_ref[j, r : r + SUB, :] = total[j * SUB : (j + 1) * SUB, :].astype(BF16)
 
 
 def mix(wide, slices):
-    n, block, virt = slices.shape
-    strip = pl.BlockSpec((n, SUB, virt), lambda r: (0, r, 0))
     return pl.pallas_call(
         mix_kernel,
         out_shape=jax.ShapeDtypeStruct(slices.shape, BF16),
-        grid=(block // SUB,),
-        in_specs=[whole(wide.shape), strip],
-        out_specs=strip,
+        grid=(1,),
+        in_specs=[whole(wide.shape), whole(slices.shape)],
+        out_specs=whole(slices.shape),
         compiler_params=params(16),
         cost_estimate=pl.CostEstimate(
             flops=10**9, bytes_accessed=4 * slices.size, transcendentals=0
@@ -106,7 +105,7 @@
             out_specs=whole((virt, virt)),
             scratch_shapes=[pltpu.VMEM((rank, tile), BF16), pltpu.VMEM((rank, virt), BF16)],
         ),
-        compiler_params=params(56, dimension_semantics=("arbitrary",)),
+        compiler_params=params(54, dimension_semantics=("arbitrary",)),
         cost_estimate=pl.CostEstimate(
             flops=4 * virt * rank * (rank + virt) + 2 * virt**3,
             bytes_accessed=2 * rank * rank + 4 * virt * rank,
@@ -116,15 +115,15 @@
     )(slot, amps, ints, x, core, fock)
 
 
-def half_kernel(place, part_a, part_b, sum_ref, send_a, send_b):
-    core = place[0]
+def half_kernel(slot, part_a, part_b, sum_ref, send_a, send_b):
+    core = slot[0]
     send_a[...] = (part_a[...] - sum_ref[core].astype(F32)).astype(BF16)
     send_b[...] = (part_b[...] - sum_ref[1 - core].astype(F32)).astype(BF16)
 
 
-def half_of(place, part_a, part_b, sums):
+def half_of(slot, part_a, part_b, sums):
     virt = part_a.shape[0]
-    rows = min(128, virt)
+    rows = min(256, virt)
     strip = pl.BlockSpec((rows, virt), lambda r, s: (r, 0))
     return pl.pallas_call(
         half_kernel,
@@ -140,25 +139,28 @@
             flops=0, bytes_accessed=16 * part_a.size, transcendentals=0
         ),
         name="half",
-    )(place, part_a, part_b, sums)
-
-
-def finish_kernel(slot, part_ref, sum_ref, mirror_ref, amp_ref, col_ref, row_ref, occ_ref, *refs):
+    )(slot, part_a, part_b, sums)
+
+
+def finish_kernel(n, ids, part_ref, sum_ref, amp_ref, col_ref, row_ref, occ_ref, *refs):
     res_ref, new_ref = refs[-2:]
+    mirror = refs[0][...]
+    for kind in range(1, n):
+        mirror = jnp.where(ids[3] == kind, refs[kind][...], mirror)
     half = part_ref[...] - sum_ref[...].astype(F32)
-    residual = half + mirror_ref[...].astype(F32).T
-    denominator = col_ref[...] + row_ref[...] - occ_ref[0] - occ_ref[1]
+    residual = half + mirror.astype(F32).T
+    denominator = col_ref[...] + row_ref[...] - occ_ref[ids[1]] - occ_ref[ids[2]]
     res_ref[...] = residual
     new_ref[...] = (amp_ref[...].astype(F32) - residual / denominator).astype(BF16)
 
 
-def finish(slot, part, sums, mirror, amps, eps_col, eps_row, occ, held):
+def finish(ids, part, sums, mirrors, amps, eps_col, eps_row, eps_occ, held):
     virt = part.shape[0]
-    rows = min(128, virt)
+    rows = min(256, virt)
     strip = pl.BlockSpec((None, rows, virt), lambda r, s: (s[0], r, 0))
-    held_specs = [pl.BlockSpec(memory_space=pl.ANY)] * len(held)
-    return pl.pallas_call(
-        finish_kernel,
+    n = len(mirrors)
+    return pl.pallas_call(
+        functools.partial(finish_kernel, n),
         out_shape=[
             jax.ShapeDtypeStruct(amps.shape, F32),
             jax.ShapeDtypeStruct(amps.shape, BF16),
@@ -169,22 +171,22 @@
             in_specs=[
                 pl.BlockSpec((rows, virt), lambda r, s: (r, 0)),
                 strip,
-                pl.BlockSpec((virt, rows), lambda r, s: (0, r)),
                 strip,
                 pl.BlockSpec((rows, 1), lambda r, s: (r, 0)),
                 whole((1, virt)),
                 pl.BlockSpec(memory_space=pltpu.SMEM),
             ]
-            + held_specs,
+            + [pl.BlockSpec((virt, rows), lambda r, s: (0, r))] * n
+            + [pl.BlockSpec(memory_space=pl.ANY)] * len(held),
             out_specs=[strip, strip],
         ),
-        input_output_aliases={8 + n: n for n in range(len(held))},
+        input_output_aliases={7 + n + m: m for m in range(len(held))},
         compiler_params=params(16, dimension_semantics=("arbitrary",)),
         cost_estimate=pl.CostEstimate(
             flops=20 * part.size, bytes_accessed=14 * part.size, transcendentals=0
         ),
         name="finish",
-    )(slot, part, sums, mirror, amps, eps_col, eps_row, occ, *held)
+    )(ids, part, sums, amps, eps_col, eps_row, eps_occ, *mirrors, *held)
 
 
 def shards(
@@ -205,19 +207,43 @@
     me_i = lax.axis_index("occi")
     me_j = lax.axis_index("occj")
     core = me_j % 2
-    place = jnp.stack([core, me_j // 2]).astype(jnp.int32)
     slot_a = jnp.reshape(core, (1,)).astype(jnp.int32)
     slot_b = 1 - slot_a
     amps = amplitudes.reshape(rows_i, virt, virt)
     ints = exch_int.reshape(rows_i, virt, virt)
 
-    def mirror_hop(flip):
-        return [
-            (p * n_second + 2 * q + s, q * n_second + 2 * p + (s ^ flip))
-            for p in range(n_first)
-            for q in range(n_first)
-            for s in range(2)
-        ]
+    size = n_first // 2
+
+    def spot(y, low, x, high, c):
+        return (2 * y + low) * n_second + 2 * (2 * x + high) + c
+
+    def send(array, flip, diagonal=None, middle=None, other=None):
+        pairs = []
+        for y in range(size):
+            for x in range(size):
+                apart = (x - y) % size
+                route = {0: diagonal, size // 2: middle}.get(apart, other)
+                for low in range(2):
+                    for high in range(2):
+                        for c in range(2):
+                            ends = dict(
+                                mirror=((y, low, x, high), (x, high, y, low)),
+                                inward=((y, low, x, high), (x, low, x, high)),
+                                outward=((x, low, x, high), (x, high, y, low)),
+                            ).get(route)
+                            if ends:
+                                pairs.append((spot(*ends[0], c), spot(*ends[1], c ^ flip)))
+        return lax.ppermute(array, AXES, pairs)
+
+    apart = (me_j // 4 - me_i // 2) % size
+    kind = jnp.where(apart == size // 2, 1, jnp.where(apart == 0, 2, 0))
+    eps_col = eps_vir.reshape(virt, 1)
+    eps_row = eps_vir.reshape(1, virt)
+
+    def ids_of(slot):
+        return jnp.stack([slot[0], me_i * rows_i + slot[0], me_j, kind]).astype(jnp.int32)
+
+    ids_a, ids_b = ids_of(slot_a), ids_of(slot_b)
 
     slices = amps.reshape(n_second, rows_i * virt // n_second, virt)
     slices = lax.all_to_all(slices, "occj", 0, 0, tiled=True)
@@ -226,24 +252,25 @@
     lane = jnp.arange(n_second * SUB, dtype=jnp.int32) % SUB
     wide = jnp.where(lane[:, None] == lane[None, :], tall, 0.0)
     part_a = ladder(slot_a, amps, ints, thc_factor, thc_core, fock_vir)
-    slices, part_a = lax.optimization_barrier((slices, part_a))
+    slices, part_a, ids_a, ids_b, eps_col = lax.optimization_barrier(
+        (slices, part_a, ids_a, ids_b, eps_col)
+    )
     sums = mix(wide, slices)
+    sums, part_a, slot_b = lax.optimization_barrier((sums, part_a, slot_b))
     sums = lax.all_to_all(sums, "occj", 0, 0, tiled=True)
     part_b = ladder(slot_b, amps, ints, thc_factor, thc_core, fock_vir)
     sums, part_b = lax.optimization_barrier((sums, part_b))
     sums = sums.reshape(rows_i, virt, virt)
-    send_a, send_b = half_of(place, part_a, part_b, sums)
-    got_a = lax.ppermute(send_a, AXES, mirror_hop(0))
-    got_b = lax.ppermute(send_b, AXES, mirror_hop(1))
-
-    occ_rows = lax.dynamic_slice_in_dim(eps_occ, me_i * rows_i, rows_i, 0)
-    occ_column = lax.dynamic_slice_in_dim(eps_occ, me_j, 1, 0)
-    occ_a = jnp.stack([jnp.where(core == 0, occ_rows[0], occ_rows[1]), occ_column[0]])
-    occ_b = jnp.stack([jnp.where(core == 0, occ_rows[1], occ_rows[0]), occ_column[0]])
-    eps_col = eps_vir.reshape(virt, 1)
-    eps_row = eps_vir.reshape(1, virt)
-    held = finish(slot_a, part_a, sums, got_a, amps, eps_col, eps_row, occ_a, ())
-    residual, updated = finish(slot_b, part_b, sums, got_b, amps, eps_col, eps_row, occ_b, held)
+    send_a, send_b = half_of(slot_a, part_a, part_b, sums)
+    near_a = send(send_a, 0, middle="inward", other="mirror")
+    got_b = send(send_b, 1, diagonal="mirror", middle="mirror", other="mirror")
+    same_a = send(send_a, 0, diagonal="mirror")
+    far_a = send(near_a, 0, middle="outward")
+
+    held = finish(ids_b, part_b, sums, (got_b,), amps, eps_col, eps_row, eps_occ, ())
+    residual, updated = finish(
+        ids_a, part_a, sums, (near_a, far_a, same_a), amps, eps_col, eps_row, eps_occ, held
+    )
     return (
         residual.reshape(rows_i, 1, virt, virt),
         updated.reshape(rows_i, 1, virt, virt),

time: 114 us -> 104 us (0.912)
  the two profiles are of different devices: /device:TPU:57 before, /device:TPU:25 now
where the time goes in v6:
time: 104 us
  Pallas kernels  41.7 us (40%)
  waiting for transfers between devices  31.7 us (30%)
  starting transfers between devices  26.3 us (25%)
  local copies, waits for them, and re-layouts  3.05 us (3%)
    pallas_call x2, Pallas kernels, ladder(): pl.pallas_call(ladder_kernel, out_shape=jax.ShapeDtypeStruct((virt, virt)...  32.7 us
    ppermute x4, waiting for transfers between devices, send(): return lax.ppermute(array, AXES, pairs)  30.8 us
    ppermute x4, starting transfers between devices, send(): return lax.ppermute(array, AXES, pairs)  10.7 us
    all_to_all x1, starting transfers between devices, shards(): slices = lax.all_to_all(slices, 'occj', 0, 0, tiled=True)  8.44 us
    all_to_all x1, starting transfers between devices, shards(): sums = lax.all_to_all(sums, 'occj', 0, 0, tiled=True)  7.11 us
    pallas_call x2, Pallas kernels, finish(): pl.pallas_call(functools.partial(finish_kernel, n), out_shape=[jax.ShapeD...  5.91 us
    unnamed x18, local copies, waits for them, and re-layouts  2.48 us
  transfers between devices with their start and end apart: 6, of which 4 were waited for; matrix products, arithmetic and copies ran while one was open for 1% of the time, Pallas kernels for 34%

profile of v6, /device:TPU:25, one launch (start us, length us, event | category | flops | bytes accessed | tf_op | source)
XLA Modules:
  0.0 103.7 jit_solution(8654128262382758530)
XLA Ops:
  0.6 0.0 copy-start.8
  0.6 0.0 copy-start.7
  0.7 8.4 %all-to-all-start = ((bf16[16,64,512]{2,1,0:T(8,128)(2,1)}), bf16[16,64,512]{2,1,0:T(8,128)(2,1)S(1)}, u32[]{:S(2)}, u32[]{:S(2)}) async-start(bf16[16,64,512]{2,1,0:T(8,128)(2,1)} %bitcast.24), calls=%async_computation | async-start | bytes 2097152 | tf_op jit(solution)/shard_map/all_to_all | solution.py:249
  9.2 0.1 convert_reduce_fusion
  9.3 0.1 copy.24
  9.4 0.1 broadcast_in_dim.7
  9.5 0.1 reshape.78
  9.6 0.1 copy.25
  9.7 0.1 compare_select_fusion.w_ref
  9.8 0.1 add_add_fusion
  9.9 16.3 %ladder.2.part_a.part_ref = f32[512,512]{1,0:T(8,128)} custom-call(s32[1]{0:T(128)} %bitcast.1.slot, bf16[2,512,512]{2,1,0:T(8,128)(2,1)} %bitcast.25, bf16[2,512,512]{2,1,0:T(8,128)(2,1)} %bitcast.35, bf16[512,2048]{1,0:T(8,128)(2,1)} %x_ref.3, bf16[2048,2048]{1,0:T(8,128)(2,1)} %core_ref.3, bf16[512,512]{1,0:T(8,128)(2,1)} %fock_ref.3), custom_call_target="tpu_custom_call" | custom-call | flops 11005853696 | bytes 12582912 | tf_op jit(solution)/shard_map/ladder/pallas_call | solution.py:92
  26.2 0.1 all-to-all-done.in_ref
  26.3 2.0 %mix.1 = bf16[16,64,512]{2,1,0:T(8,128)(2,1)} custom-call(f32[256,256]{1,0:T(8,128)S(1)} %compare_select_fusion.w_ref, bf16[16,64,512]{2,1,0:T(8,128)(2,1)S(1)} %all-to-all-done.in_ref), custom_call_target="tpu_custom_call" | custom-call | flops 1000000000 | bytes 2097152 | tf_op jit(solution)/shard_map/mix/pallas_call | solution.py:50
  28.3 7.1 %all-to-all-start.1 = ((bf16[16,64,512]{2,1,0:T(8,128)(2,1)}), bf16[16,64,512]{2,1,0:T(8,128)(2,1)S(1)}, u32[]{:S(2)}, u32[]{:S(2)}) async-start(bf16[16,64,512]{2,1,0:T(8,128)(2,1)} %mix.1), calls=%async_computation.1 | async-start | bytes 2097152 | tf_op jit(solution)/shard_map/all_to_all | solution.py:260
  35.4 0.0 copy-start.4
  35.4 0.0 copy-start.5
  35.4 16.4 %ladder.3.part_b.part_ref = f32[512,512]{1,0:T(8,128)} custom-call(s32[1]{0:T(128)} %sub.16.slot, bf16[2,512,512]{2,1,0:T(8,128)(2,1)} %bitcast.26, bf16[2,512,512]{2,1,0:T(8,128)(2,1)} %bitcast.36, bf16[512,2048]{1,0:T(8,128)(2,1)} %x_ref.3, bf16[2048,2048]{1,0:T(8,128)(2,1)} %core_ref.3, bf16[512,512]{1,0:T(8,128)(2,1)} %fock_ref.3), custom_call_target="tpu_custom_call" | custom-call | flops 11005853696 | bytes 12582912 | tf_op jit(solution)/shard_map/ladder/pallas_call | solution.py:92
  51.8 0.8 all-to-all-done.1
  52.6 1.2 %copy-done.2 = f32[512,512]{1,0:T(8,128)S(1)} copy-done((f32[512,512]{1,0:T(8,128)S(1)}, f32[512,512]{1,0:T(8,128)}, u32[]{:S(2)}) %copy-start.2) | copy-done | bytes 1048600
  53.8 1.1 %half.1 = (bf16[512,512]{1,0:T(8,128)(2,1)}, bf16[512,512]{1,0:T(8,128)(2,1)}) custom-call(s32[1]{0:T(128)} %bitcast.1.slot, f32[512,512]{1,0:T(8,128)S(1)} %copy-done.1, f32[512,512]{1,0:T(8,128)S(1)} %copy-done.2, bf16[2,512,512]{2,1,0:T(8,128)(2,1)S(1)} %bitcast.21), custom_call_target="tpu_custom_call" | custom-call | bytes 4194304 | tf_op jit(solution)/shard_map/half/pallas_call | solution.py:128
  54.9 3.5 %collective-permute-start = (bf16[512,512]{1,0:T(8,128)(2,1)}, bf16[512,512]{1,0:T(8,128)(2,1)}, u32[]{:S(2)}, u32[]{:S(2)}) collective-permute-start(bf16[512,512]{1,0:T(8,128)(2,1)} %get-tuple-element.27), channel_id=1, source_target_pairs={{4,32},{5,33},{6,48},{7,49},{20,34},{21,35},{22,50},{23,51},{8,72}... | collective-permute-start | bytes 1572872 | tf_op jit(solution)/shard_map/ppermute | solution.py:236
  58.4 4.3 %collective-permute-start.3 = (bf16[512,512]{1,0:T(8,128)(2,1)}, bf16[512,512]{1,0:T(8,128)(2,1)}, u32[]{:S(2)}, u32[]{:S(2)}) collective-permute-start(bf16[512,512]{1,0:T(8,128)(2,1)} %get-tuple-element.29), channel_id=1, source_target_pairs={{0,1},{1,0},{2,17},{3,16},{16,3},{17,2},{18,19},{19,18},{4,33},{5,... | collective-permute-start | bytes 1572872 | tf_op jit(solution)/shard_map/ppermute | solution.py:236
  62.8 1.5 %collective-permute-start.2 = (bf16[512,512]{1,0:T(8,128)(2,1)}, bf16[512,512]{1,0:T(8,128)(2,1)}, u32[]{:S(2)}, u32[]{:S(2)}) collective-permute-start(bf16[512,512]{1,0:T(8,128)(2,1)} %get-tuple-element.27), channel_id=1, source_target_pairs={{0,0},{1,1},{2,16},{3,17},{16,2},{17,3},{18,18},{19,19},{36,36},{3... | collective-permute-start | bytes 1572872 | tf_op jit(solution)/shard_map/ppermute | solution.py:236
  64.2 20.1 %collective-permute-done.refs_0_ = bf16[512,512]{1,0:T(8,128)(2,1)} collective-permute-done((bf16[512,512]{1,0:T(8,128)(2,1)}, bf16[512,512]{1,0:T(8,128)(2,1)}, u32[]{:S(2)}, u32[]{:S(2)}) %collective-permute-start) | collective-permute-done | bytes 524320 | tf_op jit(solution)/shard_map/ppermute | solution.py:236
  84.3 1.5 %collective-permute-start.1 = (bf16[512,512]{1,0:T(8,128)(2,1)}, bf16[512,512]{1,0:T(8,128)(2,1)}, u32[]{:S(2)}, u32[]{:S(2)}) collective-permute-start(bf16[512,512]{1,0:T(8,128)(2,1)} %collective-permute-done.refs_0_), channel_id=1, source_target_pairs={{72,64},{73,65},{74,80},{75,81},{88,66},{89,67},{90,82},{91,83},{1... | collective-permute-start | bytes 1572872 | tf_op jit(solution)/shard_map/ppermute | solution.py:236
  85.7 0.1 copy.27.col_ref
  85.9 10.7 %collective-permute-done.3.refs_0_ = bf16[512,512]{1,0:T(8,128)(2,1)} collective-permute-done((bf16[512,512]{1,0:T(8,128)(2,1)}, bf16[512,512]{1,0:T(8,128)(2,1)}, u32[]{:S(2)}, u32[]{:S(2)}) %collective-permute-start.3) | collective-permute-done | bytes 524320 | tf_op jit(solution)/shard_map/ppermute | solution.py:236
  96.6 1.2 %copy-done.3 = f32[512,512]{1,0:T(8,128)S(1)} copy-done((f32[512,512]{1,0:T(8,128)S(1)}, f32[512,512]{1,0:T(8,128)}, u32[]{:S(2)}) %copy-start.3) | copy-done | bytes 1048600
  97.8 2.9 %finish.2 = (f32[2,512,512]{2,1,0:T(8,128)}, bf16[2,512,512]{2,1,0:T(8,128)(2,1)}) custom-call(s32[4]{0:T(128)S(1)} %get-tuple-element.28.ids, f32[512,512]{1,0:T(8,128)S(1)} %copy-done.3, bf16[2,512,512]{2,1,0:T(8,128)(2,1)S(1)} %bitcast.22, bf16[2,512,512]{2,1,0:T(8,128)(2,1)S(1)} %bitcast.27, f32[512,1]{1,0:T(8,128)S(1)} %copy.27.col_ref, ...), custom_call_target="tpu_custom_call" | custom-call | flops 5242880 | bytes 3670016 | tf_op jit(solution)/shard_map/finish/pallas_call | solution.py:162
  100.7 0.0 collective-permute-done.2.refs_2_
  100.7 0.0 collective-permute-done.1.refs_1_
  100.7 3.0 %finish.3 = (f32[2,512,512]{2,1,0:T(8,128)}, bf16[2,512,512]{2,1,0:T(8,128)(2,1)}) custom-call(s32[4]{0:T(128)S(1)} %get-tuple-element.18.ids, f32[512,512]{1,0:T(8,128)S(1)} %copy-done.1, bf16[2,512,512]{2,1,0:T(8,128)(2,1)S(1)} %bitcast.23, bf16[2,512,512]{2,1,0:T(8,128)(2,1)S(1)} %bitcast.28, ...), custom_call_target="tpu_custom_call", output_to_operand_aliasing={{0}: (10, {}), {1}: (11, {})} | custom-call | flops 5242880 | bytes 3670016 | tf_op jit(solution)/shard_map/finish/pallas_call | solution.py:162
  (16 shorter events, 0.1 us)
Async XLA Ops:
  0.6 8.5 %copy-start.8 = (s32[16]{0:T(128)S(1)}, s32[16]{0:T(128)}, u32[]{:S(2)}) copy-start(s32[16]{0:T(128)} %param.19) | copy-start | bytes 196
  0.6 8.5 %copy-start.7 = (s32[16,6]{0,1:T(8,128)S(1)}, s32[16,6]{0,1:T(8,128)}, u32[]{:S(2)}) copy-start(s32[16,6]{0,1:T(8,128)} %param.18) | copy-start | bytes 1156
  0.7 8.6 %copy-start.6 = (f32[16,16]{1,0:T(8,128)S(1)}, f32[16,16]{1,0:T(8,128)}, u32[]{:S(2)}) copy-start(f32[16,16]{1,0:T(8,128)} %param.17) | copy-start | bytes 3076
  0.7 25.7 %all-to-all-start = ((bf16[16,64,512]{2,1,0:T(8,128)(2,1)}), bf16[16,64,512]{2,1,0:T(8,128)(2,1)S(1)}, u32[]{:S(2)}, u32[]{:S(2)}) async-start(bf16[16,64,512]{2,1,0:T(8,128)(2,1)} %bitcast.24), calls=%async_computation | async-start | bytes 2097152 | tf_op jit(solution)/shard_map/all_to_all | solution.py:249
  28.3 24.3 %all-to-all-start.1 = ((bf16[16,64,512]{2,1,0:T(8,128)(2,1)}), bf16[16,64,512]{2,1,0:T(8,128)(2,1)S(1)}, u32[]{:S(2)}, u32[]{:S(2)}) async-start(bf16[16,64,512]{2,1,0:T(8,128)(2,1)} %mix.1), calls=%async_computation.1 | async-start | bytes 2097152 | tf_op jit(solution)/shard_map/all_to_all | solution.py:260
  35.4 17.2 %copy-start.1 = (f32[512,512]{1,0:T(8,128)S(1)}, f32[512,512]{1,0:T(8,128)}, u32[]{:S(2)}) copy-start(f32[512,512]{1,0:T(8,128)} %ladder.2.part_a.part_ref) | copy-start | bytes 3145732
  35.4 50.3 %copy-start.4 = (f32[512]{0:T(512)S(1)}, f32[512]{0:T(512)}, u32[]{:S(2)}) copy-start(f32[512]{0:T(512)} %param.15) | copy-start | bytes 6148
  35.4 61.2 %copy-start.5 = (f32[16]{0:T(128)S(1)}, f32[16]{0:T(128)}, u32[]{:S(2)}) copy-start(f32[16]{0:T(128)} %occ_ref.3) | copy-start | bytes 196
  51.8 44.8 %copy-start = (bf16[2,1,512,512]{3,2,1,0:T(8,128)(2,1)S(1)}, bf16[2,1,512,512]{3,2,1,0:T(8,128)(2,1)}, u32[]{:S(2)}) copy-start(bf16[2,1,512,512]{3,2,1,0:T(8,128)(2,1)} %param.10) | copy-start | bytes 3145732
  52.6 1.2 %copy-start.2 = (f32[512,512]{1,0:T(8,128)S(1)}, f32[512,512]{1,0:T(8,128)}, u32[]{:S(2)}) copy-start(f32[512,512]{1,0:T(8,128)} %ladder.3.part_b.part_ref) | copy-start | bytes 3145732
  54.9 29.3 %collective-permute-start = (bf16[512,512]{1,0:T(8,128)(2,1)}, bf16[512,512]{1,0:T(8,128)(2,1)}, u32[]{:S(2)}, u32[]{:S(2)}) collective-permute-start(bf16[512,512]{1,0:T(8,128)(2,1)} %get-tuple-element.27), channel_id=1, source_target_pairs={{4,32},{5,33},{6,48},{7,49},{20,34},{21,35},{22,50},{23,51},{8,72}... | collective-permute-start | bytes 1572872 | tf_op jit(solution)/shard_map/ppermute | solution.py:236
  58.4 38.2 %collective-permute-start.3 = (bf16[512,512]{1,0:T(8,128)(2,1)}, bf16[512,512]{1,0:T(8,128)(2,1)}, u32[]{:S(2)}, u32[]{:S(2)}) collective-permute-start(bf16[512,512]{1,0:T(8,128)(2,1)} %get-tuple-element.29), channel_id=1, source_target_pairs={{0,1},{1,0},{2,17},{3,16},{16,3},{17,2},{18,19},{19,18},{4,33},{5,... | collective-permute-start | bytes 1572872 | tf_op jit(solution)/shard_map/ppermute | solution.py:236
  62.8 37.9 %collective-permute-start.2 = (bf16[512,512]{1,0:T(8,128)(2,1)}, bf16[512,512]{1,0:T(8,128)(2,1)}, u32[]{:S(2)}, u32[]{:S(2)}) collective-permute-start(bf16[512,512]{1,0:T(8,128)(2,1)} %get-tuple-element.27), channel_id=1, source_target_pairs={{0,0},{1,1},{2,16},{3,17},{16,2},{17,3},{18,18},{19,19},{36,36},{3... | collective-permute-start | bytes 1572872 | tf_op jit(solution)/shard_map/ppermute | solution.py:236
  84.3 16.4 %collective-permute-start.1 = (bf16[512,512]{1,0:T(8,128)(2,1)}, bf16[512,512]{1,0:T(8,128)(2,1)}, u32[]{:S(2)}, u32[]{:S(2)}) collective-permute-start(bf16[512,512]{1,0:T(8,128)(2,1)} %collective-permute-done.refs_0_), channel_id=1, source_target_pairs={{72,64},{73,65},{74,80},{75,81},{88,66},{89,67},{90,82},{91,83},{1... | collective-permute-start | bytes 1572872 | tf_op jit(solution)/shard_map/ppermute | solution.py:236
  96.6 1.2 %copy-start.3 = (f32[512,512]{1,0:T(8,128)S(1)}, f32[512,512]{1,0:T(8,128)}, u32[]{:S(2)}) copy-start(f32[512,512]{1,0:T(8,128)} %ladder.3.part_b.part_ref) | copy-start | bytes 3145732

commit v7 on v6

--- a/solution.py
+++ b/solution.py
@@ -115,24 +115,32 @@
     )(slot, amps, ints, x, core, fock)
 
 
-def half_kernel(slot, part_a, part_b, sum_ref, send_a, send_b):
+def half_kernel(slot, part_a, part_b, sum_ref, send_a, low_b, high_b):
     core = slot[0]
     send_a[...] = (part_a[...] - sum_ref[core].astype(F32)).astype(BF16)
-    send_b[...] = (part_b[...] - sum_ref[1 - core].astype(F32)).astype(BF16)
+    rounded = (part_b[...] - sum_ref[1 - core].astype(F32)).astype(BF16)
+
+    @pl.when(pl.program_id(0) == 0)
+    def _():
+        low_b[...] = rounded
+
+    @pl.when(pl.program_id(0) == 1)
+    def _():
+        high_b[...] = rounded
 
 
 def half_of(slot, part_a, part_b, sums):
     virt = part_a.shape[0]
-    rows = min(256, virt)
+    rows = virt // 2
     strip = pl.BlockSpec((rows, virt), lambda r, s: (r, 0))
     return pl.pallas_call(
         half_kernel,
-        out_shape=[jax.ShapeDtypeStruct(part_a.shape, BF16)] * 2,
+        out_shape=[jax.ShapeDtypeStruct((n, virt), BF16) for n in (virt, rows, rows)],
         grid_spec=pltpu.PrefetchScalarGridSpec(
             num_scalar_prefetch=1,
-            grid=(virt // rows,),
+            grid=(2,),
             in_specs=[strip, strip, pl.BlockSpec((2, rows, virt), lambda r, s: (0, r, 0))],
-            out_specs=[strip, strip],
+            out_specs=[strip, whole((rows, virt)), whole((rows, virt))],
         ),
         compiler_params=params(16),
         cost_estimate=pl.CostEstimate(
@@ -142,11 +150,16 @@
     )(slot, part_a, part_b, sums)
 
 
-def finish_kernel(n, ids, part_ref, sum_ref, amp_ref, col_ref, row_ref, occ_ref, *refs):
+def finish_kernel(counts, ids, part_ref, sum_ref, amp_ref, col_ref, row_ref, occ_ref, *refs):
     res_ref, new_ref = refs[-2:]
-    mirror = refs[0][...]
-    for kind in range(1, n):
-        mirror = jnp.where(ids[3] == kind, refs[kind][...], mirror)
+    pieces = []
+    for n in counts:
+        piece = refs[0][...]
+        for kind in range(1, n):
+            piece = jnp.where(ids[3] == kind, refs[kind][...], piece)
+        pieces.append(piece)
+        refs = refs[n:]
+    mirror = jnp.concatenate(pieces, axis=0)
     half = part_ref[...] - sum_ref[...].astype(F32)
     residual = half + mirror.astype(F32).T
     denominator = col_ref[...] + row_ref[...] - occ_ref[ids[1]] - occ_ref[ids[2]]
@@ -158,9 +171,10 @@
     virt = part.shape[0]
     rows = min(256, virt)
     strip = pl.BlockSpec((None, rows, virt), lambda r, s: (s[0], r, 0))
-    n = len(mirrors)
+    counts = [len(piece) for piece in mirrors]
+    mirrors = sum(mirrors, ())
     return pl.pallas_call(
-        functools.partial(finish_kernel, n),
+        functools.partial(finish_kernel, counts),
         out_shape=[
             jax.ShapeDtypeStruct(amps.shape, F32),
             jax.ShapeDtypeStruct(amps.shape, BF16),
@@ -176,11 +190,11 @@
                 whole((1, virt)),
                 pl.BlockSpec(memory_space=pltpu.SMEM),
             ]
-            + [pl.BlockSpec((virt, rows), lambda r, s: (0, r))] * n
+            + [pl.BlockSpec((m.shape[0], rows), lambda r, s: (0, r)) for m in mirrors]
             + [pl.BlockSpec(memory_space=pl.ANY)] * len(held),
             out_specs=[strip, strip],
         ),
-        input_output_aliases={7 + n + m: m for m in range(len(held))},
+        input_output_aliases={7 + sum(counts) + m: m for m in range(len(held))},
         compiler_params=params(16, dimension_semantics=("arbitrary",)),
         cost_estimate=pl.CostEstimate(
             flops=20 * part.size, bytes_accessed=14 * part.size, transcendentals=0
@@ -261,16 +275,23 @@
     part_b = ladder(slot_b, amps, ints, thc_factor, thc_core, fock_vir)
     sums, part_b = lax.optimization_barrier((sums, part_b))
     sums = sums.reshape(rows_i, virt, virt)
-    send_a, send_b = half_of(slot_a, part_a, part_b, sums)
+    send_a, low_b, high_b = half_of(slot_a, part_a, part_b, sums)
     near_a = send(send_a, 0, middle="inward", other="mirror")
-    got_b = send(send_b, 1, diagonal="mirror", middle="mirror", other="mirror")
+    near_b = send(high_b, 1, middle="inward", other="mirror")
+    low_b = send(low_b, 1, diagonal="mirror", middle="mirror", other="mirror")
     same_a = send(send_a, 0, diagonal="mirror")
+    same_b = send(high_b, 1, diagonal="mirror")
+    near_a, low_b = lax.optimization_barrier((near_a, low_b))
+    near_b, low_b = lax.optimization_barrier((near_b, low_b))
     far_a = send(near_a, 0, middle="outward")
-
-    held = finish(ids_b, part_b, sums, (got_b,), amps, eps_col, eps_row, eps_occ, ())
-    residual, updated = finish(
-        ids_a, part_a, sums, (near_a, far_a, same_a), amps, eps_col, eps_row, eps_occ, held
-    )
+    far_b = send(near_b, 0, middle="outward")
+
+    far_a, far_b = lax.optimization_barrier((far_a, far_b))
+    tables = (amps, eps_col, eps_row, eps_occ)
+    mirror_a = [(near_a, far_a, same_a)]
+    mirror_b = [(low_b,), (near_b, far_b, same_b)]
+    held = finish(ids_a, part_a, sums, mirror_a, *tables, ())
+    residual, updated = finish(ids_b, part_b, sums, mirror_b, *tables, held)
     return (
         residual.reshape(rows_i, 1, virt, virt),
         updated.reshape(rows_i, 1, virt, virt),

time: 104 us -> 110 us (1.058)
  the two profiles are of different devices: /device:TPU:25 before, /device:TPU:36 now
where the time goes in v7:
time: 110 us; the launch traced here: 108 us
  Pallas kernels  41.8 us (38%)
  waiting for transfers between devices  33.4 us (30%)
  starting transfers between devices  29 us (26%)
  local copies, waits for them, and re-layouts  2.59 us (2%)
    ppermute x7, waiting for transfers between devices, send(): return lax.ppermute(array, AXES, pairs)  33.4 us
    pallas_call x2, Pallas kernels, ladder(): pl.pallas_call(ladder_kernel, out_shape=jax.ShapeDtypeStruct((virt, virt)...  32.7 us
    ppermute x7, starting transfers between devices, send(): return lax.ppermute(array, AXES, pairs)  14.4 us
    all_to_all x1, starting transfers between devices, shards(): slices = lax.all_to_all(slices, 'occj', 0, 0, tiled=True)  7.38 us
    all_to_all x1, starting transfers between devices, shards(): sums = lax.all_to_all(sums, 'occj', 0, 0, tiled=True)  7.22 us
    pallas_call x2, Pallas kernels, finish(): pl.pallas_call(functools.partial(finish_kernel, counts), out_shape=[jax.S...  6.01 us
  transfers between devices with their start and end apart: 9, of which 2 were waited for; matrix products, arithmetic and copies ran while one was open for 1% of the time, Pallas kernels for 33%

profile of v7, /device:TPU:36, one launch (start us, length us, event | category | flops | bytes accessed | tf_op | source)
XLA Modules:
  0.0 107.9 jit_solution(13312210971319283707)
XLA Ops:
  0.7 7.4 %all-to-all-start = ((bf16[16,64,512]{2,1,0:T(8,128)(2,1)}), bf16[16,64,512]{2,1,0:T(8,128)(2,1)S(1)}, u32[]{:S(2)}, u32[]{:S(2)}) async-start(bf16[16,64,512]{2,1,0:T(8,128)(2,1)} %bitcast.24), calls=%async_computation | async-start | bytes 2097152 | tf_op jit(solution)/shard_map/all_to_all | solution.py:263
  8.1 0.1 convert_reduce_fusion
  8.2 0.1 copy.24
  8.3 0.1 broadcast_in_dim.7
  8.4 0.1 reshape.78
  8.5 0.1 copy.25
  8.7 0.1 compare_select_fusion.w_ref
  8.8 0.1 add_add_fusion
  8.9 16.3 %ladder.2.part_a.part_ref = f32[512,512]{1,0:T(8,128)} custom-call(s32[1]{0:T(128)} %bitcast.1.slot, bf16[2,512,512]{2,1,0:T(8,128)(2,1)} %bitcast.25, bf16[2,512,512]{2,1,0:T(8,128)(2,1)} %bitcast.35, bf16[512,2048]{1,0:T(8,128)(2,1)} %x_ref.3, bf16[2048,2048]{1,0:T(8,128)(2,1)} %core_ref.3, bf16[512,512]{1,0:T(8,128)(2,1)} %fock_ref.3), custom_call_target="tpu_custom_call" | custom-call | flops 11005853696 | bytes 12582912 | tf_op jit(solution)/shard_map/ladder/pallas_call | solution.py:92
  25.1 2.0 %mix.1 = bf16[16,64,512]{2,1,0:T(8,128)(2,1)} custom-call(f32[256,256]{1,0:T(8,128)S(1)} %compare_select_fusion.w_ref, bf16[16,64,512]{2,1,0:T(8,128)(2,1)S(1)} %all-to-all-done.in_ref), custom_call_target="tpu_custom_call" | custom-call | flops 1000000000 | bytes 2097152 | tf_op jit(solution)/shard_map/mix/pallas_call | solution.py:50
  27.1 7.2 %all-to-all-start.1 = ((bf16[16,64,512]{2,1,0:T(8,128)(2,1)}), bf16[16,64,512]{2,1,0:T(8,128)(2,1)S(1)}, u32[]{:S(2)}, u32[]{:S(2)}) async-start(bf16[16,64,512]{2,1,0:T(8,128)(2,1)} %mix.1), calls=%async_computation.1 | async-start | bytes 2097152 | tf_op jit(solution)/shard_map/all_to_all | solution.py:274
  34.3 0.0 copy-start.6
  34.3 0.0 copy-start.7
  34.4 16.4 %ladder.3.part_b.part_ref = f32[512,512]{1,0:T(8,128)} custom-call(s32[1]{0:T(128)} %sub.16.slot, bf16[2,512,512]{2,1,0:T(8,128)(2,1)} %bitcast.26, bf16[2,512,512]{2,1,0:T(8,128)(2,1)} %bitcast.36, bf16[512,2048]{1,0:T(8,128)(2,1)} %x_ref.3, bf16[2048,2048]{1,0:T(8,128)(2,1)} %core_ref.3, bf16[512,512]{1,0:T(8,128)(2,1)} %fock_ref.3), custom_call_target="tpu_custom_call" | custom-call | flops 11005853696 | bytes 12582912 | tf_op jit(solution)/shard_map/ladder/pallas_call | solution.py:92
  50.7 0.0 all-to-all-done.1
  50.8 1.3 %copy-done.2 = f32[512,512]{1,0:T(8,128)S(1)} copy-done((f32[512,512]{1,0:T(8,128)S(1)}, f32[512,512]{1,0:T(8,128)}, u32[]{:S(2)}) %copy-start.2) | copy-done | bytes 1048600
  52.1 1.2 %half.1 = (bf16[512,512]{1,0:T(8,128)(2,1)}, bf16[256,512]{1,0:T(8,128)(2,1)S(1)}, bf16[256,512]{1,0:T(8,128)(2,1)}) custom-call(s32[1]{0:T(128)} %bitcast.1.slot, f32[512,512]{1,0:T(8,128)S(1)} %copy-done.1, f32[512,512]{1,0:T(8,128)S(1)} %copy-done.2, bf16[2,512,512]{2,1,0:T(8,128)(2,1)S(1)} %bitcast.21), custom_call_target="tpu_custom_call" | custom-call | bytes 4194304 | tf_op jit(solution)/shard_map/half/pallas_call | solution.py:136
  53.2 5.9 %collective-permute-start.1 = (bf16[512,512]{1,0:T(8,128)(2,1)}, bf16[512,512]{1,0:T(8,128)(2,1)}, u32[]{:S(2)}, u32[]{:S(2)}) collective-permute-start(bf16[512,512]{1,0:T(8,128)(2,1)} %get-tuple-element.35), channel_id=1, source_target_pairs={{4,32},{5,33},{6,48},{7,49},{20,34},{21,35},{22,50},{23,51},{8,72}... | collective-permute-start | bytes 1572872 | tf_op jit(solution)/shard_map/ppermute | solution.py:250
  59.1 1.2 %collective-permute-start.2 = (bf16[256,512]{1,0:T(8,128)(2,1)S(1)}, bf16[256,512]{1,0:T(8,128)(2,1)S(1)}, u32[]{:S(2)}, u32[]{:S(2)}) collective-permute-start(bf16[256,512]{1,0:T(8,128)(2,1)S(1)} %get-tuple-element.36), channel_id=1, source_target_pairs={{0,1},{1,0},{2,17},{3,16},{16,3},{17,2},{18,19},{19,18},{4,33},{5,... | collective-permute-start | bytes 786440 | tf_op jit(solution)/shard_map/ppermute | solution.py:250
  60.3 2.0 %collective-permute-start = (bf16[256,512]{1,0:T(8,128)(2,1)}, bf16[256,512]{1,0:T(8,128)(2,1)}, u32[]{:S(2)}, u32[]{:S(2)}) collective-permute-start(bf16[256,512]{1,0:T(8,128)(2,1)} %get-tuple-element.34), channel_id=1, source_target_pairs={{4,33},{5,32},{6,49},{7,48},{20,35},{21,34},{22,51},{23,50},{8,73}... | collective-permute-start | bytes 786440 | tf_op jit(solution)/shard_map/ppermute | solution.py:250
  62.3 14.9 %collective-permute-done.2.refs_0_ = bf16[256,512]{1,0:T(8,128)(2,1)S(1)} collective-permute-done((bf16[256,512]{1,0:T(8,128)(2,1)S(1)}, bf16[256,512]{1,0:T(8,128)(2,1)S(1)}, u32[]{:S(2)}, u32[]{:S(2)}) %collective-permute-start.2) | collective-permute-done | bytes 262176 | tf_op jit(solution)/shard_map/ppermute | solution.py:250
  77.2 0.7 copy-done.4
  77.9 0.0 collective-permute-done.1.refs_0_
  77.9 1.3 %collective-permute-start.3 = (bf16[512,512]{1,0:T(8,128)(2,1)}, bf16[512,512]{1,0:T(8,128)(2,1)}, u32[]{:S(2)}, u32[]{:S(2)}) collective-permute-start(bf16[512,512]{1,0:T(8,128)(2,1)} %collective-permute-done.1.refs_0_), channel_id=1, source_target_pairs={{72,64},{73,65},{74,80},{75,81},{88,66},{89,67},{90,82},{91,83},{1... | collective-permute-start | bytes 1572872 | tf_op jit(solution)/shard_map/ppermute | solution.py:250
  79.2 1.5 %collective-permute-start.6 = (bf16[512,512]{1,0:T(8,128)(2,1)}, bf16[512,512]{1,0:T(8,128)(2,1)}, u32[]{:S(2)}, u32[]{:S(2)}) collective-permute-start(bf16[512,512]{1,0:T(8,128)(2,1)} %get-tuple-element.35), channel_id=1, source_target_pairs={{0,0},{1,1},{2,16},{3,17},{16,2},{17,3},{18,18},{19,19},{36,36},{3... | collective-permute-start | bytes 1572872 | tf_op jit(solution)/shard_map/ppermute | solution.py:250
  80.6 1.3 %collective-permute-start.4 = (bf16[256,512]{1,0:T(8,128)(2,1)}, bf16[256,512]{1,0:T(8,128)(2,1)}, u32[]{:S(2)}, u32[]{:S(2)}) collective-permute-start(bf16[256,512]{1,0:T(8,128)(2,1)} %collective-permute-done.refs_1_), channel_id=1, source_target_pairs={{72,64},{73,65},{74,80},{75,81},{88,66},{89,67},{90,82},{91,83},{1... | collective-permute-start | bytes 786440 | tf_op jit(solution)/shard_map/ppermute | solution.py:250
  81.9 1.4 %collective-permute-start.5 = (bf16[256,512]{1,0:T(8,128)(2,1)}, bf16[256,512]{1,0:T(8,128)(2,1)}, u32[]{:S(2)}, u32[]{:S(2)}) collective-permute-start(bf16[256,512]{1,0:T(8,128)(2,1)} %get-tuple-element.34), channel_id=1, source_target_pairs={{0,1},{1,0},{2,17},{3,16},{16,3},{17,2},{18,19},{19,18},{36,37},{3... | collective-permute-start | bytes 786440 | tf_op jit(solution)/shard_map/ppermute | solution.py:250
  83.3 0.1 copy.27.col_ref
  83.4 18.4 %collective-permute-done.4.refs_2_ = bf16[256,512]{1,0:T(8,128)(2,1)} collective-permute-done((bf16[256,512]{1,0:T(8,128)(2,1)}, bf16[256,512]{1,0:T(8,128)(2,1)}, u32[]{:S(2)}, u32[]{:S(2)}) %collective-permute-start.4) | collective-permute-done | bytes 262176 | tf_op jit(solution)/shard_map/ppermute | solution.py:250
  101.9 0.0 collective-permute-done.3.refs_1_
  101.9 3.0 %finish.2 = (f32[2,512,512]{2,1,0:T(8,128)}, bf16[2,512,512]{2,1,0:T(8,128)(2,1)}) custom-call(s32[4]{0:T(128)S(1)} %get-tuple-element.42.ids, f32[512,512]{1,0:T(8,128)S(1)} %copy-done.1, bf16[2,512,512]{2,1,0:T(8,128)(2,1)S(1)} %bitcast.22, bf16[2,512,512]{2,1,0:T(8,128)(2,1)S(1)} %bitcast.27, f32[512,1]{1,0:T(8,128)S(1)} %copy.27.col_ref, ...), custom_call_target="tpu_custom_call" | custom-call | flops 5242880 | bytes 3670016 | tf_op jit(solution)/shard_map/finish/pallas_call | solution.py:176
  105.0 3.0 %finish.3 = (f32[2,512,512]{2,1,0:T(8,128)}, bf16[2,512,512]{2,1,0:T(8,128)(2,1)}) custom-call(s32[4]{0:T(128)S(1)} %get-tuple-element.25.ids, f32[512,512]{1,0:T(8,128)S(1)} %copy-done.3, bf16[2,512,512]{2,1,0:T(8,128)(2,1)S(1)} %bitcast.23, bf16[2,512,512]{2,1,0:T(8,128)(2,1)S(1)} %bitcast.28, ...), custom_call_target="tpu_custom_call", output_to_operand_aliasing={{0}: (11, {}), {1}: (12, {})} | custom-call | flops 5242880 | bytes 3670016 | tf_op jit(solution)/shard_map/finish/pallas_call | solution.py:176
  (26 shorter events, 0.1 us)
Async XLA Ops:
  0.6 7.4 %copy-start.10 = (s32[16]{0:T(128)S(1)}, s32[16]{0:T(128)}, u32[]{:S(2)}) copy-start(s32[16]{0:T(128)} %param.19) | copy-start | bytes 196
  0.6 7.5 %copy-start.9 = (s32[16,6]{0,1:T(8,128)S(1)}, s32[16,6]{0,1:T(8,128)}, u32[]{:S(2)}) copy-start(s32[16,6]{0,1:T(8,128)} %param.18) | copy-start | bytes 1156
  0.7 7.6 %copy-start.8 = (f32[16,16]{1,0:T(8,128)S(1)}, f32[16,16]{1,0:T(8,128)}, u32[]{:S(2)}) copy-start(f32[16,16]{1,0:T(8,128)} %param.17) | copy-start | bytes 3076
  0.7 24.5 %all-to-all-start = ((bf16[16,64,512]{2,1,0:T(8,128)(2,1)}), bf16[16,64,512]{2,1,0:T(8,128)(2,1)S(1)}, u32[]{:S(2)}, u32[]{:S(2)}) async-start(bf16[16,64,512]{2,1,0:T(8,128)(2,1)} %bitcast.24), calls=%async_computation | async-start | bytes 2097152 | tf_op jit(solution)/shard_map/all_to_all | solution.py:263
  27.1 23.6 %all-to-all-start.1 = ((bf16[16,64,512]{2,1,0:T(8,128)(2,1)}), bf16[16,64,512]{2,1,0:T(8,128)(2,1)S(1)}, u32[]{:S(2)}, u32[]{:S(2)}) async-start(bf16[16,64,512]{2,1,0:T(8,128)(2,1)} %mix.1), calls=%async_computation.1 | async-start | bytes 2097152 | tf_op jit(solution)/shard_map/all_to_all | solution.py:274
  34.3 16.4 %copy-start.1 = (f32[512,512]{1,0:T(8,128)S(1)}, f32[512,512]{1,0:T(8,128)}, u32[]{:S(2)}) copy-start(f32[512,512]{1,0:T(8,128)} %ladder.2.part_a.part_ref) | copy-start | bytes 3145732
  34.3 49.0 %copy-start.6 = (f32[512]{0:T(512)S(1)}, f32[512]{0:T(512)}, u32[]{:S(2)}) copy-start(f32[512]{0:T(512)} %param.15) | copy-start | bytes 6148
  34.3 67.5 %copy-start.7 = (f32[16]{0:T(128)S(1)}, f32[16]{0:T(128)}, u32[]{:S(2)}) copy-start(f32[16]{0:T(128)} %occ_ref.3) | copy-start | bytes 196
  50.7 51.1 %copy-start = (bf16[2,1,512,512]{3,2,1,0:T(8,128)(2,1)S(1)}, bf16[2,1,512,512]{3,2,1,0:T(8,128)(2,1)}, u32[]{:S(2)}) copy-start(bf16[2,1,512,512]{3,2,1,0:T(8,128)(2,1)} %param.10) | copy-start | bytes 3145732
  50.8 1.3 %copy-start.2 = (f32[512,512]{1,0:T(8,128)S(1)}, f32[512,512]{1,0:T(8,128)}, u32[]{:S(2)}) copy-start(f32[512,512]{1,0:T(8,128)} %ladder.3.part_b.part_ref) | copy-start | bytes 3145732
  53.2 24.7 %collective-permute-start.1 = (bf16[512,512]{1,0:T(8,128)(2,1)}, bf16[512,512]{1,0:T(8,128)(2,1)}, u32[]{:S(2)}, u32[]{:S(2)}) collective-permute-start(bf16[512,512]{1,0:T(8,128)(2,1)} %get-tuple-element.35), channel_id=1, source_target_pairs={{4,32},{5,33},{6,48},{7,49},{20,34},{21,35},{22,50},{23,51},{8,72}... | collective-permute-start | bytes 1572872 | tf_op jit(solution)/shard_map/ppermute | solution.py:250
  59.1 18.1 %collective-permute-start.2 = (bf16[256,512]{1,0:T(8,128)(2,1)S(1)}, bf16[256,512]{1,0:T(8,128)(2,1)S(1)}, u32[]{:S(2)}, u32[]{:S(2)}) collective-permute-start(bf16[256,512]{1,0:T(8,128)(2,1)S(1)} %get-tuple-element.36), channel_id=1, source_target_pairs={{0,1},{1,0},{2,17},{3,16},{16,3},{17,2},{18,19},{19,18},{4,33},{5,... | collective-permute-start | bytes 786440 | tf_op jit(solution)/shard_map/ppermute | solution.py:250
  60.3 20.3 %collective-permute-start = (bf16[256,512]{1,0:T(8,128)(2,1)}, bf16[256,512]{1,0:T(8,128)(2,1)}, u32[]{:S(2)}, u32[]{:S(2)}) collective-permute-start(bf16[256,512]{1,0:T(8,128)(2,1)} %get-tuple-element.34), channel_id=1, source_target_pairs={{4,33},{5,32},{6,49},{7,48},{20,35},{21,34},{22,51},{23,50},{8,73}... | collective-permute-start | bytes 786440 | tf_op jit(solution)/shard_map/ppermute | solution.py:250
  77.2 0.7 copy-start.4
  77.9 24.0 %collective-permute-start.3 = (bf16[512,512]{1,0:T(8,128)(2,1)}, bf16[512,512]{1,0:T(8,128)(2,1)}, u32[]{:S(2)}, u32[]{:S(2)}) collective-permute-start(bf16[512,512]{1,0:T(8,128)(2,1)} %collective-permute-done.1.refs_0_), channel_id=1, source_target_pairs={{72,64},{73,65},{74,80},{75,81},{88,66},{89,67},{90,82},{91,83},{1... | collective-permute-start | bytes 1572872 | tf_op jit(solution)/shard_map/ppermute | solution.py:250
  79.2 22.7 %collective-permute-start.6 = (bf16[512,512]{1,0:T(8,128)(2,1)}, bf16[512,512]{1,0:T(8,128)(2,1)}, u32[]{:S(2)}, u32[]{:S(2)}) collective-permute-start(bf16[512,512]{1,0:T(8,128)(2,1)} %get-tuple-element.35), channel_id=1, source_target_pairs={{0,0},{1,1},{2,16},{3,17},{16,2},{17,3},{18,18},{19,19},{36,36},{3... | collective-permute-start | bytes 1572872 | tf_op jit(solution)/shard_map/ppermute | solution.py:250
  80.6 21.2 %collective-permute-start.4 = (bf16[256,512]{1,0:T(8,128)(2,1)}, bf16[256,512]{1,0:T(8,128)(2,1)}, u32[]{:S(2)}, u32[]{:S(2)}) collective-permute-start(bf16[256,512]{1,0:T(8,128)(2,1)} %collective-permute-done.refs_1_), channel_id=1, source_target_pairs={{72,64},{73,65},{74,80},{75,81},{88,66},{89,67},{90,82},{91,83},{1... | collective-permute-start | bytes 786440 | tf_op jit(solution)/shard_map/ppermute | solution.py:250
  81.9 23.0 %collective-permute-start.5 = (bf16[256,512]{1,0:T(8,128)(2,1)}, bf16[256,512]{1,0:T(8,128)(2,1)}, u32[]{:S(2)}, u32[]{:S(2)}) collective-permute-start(bf16[256,512]{1,0:T(8,128)(2,1)} %get-tuple-element.34), channel_id=1, source_target_pairs={{0,1},{1,0},{2,17},{3,16},{16,3},{17,2},{18,19},{19,18},{36,37},{3... | collective-permute-start | bytes 786440 | tf_op jit(solution)/shard_map/ppermute | solution.py:250
  101.9 3.1 %copy-start.3 = (f32[512,512]{1,0:T(8,128)S(1)}, f32[512,512]{1,0:T(8,128)}, u32[]{:S(2)}) copy-start(f32[512,512]{1,0:T(8,128)} %ladder.3.part_b.part_ref) | copy-start | bytes 3145732
  101.9 3.1 %copy-start.5 = (bf16[256,512]{1,0:T(8,128)(2,1)S(1)}, bf16[256,512]{1,0:T(8,128)(2,1)}, u32[]{:S(2)}) copy-start(bf16[256,512]{1,0:T(8,128)(2,1)} %copy-done.4) | copy-start | bytes 786436

commit v8 on v7

--- a/solution.py
+++ b/solution.py
@@ -281,7 +281,6 @@
     low_b = send(low_b, 1, diagonal="mirror", middle="mirror", other="mirror")
     same_a = send(send_a, 0, diagonal="mirror")
     same_b = send(high_b, 1, diagonal="mirror")
-    near_a, low_b = lax.optimization_barrier((near_a, low_b))
     near_b, low_b = lax.optimization_barrier((near_b, low_b))
     far_a = send(near_a, 0, middle="outward")
     far_b = send(near_b, 0, middle="outward")

time: 110 us -> 102 us (0.927)
  waiting for transfers between devices: 33.4 us -> 25.4 us
    ppermute x7, waiting for transfers between devices: 33.4 us -> 25.4 us  [send(): return lax.ppermute(array, AXES, pairs)]
  transfers between devices with their start and end apart: 9 -> 9, of which waited for: 2 -> 3; matrix products, arithmetic and copies ran while one was open for 1% -> 1% of each run, Pallas kernels for 33% -> 36%
where the time goes in v8:
time: 102 us; the launch traced here: 100 us
  Pallas kernels  41.8 us (41%)
  starting transfers between devices  29 us (28%)
  waiting for transfers between devices  25.4 us (25%)
  local copies, waits for them, and re-layouts  2.59 us (3%)
    pallas_call x2, Pallas kernels, ladder(): pl.pallas_call(ladder_kernel, out_shape=jax.ShapeDtypeStruct((virt, virt)...  32.7 us
    ppermute x7, waiting for transfers between devices, send(): return lax.ppermute(array, AXES, pairs)  25.4 us
    ppermute x7, starting transfers between devices, send(): return lax.ppermute(array, AXES, pairs)  14.4 us
    all_to_all x1, starting transfers between devices, shards(): slices = lax.all_to_all(slices, 'occj', 0, 0, tiled=True)  7.38 us
    all_to_all x1, starting transfers between devices, shards(): sums = lax.all_to_all(sums, 'occj', 0, 0, tiled=True)  7.22 us
    pallas_call x2, Pallas kernels, finish(): pl.pallas_call(functools.partial(finish_kernel, counts), out_shape=[jax.S...  6.01 us
  transfers between devices with their start and end apart: 9, of which 3 were waited for; matrix products, arithmetic and copies ran while one was open for 1% of the time, Pallas kernels for 36%

profile of v8, /device:TPU:36, one launch (start us, length us, event | category | flops | bytes accessed | tf_op | source)
XLA Modules:
  0.0 100.0 jit_solution(8397969167212831981)
XLA Ops:
  0.7 7.4 %all-to-all-start = ((bf16[16,64,512]{2,1,0:T(8,128)(2,1)}), bf16[16,64,512]{2,1,0:T(8,128)(2,1)S(1)}, u32[]{:S(2)}, u32[]{:S(2)}) async-start(bf16[16,64,512]{2,1,0:T(8,128)(2,1)} %bitcast.24), calls=%async_computation | async-start | bytes 2097152 | tf_op jit(solution)/shard_map/all_to_all | solution.py:263
  8.1 0.1 convert_reduce_fusion
  8.2 0.1 copy.24
  8.3 0.1 broadcast_in_dim.7
  8.4 0.1 reshape.78
  8.5 0.1 copy.25
  8.7 0.1 compare_select_fusion.w_ref
  8.8 0.1 add_add_fusion
  8.9 16.3 %ladder.2.part_a.part_ref = f32[512,512]{1,0:T(8,128)} custom-call(s32[1]{0:T(128)} %bitcast.1.slot, bf16[2,512,512]{2,1,0:T(8,128)(2,1)} %bitcast.25, bf16[2,512,512]{2,1,0:T(8,128)(2,1)} %bitcast.35, bf16[512,2048]{1,0:T(8,128)(2,1)} %x_ref.3, bf16[2048,2048]{1,0:T(8,128)(2,1)} %core_ref.3, bf16[512,512]{1,0:T(8,128)(2,1)} %fock_ref.3), custom_call_target="tpu_custom_call" | custom-call | flops 11005853696 | bytes 12582912 | tf_op jit(solution)/shard_map/ladder/pallas_call | solution.py:92
  25.1 2.0 %mix.1 = bf16[16,64,512]{2,1,0:T(8,128)(2,1)} custom-call(f32[256,256]{1,0:T(8,128)S(1)} %compare_select_fusion.w_ref, bf16[16,64,512]{2,1,0:T(8,128)(2,1)S(1)} %all-to-all-done.in_ref), custom_call_target="tpu_custom_call" | custom-call | flops 1000000000 | bytes 2097152 | tf_op jit(solution)/shard_map/mix/pallas_call | solution.py:50
  27.1 7.2 %all-to-all-start.1 = ((bf16[16,64,512]{2,1,0:T(8,128)(2,1)}), bf16[16,64,512]{2,1,0:T(8,128)(2,1)S(1)}, u32[]{:S(2)}, u32[]{:S(2)}) async-start(bf16[16,64,512]{2,1,0:T(8,128)(2,1)} %mix.1), calls=%async_computation.1 | async-start | bytes 2097152 | tf_op jit(solution)/shard_map/all_to_all | solution.py:274
  34.3 0.0 copy-start.6
  34.3 0.0 copy-start.7
  34.4 16.4 %ladder.3.part_b.part_ref = f32[512,512]{1,0:T(8,128)} custom-call(s32[1]{0:T(128)} %sub.16.slot, bf16[2,512,512]{2,1,0:T(8,128)(2,1)} %bitcast.26, bf16[2,512,512]{2,1,0:T(8,128)(2,1)} %bitcast.36, bf16[512,2048]{1,0:T(8,128)(2,1)} %x_ref.3, bf16[2048,2048]{1,0:T(8,128)(2,1)} %core_ref.3, bf16[512,512]{1,0:T(8,128)(2,1)} %fock_ref.3), custom_call_target="tpu_custom_call" | custom-call | flops 11005853696 | bytes 12582912 | tf_op jit(solution)/shard_map/ladder/pallas_call | solution.py:92
  50.7 0.0 all-to-all-done.1
  50.8 1.3 %copy-done.2 = f32[512,512]{1,0:T(8,128)S(1)} copy-done((f32[512,512]{1,0:T(8,128)S(1)}, f32[512,512]{1,0:T(8,128)}, u32[]{:S(2)}) %copy-start.2) | copy-done | bytes 1048600
  52.1 1.2 %half.1 = (bf16[512,512]{1,0:T(8,128)(2,1)}, bf16[256,512]{1,0:T(8,128)(2,1)S(1)}, bf16[256,512]{1,0:T(8,128)(2,1)}) custom-call(s32[1]{0:T(128)} %bitcast.1.slot, f32[512,512]{1,0:T(8,128)S(1)} %copy-done.1, f32[512,512]{1,0:T(8,128)S(1)} %copy-done.2, bf16[2,512,512]{2,1,0:T(8,128)(2,1)S(1)} %bitcast.21), custom_call_target="tpu_custom_call" | custom-call | bytes 4194304 | tf_op jit(solution)/shard_map/half/pallas_call | solution.py:136
  53.2 5.9 %collective-permute-start.2 = (bf16[512,512]{1,0:T(8,128)(2,1)}, bf16[512,512]{1,0:T(8,128)(2,1)}, u32[]{:S(2)}, u32[]{:S(2)}) collective-permute-start(bf16[512,512]{1,0:T(8,128)(2,1)} %get-tuple-element.36), channel_id=1, source_target_pairs={{4,32},{5,33},{6,48},{7,49},{20,34},{21,35},{22,50},{23,51},{8,72}... | collective-permute-start | bytes 1572872 | tf_op jit(solution)/shard_map/ppermute | solution.py:250
  59.1 1.2 %collective-permute-start.1 = (bf16[256,512]{1,0:T(8,128)(2,1)S(1)}, bf16[256,512]{1,0:T(8,128)(2,1)S(1)}, u32[]{:S(2)}, u32[]{:S(2)}) collective-permute-start(bf16[256,512]{1,0:T(8,128)(2,1)S(1)} %get-tuple-element.33), channel_id=1, source_target_pairs={{0,1},{1,0},{2,17},{3,16},{16,3},{17,2},{18,19},{19,18},{4,33},{5,... | collective-permute-start | bytes 786440 | tf_op jit(solution)/shard_map/ppermute | solution.py:250
  60.3 2.0 %collective-permute-start = (bf16[256,512]{1,0:T(8,128)(2,1)}, bf16[256,512]{1,0:T(8,128)(2,1)}, u32[]{:S(2)}, u32[]{:S(2)}) collective-permute-start(bf16[256,512]{1,0:T(8,128)(2,1)} %get-tuple-element.32), channel_id=1, source_target_pairs={{4,33},{5,32},{6,49},{7,48},{20,35},{21,34},{22,51},{23,50},{8,73}... | collective-permute-start | bytes 786440 | tf_op jit(solution)/shard_map/ppermute | solution.py:250
  62.3 8.6 %collective-permute-done.2.refs_0_ = bf16[512,512]{1,0:T(8,128)(2,1)} collective-permute-done((bf16[512,512]{1,0:T(8,128)(2,1)}, bf16[512,512]{1,0:T(8,128)(2,1)}, u32[]{:S(2)}, u32[]{:S(2)}) %collective-permute-start.2) | collective-permute-done | bytes 524320 | tf_op jit(solution)/shard_map/ppermute | solution.py:250
  70.9 1.3 %collective-permute-start.3 = (bf16[512,512]{1,0:T(8,128)(2,1)}, bf16[512,512]{1,0:T(8,128)(2,1)}, u32[]{:S(2)}, u32[]{:S(2)}) collective-permute-start(bf16[512,512]{1,0:T(8,128)(2,1)} %collective-permute-done.2.refs_0_), channel_id=1, source_target_pairs={{72,64},{73,65},{74,80},{75,81},{88,66},{89,67},{90,82},{91,83},{1... | collective-permute-start | bytes 1572872 | tf_op jit(solution)/shard_map/ppermute | solution.py:250
  72.2 1.5 %collective-permute-start.6 = (bf16[512,512]{1,0:T(8,128)(2,1)}, bf16[512,512]{1,0:T(8,128)(2,1)}, u32[]{:S(2)}, u32[]{:S(2)}) collective-permute-start(bf16[512,512]{1,0:T(8,128)(2,1)} %get-tuple-element.36), channel_id=1, source_target_pairs={{0,0},{1,1},{2,16},{3,17},{16,2},{17,3},{18,18},{19,19},{36,36},{3... | collective-permute-start | bytes 1572872 | tf_op jit(solution)/shard_map/ppermute | solution.py:250
  73.7 3.5 %collective-permute-done.1.refs_0_ = bf16[256,512]{1,0:T(8,128)(2,1)S(1)} collective-permute-done((bf16[256,512]{1,0:T(8,128)(2,1)S(1)}, bf16[256,512]{1,0:T(8,128)(2,1)S(1)}, u32[]{:S(2)}, u32[]{:S(2)}) %collective-permute-start.1) | collective-permute-done | bytes 262176 | tf_op jit(solution)/shard_map/ppermute | solution.py:250
  77.2 0.7 copy-done.4
  77.9 0.0 collective-permute-done.refs_1_
  77.9 1.3 %collective-permute-start.4 = (bf16[256,512]{1,0:T(8,128)(2,1)}, bf16[256,512]{1,0:T(8,128)(2,1)}, u32[]{:S(2)}, u32[]{:S(2)}) collective-permute-start(bf16[256,512]{1,0:T(8,128)(2,1)} %collective-permute-done.refs_1_), channel_id=1, source_target_pairs={{72,64},{73,65},{74,80},{75,81},{88,66},{89,67},{90,82},{91,83},{1... | collective-permute-start | bytes 786440 | tf_op jit(solution)/shard_map/ppermute | solution.py:250
  79.2 1.4 %collective-permute-start.5 = (bf16[256,512]{1,0:T(8,128)(2,1)}, bf16[256,512]{1,0:T(8,128)(2,1)}, u32[]{:S(2)}, u32[]{:S(2)}) collective-permute-start(bf16[256,512]{1,0:T(8,128)(2,1)} %get-tuple-element.32), channel_id=1, source_target_pairs={{0,1},{1,0},{2,17},{3,16},{16,3},{17,2},{18,19},{19,18},{36,37},{3... | collective-permute-start | bytes 786440 | tf_op jit(solution)/shard_map/ppermute | solution.py:250
  80.5 0.1 copy.27.col_ref
  80.7 13.2 %collective-permute-done.4.refs_2_ = bf16[256,512]{1,0:T(8,128)(2,1)} collective-permute-done((bf16[256,512]{1,0:T(8,128)(2,1)}, bf16[256,512]{1,0:T(8,128)(2,1)}, u32[]{:S(2)}, u32[]{:S(2)}) %collective-permute-start.4) | collective-permute-done | bytes 262176 | tf_op jit(solution)/shard_map/ppermute | solution.py:250
  94.0 3.0 %finish.2 = (f32[2,512,512]{2,1,0:T(8,128)}, bf16[2,512,512]{2,1,0:T(8,128)(2,1)}) custom-call(s32[4]{0:T(128)S(1)} %get-tuple-element.38.ids, f32[512,512]{1,0:T(8,128)S(1)} %copy-done.1, bf16[2,512,512]{2,1,0:T(8,128)(2,1)S(1)} %bitcast.22, bf16[2,512,512]{2,1,0:T(8,128)(2,1)S(1)} %bitcast.27, f32[512,1]{1,0:T(8,128)S(1)} %copy.27.col_ref, ...), custom_call_target="tpu_custom_call" | custom-call | flops 5242880 | bytes 3670016 | tf_op jit(solution)/shard_map/finish/pallas_call | solution.py:176
  97.0 3.0 %finish.3 = (f32[2,512,512]{2,1,0:T(8,128)}, bf16[2,512,512]{2,1,0:T(8,128)(2,1)}) custom-call(s32[4]{0:T(128)S(1)} %get-tuple-element.23.ids, f32[512,512]{1,0:T(8,128)S(1)} %copy-done.3, bf16[2,512,512]{2,1,0:T(8,128)(2,1)S(1)} %bitcast.23, bf16[2,512,512]{2,1,0:T(8,128)(2,1)S(1)} %bitcast.28, ...), custom_call_target="tpu_custom_call", output_to_operand_aliasing={{0}: (11, {}), {1}: (12, {})} | custom-call | flops 5242880 | bytes 3670016 | tf_op jit(solution)/shard_map/finish/pallas_call | solution.py:176
  (26 shorter events, 0.1 us)
Async XLA Ops:
  0.6 7.4 %copy-start.10 = (s32[16]{0:T(128)S(1)}, s32[16]{0:T(128)}, u32[]{:S(2)}) copy-start(s32[16]{0:T(128)} %param.19) | copy-start | bytes 196
  0.6 7.5 %copy-start.9 = (s32[16,6]{0,1:T(8,128)S(1)}, s32[16,6]{0,1:T(8,128)}, u32[]{:S(2)}) copy-start(s32[16,6]{0,1:T(8,128)} %param.18) | copy-start | bytes 1156
  0.7 7.6 %copy-start.8 = (f32[16,16]{1,0:T(8,128)S(1)}, f32[16,16]{1,0:T(8,128)}, u32[]{:S(2)}) copy-start(f32[16,16]{1,0:T(8,128)} %param.17) | copy-start | bytes 3076
  0.7 24.5 %all-to-all-start = ((bf16[16,64,512]{2,1,0:T(8,128)(2,1)}), bf16[16,64,512]{2,1,0:T(8,128)(2,1)S(1)}, u32[]{:S(2)}, u32[]{:S(2)}) async-start(bf16[16,64,512]{2,1,0:T(8,128)(2,1)} %bitcast.24), calls=%async_computation | async-start | bytes 2097152 | tf_op jit(solution)/shard_map/all_to_all | solution.py:263
  27.1 23.6 %all-to-all-start.1 = ((bf16[16,64,512]{2,1,0:T(8,128)(2,1)}), bf16[16,64,512]{2,1,0:T(8,128)(2,1)S(1)}, u32[]{:S(2)}, u32[]{:S(2)}) async-start(bf16[16,64,512]{2,1,0:T(8,128)(2,1)} %mix.1), calls=%async_computation.1 | async-start | bytes 2097152 | tf_op jit(solution)/shard_map/all_to_all | solution.py:274
  34.3 16.4 %copy-start.1 = (f32[512,512]{1,0:T(8,128)S(1)}, f32[512,512]{1,0:T(8,128)}, u32[]{:S(2)}) copy-start(f32[512,512]{1,0:T(8,128)} %ladder.2.part_a.part_ref) | copy-start | bytes 3145732
  34.3 46.2 %copy-start.6 = (f32[512]{0:T(512)S(1)}, f32[512]{0:T(512)}, u32[]{:S(2)}) copy-start(f32[512]{0:T(512)} %param.15) | copy-start | bytes 6148
  34.3 59.6 %copy-start.7 = (f32[16]{0:T(128)S(1)}, f32[16]{0:T(128)}, u32[]{:S(2)}) copy-start(f32[16]{0:T(128)} %occ_ref.3) | copy-start | bytes 196
  50.7 43.2 %copy-start = (bf16[2,1,512,512]{3,2,1,0:T(8,128)(2,1)S(1)}, bf16[2,1,512,512]{3,2,1,0:T(8,128)(2,1)}, u32[]{:S(2)}) copy-start(bf16[2,1,512,512]{3,2,1,0:T(8,128)(2,1)} %param.10) | copy-start | bytes 3145732
  50.8 1.3 %copy-start.2 = (f32[512,512]{1,0:T(8,128)S(1)}, f32[512,512]{1,0:T(8,128)}, u32[]{:S(2)}) copy-start(f32[512,512]{1,0:T(8,128)} %ladder.3.part_b.part_ref) | copy-start | bytes 3145732
  53.2 17.7 %collective-permute-start.2 = (bf16[512,512]{1,0:T(8,128)(2,1)}, bf16[512,512]{1,0:T(8,128)(2,1)}, u32[]{:S(2)}, u32[]{:S(2)}) collective-permute-start(bf16[512,512]{1,0:T(8,128)(2,1)} %get-tuple-element.36), channel_id=1, source_target_pairs={{4,32},{5,33},{6,48},{7,49},{20,34},{21,35},{22,50},{23,51},{8,72}... | collective-permute-start | bytes 1572872 | tf_op jit(solution)/shard_map/ppermute | solution.py:250
  59.1 18.1 %collective-permute-start.1 = (bf16[256,512]{1,0:T(8,128)(2,1)S(1)}, bf16[256,512]{1,0:T(8,128)(2,1)S(1)}, u32[]{:S(2)}, u32[]{:S(2)}) collective-permute-start(bf16[256,512]{1,0:T(8,128)(2,1)S(1)} %get-tuple-element.33), channel_id=1, source_target_pairs={{0,1},{1,0},{2,17},{3,16},{16,3},{17,2},{18,19},{19,18},{4,33},{5,... | collective-permute-start | bytes 786440 | tf_op jit(solution)/shard_map/ppermute | solution.py:250
  60.3 17.6 %collective-permute-start = (bf16[256,512]{1,0:T(8,128)(2,1)}, bf16[256,512]{1,0:T(8,128)(2,1)}, u32[]{:S(2)}, u32[]{:S(2)}) collective-permute-start(bf16[256,512]{1,0:T(8,128)(2,1)} %get-tuple-element.32), channel_id=1, source_target_pairs={{4,33},{5,32},{6,49},{7,48},{20,35},{21,34},{22,51},{23,50},{8,73}... | collective-permute-start | bytes 786440 | tf_op jit(solution)/shard_map/ppermute | solution.py:250
  70.9 23.0 %collective-permute-start.3 = (bf16[512,512]{1,0:T(8,128)(2,1)}, bf16[512,512]{1,0:T(8,128)(2,1)}, u32[]{:S(2)}, u32[]{:S(2)}) collective-permute-start(bf16[512,512]{1,0:T(8,128)(2,1)} %collective-permute-done.2.refs_0_), channel_id=1, source_target_pairs={{72,64},{73,65},{74,80},{75,81},{88,66},{89,67},{90,82},{91,83},{1... | collective-permute-start | bytes 1572872 | tf_op jit(solution)/shard_map/ppermute | solution.py:250
  72.2 21.7 %collective-permute-start.6 = (bf16[512,512]{1,0:T(8,128)(2,1)}, bf16[512,512]{1,0:T(8,128)(2,1)}, u32[]{:S(2)}, u32[]{:S(2)}) collective-permute-start(bf16[512,512]{1,0:T(8,128)(2,1)} %get-tuple-element.36), channel_id=1, source_target_pairs={{0,0},{1,1},{2,16},{3,17},{16,2},{17,3},{18,18},{19,19},{36,36},{3... | collective-permute-start | bytes 1572872 | tf_op jit(solution)/shard_map/ppermute | solution.py:250
  77.2 0.7 copy-start.4
  77.9 16.0 %collective-permute-start.4 = (bf16[256,512]{1,0:T(8,128)(2,1)}, bf16[256,512]{1,0:T(8,128)(2,1)}, u32[]{:S(2)}, u32[]{:S(2)}) collective-permute-start(bf16[256,512]{1,0:T(8,128)(2,1)} %collective-permute-done.refs_1_), channel_id=1, source_target_pairs={{72,64},{73,65},{74,80},{75,81},{88,66},{89,67},{90,82},{91,83},{1... | collective-permute-start | bytes 786440 | tf_op jit(solution)/shard_map/ppermute | solution.py:250
  79.2 17.8 %collective-permute-start.5 = (bf16[256,512]{1,0:T(8,128)(2,1)}, bf16[256,512]{1,0:T(8,128)(2,1)}, u32[]{:S(2)}, u32[]{:S(2)}) collective-permute-start(bf16[256,512]{1,0:T(8,128)(2,1)} %get-tuple-element.32), channel_id=1, source_target_pairs={{0,1},{1,0},{2,17},{3,16},{16,3},{17,2},{18,19},{19,18},{36,37},{3... | collective-permute-start | bytes 786440 | tf_op jit(solution)/shard_map/ppermute | solution.py:250
  94.0 3.1 %copy-start.3 = (f32[512,512]{1,0:T(8,128)S(1)}, f32[512,512]{1,0:T(8,128)}, u32[]{:S(2)}) copy-start(f32[512,512]{1,0:T(8,128)} %ladder.3.part_b.part_ref) | copy-start | bytes 3145732
  94.0 3.1 %copy-start.5 = (bf16[256,512]{1,0:T(8,128)(2,1)S(1)}, bf16[256,512]{1,0:T(8,128)(2,1)}, u32[]{:S(2)}) copy-start(bf16[256,512]{1,0:T(8,128)(2,1)} %copy-done.4) | copy-start | bytes 786436

commit v9 on v8

--- a/solution.py
+++ b/solution.py
@@ -115,10 +115,11 @@
     )(slot, amps, ints, x, core, fock)
 
 
-def half_kernel(slot, part_a, part_b, sum_ref, send_a, low_b, high_b):
+def half_kernel(slot, part_a, part_b, sum_ref, send_a, send_b, low_b, high_b):
     core = slot[0]
     send_a[...] = (part_a[...] - sum_ref[core].astype(F32)).astype(BF16)
     rounded = (part_b[...] - sum_ref[1 - core].astype(F32)).astype(BF16)
+    send_b[...] = rounded
 
     @pl.when(pl.program_id(0) == 0)
     def _():
@@ -135,12 +136,12 @@
     strip = pl.BlockSpec((rows, virt), lambda r, s: (r, 0))
     return pl.pallas_call(
         half_kernel,
-        out_shape=[jax.ShapeDtypeStruct((n, virt), BF16) for n in (virt, rows, rows)],
+        out_shape=[jax.ShapeDtypeStruct((n, virt), BF16) for n in (virt, virt, rows, rows)],
         grid_spec=pltpu.PrefetchScalarGridSpec(
             num_scalar_prefetch=1,
             grid=(2,),
             in_specs=[strip, strip, pl.BlockSpec((2, rows, virt), lambda r, s: (0, r, 0))],
-            out_specs=[strip, whole((rows, virt)), whole((rows, virt))],
+            out_specs=[strip, strip, whole((rows, virt)), whole((rows, virt))],
         ),
         compiler_params=params(16),
         cost_estimate=pl.CostEstimate(
@@ -150,57 +151,74 @@
     )(slot, part_a, part_b, sums)
 
 
-def finish_kernel(counts, ids, part_ref, sum_ref, amp_ref, col_ref, row_ref, occ_ref, *refs):
-    res_ref, new_ref = refs[-2:]
-    pieces = []
-    for n in counts:
-        piece = refs[0][...]
-        for kind in range(1, n):
-            piece = jnp.where(ids[3] == kind, refs[kind][...], piece)
-        pieces.append(piece)
-        refs = refs[n:]
-    mirror = jnp.concatenate(pieces, axis=0)
-    half = part_ref[...] - sum_ref[...].astype(F32)
-    residual = half + mirror.astype(F32).T
-    denominator = col_ref[...] + row_ref[...] - occ_ref[ids[1]] - occ_ref[ids[2]]
-    res_ref[...] = residual
-    new_ref[...] = (amp_ref[...].astype(F32) - residual / denominator).astype(BF16)
-
-
-def finish(ids, part, sums, mirrors, amps, eps_col, eps_row, eps_occ, held):
-    virt = part.shape[0]
-    rows = min(256, virt)
-    strip = pl.BlockSpec((None, rows, virt), lambda r, s: (s[0], r, 0))
-    counts = [len(piece) for piece in mirrors]
-    mirrors = sum(mirrors, ())
+def finish_kernel(ids, part_a, part_b, sum_ref, amp_ref, col_ref, row_ref, occ_ref, *refs):
+    near_a, far_a, same_a, low_b, near_b, far_b, same_b, res_ref, new_ref = refs
+    step = pl.program_id(0)
+    middle, diagonal = ids[5] == 1, ids[5] == 2
+
+    def finish(part_ref, first, mirror):
+        half = part_ref[...] - sum_ref[...].astype(F32)
+        residual = half + mirror.astype(F32).T
+        denominator = col_ref[...] + row_ref[...] - occ_ref[first] - occ_ref[ids[4]]
+        res_ref[...] = residual
+        new_ref[...] = (amp_ref[...].astype(F32) - residual / denominator).astype(BF16)
+
+    @pl.when(step < 2)
+    def _():
+        mirror = jnp.where(middle, far_a[...], near_a[...])
+        finish(part_a, ids[1], jnp.where(diagonal, same_a[...], mirror))
+
+    @pl.when(step >= 2)
+    def _():
+        high = jnp.where(middle, far_b[...], near_b[...])
+        mirror = jnp.concatenate([low_b[...], high], axis=0)
+        finish(part_b, ids[3], jnp.where(diagonal, same_b[...], mirror))
+
+
+def finish(ids, part_a, part_b, sums, amps, eps_col, eps_row, eps_occ, mirror_a, mirror_b):
+    virt = part_a.shape[0]
+    rows = virt // 2
+    strip = pl.BlockSpec(
+        (None, rows, virt), lambda g, s: (jnp.where(g < 2, s[0], s[2]), g % 2, 0)
+    )
+
+    def early(g, s):
+        return jnp.minimum(g, 1)
+
+    def late(g, s):
+        return jnp.maximum(g - 2, 0)
+
+    def across(m, at):
+        return pl.BlockSpec((m.shape[0], rows), lambda g, s: (0, at(g, s)))
+
     return pl.pallas_call(
-        functools.partial(finish_kernel, counts),
+        finish_kernel,
         out_shape=[
             jax.ShapeDtypeStruct(amps.shape, F32),
             jax.ShapeDtypeStruct(amps.shape, BF16),
         ],
         grid_spec=pltpu.PrefetchScalarGridSpec(
             num_scalar_prefetch=1,
-            grid=(virt // rows,),
+            grid=(4,),
             in_specs=[
-                pl.BlockSpec((rows, virt), lambda r, s: (r, 0)),
+                pl.BlockSpec((rows, virt), lambda g, s: (early(g, s), 0)),
+                pl.BlockSpec((rows, virt), lambda g, s: (late(g, s), 0)),
                 strip,
                 strip,
-                pl.BlockSpec((rows, 1), lambda r, s: (r, 0)),
+                pl.BlockSpec((rows, 1), lambda g, s: (g % 2, 0)),
                 whole((1, virt)),
                 pl.BlockSpec(memory_space=pltpu.SMEM),
             ]
-            + [pl.BlockSpec((m.shape[0], rows), lambda r, s: (0, r)) for m in mirrors]
-            + [pl.BlockSpec(memory_space=pl.ANY)] * len(held),
+            + [across(m, early) for m in mirror_a]
+            + [across(m, late) for m in mirror_b],
             out_specs=[strip, strip],
         ),
-        input_output_aliases={7 + sum(counts) + m: m for m in range(len(held))},
-        compiler_params=params(16, dimension_semantics=("arbitrary",)),
+        compiler_params=params(24, dimension_semantics=("arbitrary",)),
         cost_estimate=pl.CostEstimate(
-            flops=20 * part.size, bytes_accessed=14 * part.size, transcendentals=0
+            flops=40 * part_a.size, bytes_accessed=28 * part_a.size, transcendentals=0
         ),
         name="finish",
-    )(ids, part, sums, amps, eps_col, eps_row, eps_occ, *mirrors, *held)
+    )(ids, part_a, part_b, sums, amps, eps_col, eps_row, eps_occ, *mirror_a, *mirror_b)
 
 
 def shards(
@@ -254,10 +272,8 @@
     eps_col = eps_vir.reshape(virt, 1)
     eps_row = eps_vir.reshape(1, virt)
 
-    def ids_of(slot):
-        return jnp.stack([slot[0], me_i * rows_i + slot[0], me_j, kind]).astype(jnp.int32)
-
-    ids_a, ids_b = ids_of(slot_a), ids_of(slot_b)
+    pair_ids = [slot_a[0], me_i * rows_i + slot_a[0], slot_b[0], me_i * rows_i + slot_b[0]]
+    ids = jnp.stack([*pair_ids, me_j, kind]).astype(jnp.int32)
 
     slices = amps.reshape(n_second, rows_i * virt // n_second, virt)
     slices = lax.all_to_all(slices, "occj", 0, 0, tiled=True)
@@ -266,31 +282,26 @@
     lane = jnp.arange(n_second * SUB, dtype=jnp.int32) % SUB
     wide = jnp.where(lane[:, None] == lane[None, :], tall, 0.0)
     part_a = ladder(slot_a, amps, ints, thc_factor, thc_core, fock_vir)
-    slices, part_a, ids_a, ids_b, eps_col = lax.optimization_barrier(
-        (slices, part_a, ids_a, ids_b, eps_col)
-    )
+    slices, part_a, ids, eps_col = lax.optimization_barrier((slices, part_a, ids, eps_col))
     sums = mix(wide, slices)
     sums, part_a, slot_b = lax.optimization_barrier((sums, part_a, slot_b))
     sums = lax.all_to_all(sums, "occj", 0, 0, tiled=True)
     part_b = ladder(slot_b, amps, ints, thc_factor, thc_core, fock_vir)
     sums, part_b = lax.optimization_barrier((sums, part_b))
     sums = sums.reshape(rows_i, virt, virt)
-    send_a, low_b, high_b = half_of(slot_a, part_a, part_b, sums)
+    send_a, send_b, low_b, high_b = half_of(slot_a, part_a, part_b, sums)
     near_a = send(send_a, 0, middle="inward", other="mirror")
     near_b = send(high_b, 1, middle="inward", other="mirror")
-    low_b = send(low_b, 1, diagonal="mirror", middle="mirror", other="mirror")
+    low_b = send(low_b, 1, middle="mirror", other="mirror")
     same_a = send(send_a, 0, diagonal="mirror")
-    same_b = send(high_b, 1, diagonal="mirror")
+    same_b = send(send_b, 1, diagonal="mirror")
     near_b, low_b = lax.optimization_barrier((near_b, low_b))
     far_a = send(near_a, 0, middle="outward")
     far_b = send(near_b, 0, middle="outward")
-
-    far_a, far_b = lax.optimization_barrier((far_a, far_b))
-    tables = (amps, eps_col, eps_row, eps_occ)
-    mirror_a = [(near_a, far_a, same_a)]
-    mirror_b = [(low_b,), (near_b, far_b, same_b)]
-    held = finish(ids_a, part_a, sums, mirror_a, *tables, ())
-    residual, updated = finish(ids_b, part_b, sums, mirror_b, *tables, held)
+    mirror_a, mirror_b = (near_a, far_a, same_a), (low_b, near_b, far_b, same_b)
+    residual, updated = finish(
+        ids, part_a, part_b, sums, amps, eps_col, eps_row, eps_occ, mirror_a, mirror_b
+    )
     return (
         residual.reshape(rows_i, 1, virt, virt),
         updated.reshape(rows_i, 1, virt, virt),

time: 102 us -> 104 us (1.020); the launches traced: 100 us -> 104 us
  local copies, waits for them, and re-layouts: 2.59 us -> 4.85 us
  starting transfers between devices: 29 us -> 31 us
    unnamed x22, local copies, waits for them, and re-layouts: 2.03 us -> 4.2 us
    ppermute x7, starting transfers between devices: 14.4 us -> 16.4 us  [send(): return lax.ppermute(array, AXES, pairs)]
    pallas_call x2 -> x1, Pallas kernels: 6.01 us -> 5.33 us  [finish(): pl.pallas_call(finish_kernel, out_shape=[jax.ShapeDtypeStruct(amps.shape,...]
  transfers between devices with their start and end apart: 9 -> 9, of which waited for: 3 -> 4; matrix products, arithmetic and copies ran while one was open for 1% -> 1% of each run, Pallas kernels for 36% -> 31%
where the time goes in v9:
time: 104 us
  Pallas kernels  41.1 us (40%)
  starting transfers between devices  31 us (30%)
  waiting for transfers between devices  25.5 us (25%)
  local copies, waits for them, and re-layouts  4.85 us (5%)
    pallas_call x2, Pallas kernels, ladder(): pl.pallas_call(ladder_kernel, out_shape=jax.ShapeDtypeStruct((virt, virt)...  32.6 us
    ppermute x7, waiting for transfers between devices, send(): return lax.ppermute(array, AXES, pairs)  25.5 us
    ppermute x7, starting transfers between devices, send(): return lax.ppermute(array, AXES, pairs)  16.4 us
    all_to_all x1, starting transfers between devices, shards(): slices = lax.all_to_all(slices, 'occj', 0, 0, tiled=True)  7.38 us
    all_to_all x1, starting transfers between devices, shards(): sums = lax.all_to_all(sums, 'occj', 0, 0, tiled=True)  7.23 us
    pallas_call x1, Pallas kernels, finish(): pl.pallas_call(finish_kernel, out_shape=[jax.ShapeDtypeStruct(amps.shape,...  5.33 us
    unnamed x22, local copies, waits for them, and re-layouts  4.2 us
  transfers between devices with their start and end apart: 9, of which 4 were waited for; matrix products, arithmetic and copies ran while one was open for 1% of the time, Pallas kernels for 31%

profile of v9, /device:TPU:36, one launch (start us, length us, event | category | flops | bytes accessed | tf_op | source)
XLA Modules:
  0.0 103.6 jit_solution(7978442493381106518)
XLA Ops:
  0.7 7.4 %all-to-all-start = ((bf16[16,64,512]{2,1,0:T(8,128)(2,1)}), bf16[16,64,512]{2,1,0:T(8,128)(2,1)S(1)}, u32[]{:S(2)}, u32[]{:S(2)}) async-start(bf16[16,64,512]{2,1,0:T(8,128)(2,1)} %bitcast.23), calls=%async_computation | async-start | bytes 2097152 | tf_op jit(solution)/shard_map/all_to_all | solution.py:279
  8.1 0.1 convert_reduce_fusion
  8.2 0.1 copy.21
  8.3 0.1 broadcast_in_dim.7
  8.4 0.1 reshape.78
  8.5 0.1 copy.22
  8.7 0.1 compare_select_fusion.w_ref
  8.8 0.1 stack.19.ids
  8.9 16.3 %ladder.2.part_a = f32[512,512]{1,0:T(8,128)} custom-call(s32[1]{0:T(128)} %bitcast.1.slot, bf16[2,512,512]{2,1,0:T(8,128)(2,1)} %bitcast.24, bf16[2,512,512]{2,1,0:T(8,128)(2,1)} %bitcast.31, bf16[512,2048]{1,0:T(8,128)(2,1)} %x_ref.3, bf16[2048,2048]{1,0:T(8,128)(2,1)} %core_ref.3, bf16[512,512]{1,0:T(8,128)(2,1)} %fock_ref.3), custom_call_target="tpu_custom_call" | custom-call | flops 11005853696 | bytes 12582912 | tf_op jit(solution)/shard_map/ladder/pallas_call | solution.py:92
  25.1 2.0 %mix.1 = bf16[16,64,512]{2,1,0:T(8,128)(2,1)} custom-call(f32[256,256]{1,0:T(8,128)S(1)} %compare_select_fusion.w_ref, bf16[16,64,512]{2,1,0:T(8,128)(2,1)S(1)} %all-to-all-done.in_ref), custom_call_target="tpu_custom_call" | custom-call | flops 1000000000 | bytes 2097152 | tf_op jit(solution)/shard_map/mix/pallas_call | solution.py:50
  27.1 7.2 %all-to-all-start.1 = ((bf16[16,64,512]{2,1,0:T(8,128)(2,1)}), bf16[16,64,512]{2,1,0:T(8,128)(2,1)S(1)}, u32[]{:S(2)}, u32[]{:S(2)}) async-start(bf16[16,64,512]{2,1,0:T(8,128)(2,1)} %mix.1), calls=%async_computation.1 | async-start | bytes 2097152 | tf_op jit(solution)/shard_map/all_to_all | solution.py:288
  34.4 0.0 copy-start.6
  34.4 0.0 copy-start.7
  34.4 16.4 %ladder.3.part_b = f32[512,512]{1,0:T(8,128)} custom-call(s32[1]{0:T(128)} %sub.13.slot, bf16[2,512,512]{2,1,0:T(8,128)(2,1)} %bitcast.25, bf16[2,512,512]{2,1,0:T(8,128)(2,1)} %bitcast.32, bf16[512,2048]{1,0:T(8,128)(2,1)} %x_ref.3, bf16[2048,2048]{1,0:T(8,128)(2,1)} %core_ref.3, bf16[512,512]{1,0:T(8,128)(2,1)} %fock_ref.3), custom_call_target="tpu_custom_call" | custom-call | flops 11005853696 | bytes 12582912 | tf_op jit(solution)/shard_map/ladder/pallas_call | solution.py:92
  50.8 1.3 %copy-done.2 = f32[512,512]{1,0:T(8,128)S(1)} copy-done((f32[512,512]{1,0:T(8,128)S(1)}, f32[512,512]{1,0:T(8,128)}, u32[]{:S(2)}) %copy-start.2) | copy-done | bytes 1048600
  52.1 1.1 %half.1 = (bf16[512,512]{1,0:T(8,128)(2,1)}, bf16[512,512]{1,0:T(8,128)(2,1)}, bf16[256,512]{1,0:T(8,128)(2,1)S(1)}, bf16[256,512]{1,0:T(8,128)(2,1)S(1)}) custom-call(s32[1]{0:T(128)} %bitcast.1.slot, f32[512,512]{1,0:T(8,128)S(1)} %copy-done.1, f32[512,512]{1,0:T(8,128)S(1)} %copy-done.2, bf16[2,512,512]{2,1,0:T(8,128)(2,1)S(1)} %bitcast.21), custom_call_target="tpu_custom_call" | custom-call | bytes 4194304 | tf_op jit(solution)/shard_map/half/pallas_call | solution.py:137
  53.2 5.9 %collective-permute-start = (bf16[512,512]{1,0:T(8,128)(2,1)}, bf16[512,512]{1,0:T(8,128)(2,1)}, u32[]{:S(2)}, u32[]{:S(2)}) collective-permute-start(bf16[512,512]{1,0:T(8,128)(2,1)} %get-tuple-element.28), channel_id=1, source_target_pairs={{4,32},{5,33},{6,48},{7,49},{20,34},{21,35},{22,50},{23,51},{8,72}... | collective-permute-start | bytes 1572872 | tf_op jit(solution)/shard_map/ppermute | solution.py:268
  59.1 2.0 %collective-permute-start.3 = (bf16[256,512]{1,0:T(8,128)(2,1)S(1)}, bf16[256,512]{1,0:T(8,128)(2,1)}, u32[]{:S(2)}, u32[]{:S(2)}) collective-permute-start(bf16[256,512]{1,0:T(8,128)(2,1)S(1)} %get-tuple-element.29), channel_id=1, source_target_pairs={{4,33},{5,32},{6,49},{7,48},{20,35},{21,34},{22,51},{23,50},{8,73}... | collective-permute-start | bytes 786440 | tf_op jit(solution)/shard_map/ppermute | solution.py:268
  61.1 3.0 %collective-permute-start.4 = (bf16[256,512]{1,0:T(8,128)(2,1)S(1)}, bf16[256,512]{1,0:T(8,128)(2,1)S(1)}, u32[]{:S(2)}, u32[]{:S(2)}) collective-permute-start(bf16[256,512]{1,0:T(8,128)(2,1)S(1)} %get-tuple-element.30), channel_id=1, source_target_pairs={{4,33},{5,32},{6,49},{7,48},{20,35},{21,34},{22,51},{23,50},{8,65}... | collective-permute-start | bytes 786440 | tf_op jit(solution)/shard_map/ppermute | solution.py:268
  64.2 1.5 %collective-permute-start.2 = (bf16[512,512]{1,0:T(8,128)(2,1)}, bf16[512,512]{1,0:T(8,128)(2,1)}, u32[]{:S(2)}, u32[]{:S(2)}) collective-permute-start(bf16[512,512]{1,0:T(8,128)(2,1)} %get-tuple-element.28), channel_id=1, source_target_pairs={{0,0},{1,1},{2,16},{3,17},{16,2},{17,3},{18,18},{19,19},{36,36},{3... | collective-permute-start | bytes 1572872 | tf_op jit(solution)/shard_map/ppermute | solution.py:268
  65.6 1.4 %collective-permute-start.6 = (bf16[512,512]{1,0:T(8,128)(2,1)}, bf16[512,512]{1,0:T(8,128)(2,1)}, u32[]{:S(2)}, u32[]{:S(2)}) collective-permute-start(bf16[512,512]{1,0:T(8,128)(2,1)} %get-tuple-element.33), channel_id=1, source_target_pairs={{0,1},{1,0},{2,17},{3,16},{16,3},{17,2},{18,19},{19,18},{36,37},{3... | collective-permute-start | bytes 1572872 | tf_op jit(solution)/shard_map/ppermute | solution.py:268
  67.1 3.8 %collective-permute-done.refs_0_ = bf16[512,512]{1,0:T(8,128)(2,1)} collective-permute-done((bf16[512,512]{1,0:T(8,128)(2,1)}, bf16[512,512]{1,0:T(8,128)(2,1)}, u32[]{:S(2)}, u32[]{:S(2)}) %collective-permute-start) | collective-permute-done | bytes 524320 | tf_op jit(solution)/shard_map/ppermute | solution.py:268
  70.9 1.3 %collective-permute-start.1 = (bf16[512,512]{1,0:T(8,128)(2,1)}, bf16[512,512]{1,0:T(8,128)(2,1)}, u32[]{:S(2)}, u32[]{:S(2)}) collective-permute-start(bf16[512,512]{1,0:T(8,128)(2,1)} %collective-permute-done.refs_0_), channel_id=1, source_target_pairs={{72,64},{73,65},{74,80},{75,81},{88,66},{89,67},{90,82},{91,83},{1... | collective-permute-start | bytes 1572872 | tf_op jit(solution)/shard_map/ppermute | solution.py:268
  72.2 3.4 %collective-permute-done.3.refs_4_ = bf16[256,512]{1,0:T(8,128)(2,1)} collective-permute-done((bf16[256,512]{1,0:T(8,128)(2,1)S(1)}, bf16[256,512]{1,0:T(8,128)(2,1)}, u32[]{:S(2)}, u32[]{:S(2)}) %collective-permute-start.3) | collective-permute-done | bytes 262176 | tf_op jit(solution)/shard_map/ppermute | solution.py:268
  75.6 6.0 %collective-permute-done.4.refs_3_ = bf16[256,512]{1,0:T(8,128)(2,1)S(1)} collective-permute-done((bf16[256,512]{1,0:T(8,128)(2,1)S(1)}, bf16[256,512]{1,0:T(8,128)(2,1)S(1)}, u32[]{:S(2)}, u32[]{:S(2)}) %collective-permute-start.4) | collective-permute-done | bytes 262176 | tf_op jit(solution)/shard_map/ppermute | solution.py:268
  81.6 0.7 copy-done.4
  82.3 1.3 %collective-permute-start.5 = (bf16[256,512]{1,0:T(8,128)(2,1)}, bf16[256,512]{1,0:T(8,128)(2,1)}, u32[]{:S(2)}, u32[]{:S(2)}) collective-permute-start(bf16[256,512]{1,0:T(8,128)(2,1)} %collective-permute-done.3.refs_4_), channel_id=1, source_target_pairs={{72,64},{73,65},{74,80},{75,81},{88,66},{89,67},{90,82},{91,83},{1... | collective-permute-start | bytes 786440 | tf_op jit(solution)/shard_map/ppermute | solution.py:268
  83.6 0.1 copy.23.col_ref
  83.7 12.3 %collective-permute-done.5.refs_5_ = bf16[256,512]{1,0:T(8,128)(2,1)} collective-permute-done((bf16[256,512]{1,0:T(8,128)(2,1)}, bf16[256,512]{1,0:T(8,128)(2,1)}, u32[]{:S(2)}, u32[]{:S(2)}) %collective-permute-start.5) | collective-permute-done | bytes 262176 | tf_op jit(solution)/shard_map/ppermute | solution.py:268
  96.1 1.2 %copy-done.3 = f32[512,512]{1,0:T(8,128)S(1)} copy-done((f32[512,512]{1,0:T(8,128)S(1)}, f32[512,512]{1,0:T(8,128)}, u32[]{:S(2)}) %copy-start.3) | copy-done | bytes 1048600
  97.3 0.9 copy-done.5
  98.2 5.3 %finish.1 = (f32[2,512,512]{2,1,0:T(8,128)}, bf16[2,512,512]{2,1,0:T(8,128)(2,1)}) custom-call(s32[6]{0:T(128)S(1)} %stack.19.ids, f32[512,512]{1,0:T(8,128)S(1)} %copy-done.1, f32[512,512]{1,0:T(8,128)S(1)} %copy-done.3, bf16[2,512,512]{2,1,0:T(8,128)(2,1)S(1)} %bitcast.22, bf16[2,512,512]{2,1,0:T(8,128)(2,1)S(1)} %bitcast.26, f32[512,1]{1,0:T(8,128)S(1)} %copy.23.col_ref, ...), custom_call_target="tpu_custom_call" | custom-call | flops 10485760 | bytes 7340032 | tf_op jit(solution)/shard_map/finish/pallas_call | solution.py:194
  (25 shorter events, 0.1 us)
Async XLA Ops:
  0.6 7.4 %copy-start.10 = (s32[16]{0:T(128)S(1)}, s32[16]{0:T(128)}, u32[]{:S(2)}) copy-start(s32[16]{0:T(128)} %param.19) | copy-start | bytes 196
  0.6 7.5 %copy-start.9 = (s32[16,6]{0,1:T(8,128)S(1)}, s32[16,6]{0,1:T(8,128)}, u32[]{:S(2)}) copy-start(s32[16,6]{0,1:T(8,128)} %param.18) | copy-start | bytes 1156
  0.7 7.6 %copy-start.8 = (f32[16,16]{1,0:T(8,128)S(1)}, f32[16,16]{1,0:T(8,128)}, u32[]{:S(2)}) copy-start(f32[16,16]{1,0:T(8,128)} %param.17) | copy-start | bytes 3076
  0.7 24.5 %all-to-all-start = ((bf16[16,64,512]{2,1,0:T(8,128)(2,1)}), bf16[16,64,512]{2,1,0:T(8,128)(2,1)S(1)}, u32[]{:S(2)}, u32[]{:S(2)}) async-start(bf16[16,64,512]{2,1,0:T(8,128)(2,1)} %bitcast.23), calls=%async_computation | async-start | bytes 2097152 | tf_op jit(solution)/shard_map/all_to_all | solution.py:279
  27.1 23.6 %all-to-all-start.1 = ((bf16[16,64,512]{2,1,0:T(8,128)(2,1)}), bf16[16,64,512]{2,1,0:T(8,128)(2,1)S(1)}, u32[]{:S(2)}, u32[]{:S(2)}) async-start(bf16[16,64,512]{2,1,0:T(8,128)(2,1)} %mix.1), calls=%async_computation.1 | async-start | bytes 2097152 | tf_op jit(solution)/shard_map/all_to_all | solution.py:288
  34.3 16.4 %copy-start.1 = (f32[512,512]{1,0:T(8,128)S(1)}, f32[512,512]{1,0:T(8,128)}, u32[]{:S(2)}) copy-start(f32[512,512]{1,0:T(8,128)} %ladder.2.part_a) | copy-start | bytes 3145732
  34.4 49.2 %copy-start.6 = (f32[512]{0:T(512)S(1)}, f32[512]{0:T(512)}, u32[]{:S(2)}) copy-start(f32[512]{0:T(512)} %param.15) | copy-start | bytes 6148
  34.4 61.7 %copy-start.7 = (f32[16]{0:T(128)S(1)}, f32[16]{0:T(128)}, u32[]{:S(2)}) copy-start(f32[16]{0:T(128)} %occ_ref.1) | copy-start | bytes 196
  50.7 45.3 %copy-start = (bf16[2,1,512,512]{3,2,1,0:T(8,128)(2,1)S(1)}, bf16[2,1,512,512]{3,2,1,0:T(8,128)(2,1)}, u32[]{:S(2)}) copy-start(bf16[2,1,512,512]{3,2,1,0:T(8,128)(2,1)} %param.10) | copy-start | bytes 3145732
  50.8 1.3 %copy-start.2 = (f32[512,512]{1,0:T(8,128)S(1)}, f32[512,512]{1,0:T(8,128)}, u32[]{:S(2)}) copy-start(f32[512,512]{1,0:T(8,128)} %ladder.3.part_b) | copy-start | bytes 3145732
  53.2 17.7 %collective-permute-start = (bf16[512,512]{1,0:T(8,128)(2,1)}, bf16[512,512]{1,0:T(8,128)(2,1)}, u32[]{:S(2)}, u32[]{:S(2)}) collective-permute-start(bf16[512,512]{1,0:T(8,128)(2,1)} %get-tuple-element.28), channel_id=1, source_target_pairs={{4,32},{5,33},{6,48},{7,49},{20,34},{21,35},{22,50},{23,51},{8,72}... | collective-permute-start | bytes 1572872 | tf_op jit(solution)/shard_map/ppermute | solution.py:268
  59.1 16.5 %collective-permute-start.3 = (bf16[256,512]{1,0:T(8,128)(2,1)S(1)}, bf16[256,512]{1,0:T(8,128)(2,1)}, u32[]{:S(2)}, u32[]{:S(2)}) collective-permute-start(bf16[256,512]{1,0:T(8,128)(2,1)S(1)} %get-tuple-element.29), channel_id=1, source_target_pairs={{4,33},{5,32},{6,49},{7,48},{20,35},{21,34},{22,51},{23,50},{8,73}... | collective-permute-start | bytes 786440 | tf_op jit(solution)/shard_map/ppermute | solution.py:268
  61.1 20.5 %collective-permute-start.4 = (bf16[256,512]{1,0:T(8,128)(2,1)S(1)}, bf16[256,512]{1,0:T(8,128)(2,1)S(1)}, u32[]{:S(2)}, u32[]{:S(2)}) collective-permute-start(bf16[256,512]{1,0:T(8,128)(2,1)S(1)} %get-tuple-element.30), channel_id=1, source_target_pairs={{4,33},{5,32},{6,49},{7,48},{20,35},{21,34},{22,51},{23,50},{8,65}... | collective-permute-start | bytes 786440 | tf_op jit(solution)/shard_map/ppermute | solution.py:268
  64.2 31.9 %collective-permute-start.2 = (bf16[512,512]{1,0:T(8,128)(2,1)}, bf16[512,512]{1,0:T(8,128)(2,1)}, u32[]{:S(2)}, u32[]{:S(2)}) collective-permute-start(bf16[512,512]{1,0:T(8,128)(2,1)} %get-tuple-element.28), channel_id=1, source_target_pairs={{0,0},{1,1},{2,16},{3,17},{16,2},{17,3},{18,18},{19,19},{36,36},{3... | collective-permute-start | bytes 1572872 | tf_op jit(solution)/shard_map/ppermute | solution.py:268
  65.6 30.4 %collective-permute-start.6 = (bf16[512,512]{1,0:T(8,128)(2,1)}, bf16[512,512]{1,0:T(8,128)(2,1)}, u32[]{:S(2)}, u32[]{:S(2)}) collective-permute-start(bf16[512,512]{1,0:T(8,128)(2,1)} %get-tuple-element.33), channel_id=1, source_target_pairs={{0,1},{1,0},{2,17},{3,16},{16,3},{17,2},{18,19},{19,18},{36,37},{3... | collective-permute-start | bytes 1572872 | tf_op jit(solution)/shard_map/ppermute | solution.py:268
  70.9 25.1 %collective-permute-start.1 = (bf16[512,512]{1,0:T(8,128)(2,1)}, bf16[512,512]{1,0:T(8,128)(2,1)}, u32[]{:S(2)}, u32[]{:S(2)}) collective-permute-start(bf16[512,512]{1,0:T(8,128)(2,1)} %collective-permute-done.refs_0_), channel_id=1, source_target_pairs={{72,64},{73,65},{74,80},{75,81},{88,66},{89,67},{90,82},{91,83},{1... | collective-permute-start | bytes 1572872 | tf_op jit(solution)/shard_map/ppermute | solution.py:268
  81.6 0.7 copy-start.4
  82.3 13.7 %collective-permute-start.5 = (bf16[256,512]{1,0:T(8,128)(2,1)}, bf16[256,512]{1,0:T(8,128)(2,1)}, u32[]{:S(2)}, u32[]{:S(2)}) collective-permute-start(bf16[256,512]{1,0:T(8,128)(2,1)} %collective-permute-done.3.refs_4_), channel_id=1, source_target_pairs={{72,64},{73,65},{74,80},{75,81},{88,66},{89,67},{90,82},{91,83},{1... | collective-permute-start | bytes 786440 | tf_op jit(solution)/shard_map/ppermute | solution.py:268
  96.1 1.2 %copy-start.3 = (f32[512,512]{1,0:T(8,128)S(1)}, f32[512,512]{1,0:T(8,128)}, u32[]{:S(2)}) copy-start(f32[512,512]{1,0:T(8,128)} %ladder.3.part_b) | copy-start | bytes 3145732
  97.3 0.9 copy-start.5

commit v10 on v8

--- a/solution.py
+++ b/solution.py
@@ -115,10 +115,11 @@
     )(slot, amps, ints, x, core, fock)
 
 
-def half_kernel(slot, part_a, part_b, sum_ref, send_a, low_b, high_b):
+def half_kernel(slot, part_a, part_b, sum_ref, send_a, send_b, low_b, high_b):
     core = slot[0]
     send_a[...] = (part_a[...] - sum_ref[core].astype(F32)).astype(BF16)
     rounded = (part_b[...] - sum_ref[1 - core].astype(F32)).astype(BF16)
+    send_b[...] = rounded
 
     @pl.when(pl.program_id(0) == 0)
     def _():
@@ -135,12 +136,12 @@
     strip = pl.BlockSpec((rows, virt), lambda r, s: (r, 0))
     return pl.pallas_call(
         half_kernel,
-        out_shape=[jax.ShapeDtypeStruct((n, virt), BF16) for n in (virt, rows, rows)],
+        out_shape=[jax.ShapeDtypeStruct((n, virt), BF16) for n in (virt, virt, rows, rows)],
         grid_spec=pltpu.PrefetchScalarGridSpec(
             num_scalar_prefetch=1,
             grid=(2,),
             in_specs=[strip, strip, pl.BlockSpec((2, rows, virt), lambda r, s: (0, r, 0))],
-            out_specs=[strip, whole((rows, virt)), whole((rows, virt))],
+            out_specs=[strip, strip, whole((rows, virt)), whole((rows, virt))],
         ),
         compiler_params=params(16),
         cost_estimate=pl.CostEstimate(
@@ -150,16 +151,12 @@
     )(slot, part_a, part_b, sums)
 
 
-def finish_kernel(counts, ids, part_ref, sum_ref, amp_ref, col_ref, row_ref, occ_ref, *refs):
+def finish_kernel(split, ids, part_ref, sum_ref, amp_ref, col_ref, row_ref, occ_ref, *refs):
     res_ref, new_ref = refs[-2:]
-    pieces = []
-    for n in counts:
-        piece = refs[0][...]
-        for kind in range(1, n):
-            piece = jnp.where(ids[3] == kind, refs[kind][...], piece)
-        pieces.append(piece)
-        refs = refs[n:]
-    mirror = jnp.concatenate(pieces, axis=0)
+    mirror = jnp.where(ids[3] == 1, refs[1][...], refs[0][...])
+    if split:
+        mirror = jnp.concatenate([refs[3][...], mirror], axis=0)
+    mirror = jnp.where(ids[3] == 2, refs[2][...], mirror)
     half = part_ref[...] - sum_ref[...].astype(F32)
     residual = half + mirror.astype(F32).T
     denominator = col_ref[...] + row_ref[...] - occ_ref[ids[1]] - occ_ref[ids[2]]
@@ -171,10 +168,8 @@
     virt = part.shape[0]
     rows = min(256, virt)
     strip = pl.BlockSpec((None, rows, virt), lambda r, s: (s[0], r, 0))
-    counts = [len(piece) for piece in mirrors]
-    mirrors = sum(mirrors, ())
     return pl.pallas_call(
-        functools.partial(finish_kernel, counts),
+        functools.partial(finish_kernel, len(mirrors) > 3),
         out_shape=[
             jax.ShapeDtypeStruct(amps.shape, F32),
             jax.ShapeDtypeStruct(amps.shape, BF16),
@@ -194,7 +189,7 @@
             + [pl.BlockSpec(memory_space=pl.ANY)] * len(held),
             out_specs=[strip, strip],
         ),
-        input_output_aliases={7 + sum(counts) + m: m for m in range(len(held))},
+        input_output_aliases={7 + len(mirrors) + m: m for m in range(len(held))},
         compiler_params=params(16, dimension_semantics=("arbitrary",)),
         cost_estimate=pl.CostEstimate(
             flops=20 * part.size, bytes_accessed=14 * part.size, transcendentals=0
@@ -275,20 +270,20 @@
     part_b = ladder(slot_b, amps, ints, thc_factor, thc_core, fock_vir)
     sums, part_b = lax.optimization_barrier((sums, part_b))
     sums = sums.reshape(rows_i, virt, virt)
-    send_a, low_b, high_b = half_of(slot_a, part_a, part_b, sums)
+    send_a, send_b, low_b, high_b = half_of(slot_a, part_a, part_b, sums)
     near_a = send(send_a, 0, middle="inward", other="mirror")
+    low_b = send(low_b, 1, middle="mirror", other="mirror")
     near_b = send(high_b, 1, middle="inward", other="mirror")
-    low_b = send(low_b, 1, diagonal="mirror", middle="mirror", other="mirror")
     same_a = send(send_a, 0, diagonal="mirror")
-    same_b = send(high_b, 1, diagonal="mirror")
-    near_b, low_b = lax.optimization_barrier((near_b, low_b))
+    same_b = send(send_b, 1, diagonal="mirror")
+    low_b, near_b = lax.optimization_barrier((low_b, near_b))
     far_a = send(near_a, 0, middle="outward")
     far_b = send(near_b, 0, middle="outward")
 
     far_a, far_b = lax.optimization_barrier((far_a, far_b))
     tables = (amps, eps_col, eps_row, eps_occ)
-    mirror_a = [(near_a, far_a, same_a)]
-    mirror_b = [(low_b,), (near_b, far_b, same_b)]
+    mirror_a = (near_a, far_a, same_a)
+    mirror_b = (near_b, far_b, same_b, low_b)
     held = finish(ids_a, part_a, sums, mirror_a, *tables, ())
     residual, updated = finish(ids_b, part_b, sums, mirror_b, *tables, held)
     return (

time: 102 us -> 107 us (1.049)
  the two profiles are of different devices: /device:TPU:36 before, /device:TPU:33 now
where the time goes in v10:
time: 107 us; the launch traced here: 106 us
  Pallas kernels  41.8 us (39%)
  starting transfers between devices  33.7 us (31%)
  waiting for transfers between devices  27.3 us (26%)
  local copies, waits for them, and re-layouts  2.53 us (2%)
    pallas_call x2, Pallas kernels, ladder(): pl.pallas_call(ladder_kernel, out_shape=jax.ShapeDtypeStruct((virt, virt)...  32.7 us
    ppermute x7, waiting for transfers between devices, send(): return lax.ppermute(array, AXES, pairs)  26.4 us
    ppermute x7, starting transfers between devices, send(): return lax.ppermute(array, AXES, pairs)  19 us
    all_to_all x1, starting transfers between devices, shards(): slices = lax.all_to_all(slices, 'occj', 0, 0, tiled=True)  7.54 us
    all_to_all x1, starting transfers between devices, shards(): sums = lax.all_to_all(sums, 'occj', 0, 0, tiled=True)  7.11 us
    pallas_call x2, Pallas kernels, finish(): pl.pallas_call(functools.partial(finish_kernel, len(mirrors) > 3), out_sh...  6.05 us
  transfers between devices with their start and end apart: 9, of which 5 were waited for; matrix products, arithmetic and copies ran while one was open for 1% of the time, Pallas kernels for 34%

profile of v10, /device:TPU:33, one launch (start us, length us, event | category | flops | bytes accessed | tf_op | source)
XLA Modules:
  0.0 106.5 jit_solution(3561562135187825128)
XLA Ops:
  0.7 7.5 %all-to-all-start = ((bf16[16,64,512]{2,1,0:T(8,128)(2,1)}), bf16[16,64,512]{2,1,0:T(8,128)(2,1)S(1)}, u32[]{:S(2)}, u32[]{:S(2)}) async-start(bf16[16,64,512]{2,1,0:T(8,128)(2,1)} %bitcast.24), calls=%async_computation | async-start | bytes 2097152 | tf_op jit(solution)/shard_map/all_to_all | solution.py:258
  8.3 0.1 convert_reduce_fusion
  8.4 0.1 copy.24
  8.5 0.1 broadcast_in_dim.7
  8.6 0.1 reshape.78
  8.7 0.1 copy.25
  8.8 0.1 compare_select_fusion.w_ref
  8.9 0.1 add_add_fusion
  9.0 16.3 %ladder.2.part_a.part_ref = f32[512,512]{1,0:T(8,128)} custom-call(s32[1]{0:T(128)} %bitcast.1.slot, bf16[2,512,512]{2,1,0:T(8,128)(2,1)} %bitcast.25, bf16[2,512,512]{2,1,0:T(8,128)(2,1)} %bitcast.35, bf16[512,2048]{1,0:T(8,128)(2,1)} %x_ref.3, bf16[2048,2048]{1,0:T(8,128)(2,1)} %core_ref.3, bf16[512,512]{1,0:T(8,128)(2,1)} %fock_ref.3), custom_call_target="tpu_custom_call" | custom-call | flops 11005853696 | bytes 12582912 | tf_op jit(solution)/shard_map/ladder/pallas_call | solution.py:92
  25.3 0.1 all-to-all-done.in_ref
  25.4 2.0 %mix.1 = bf16[16,64,512]{2,1,0:T(8,128)(2,1)} custom-call(f32[256,256]{1,0:T(8,128)S(1)} %compare_select_fusion.w_ref, bf16[16,64,512]{2,1,0:T(8,128)(2,1)S(1)} %all-to-all-done.in_ref), custom_call_target="tpu_custom_call" | custom-call | flops 1000000000 | bytes 2097152 | tf_op jit(solution)/shard_map/mix/pallas_call | solution.py:50
  27.4 7.1 %all-to-all-start.1 = ((bf16[16,64,512]{2,1,0:T(8,128)(2,1)}), bf16[16,64,512]{2,1,0:T(8,128)(2,1)S(1)}, u32[]{:S(2)}, u32[]{:S(2)}) async-start(bf16[16,64,512]{2,1,0:T(8,128)(2,1)} %mix.1), calls=%async_computation.1 | async-start | bytes 2097152 | tf_op jit(solution)/shard_map/all_to_all | solution.py:269
  34.5 0.0 copy-start.6
  34.5 0.0 copy-start.7
  34.5 16.4 %ladder.3.part_b.part_ref = f32[512,512]{1,0:T(8,128)} custom-call(s32[1]{0:T(128)} %sub.16.slot, bf16[2,512,512]{2,1,0:T(8,128)(2,1)} %bitcast.26, bf16[2,512,512]{2,1,0:T(8,128)(2,1)} %bitcast.36, bf16[512,2048]{1,0:T(8,128)(2,1)} %x_ref.3, bf16[2048,2048]{1,0:T(8,128)(2,1)} %core_ref.3, bf16[512,512]{1,0:T(8,128)(2,1)} %fock_ref.3), custom_call_target="tpu_custom_call" | custom-call | flops 11005853696 | bytes 12582912 | tf_op jit(solution)/shard_map/ladder/pallas_call | solution.py:92
  50.9 0.8 all-to-all-done.1
  51.7 1.2 %copy-done.2 = f32[512,512]{1,0:T(8,128)S(1)} copy-done((f32[512,512]{1,0:T(8,128)S(1)}, f32[512,512]{1,0:T(8,128)}, u32[]{:S(2)}) %copy-start.2) | copy-done | bytes 1048600
  52.9 1.1 %half.1 = (bf16[512,512]{1,0:T(8,128)(2,1)}, bf16[512,512]{1,0:T(8,128)(2,1)}, bf16[256,512]{1,0:T(8,128)(2,1)S(1)}, bf16[256,512]{1,0:T(8,128)(2,1)S(1)}) custom-call(s32[1]{0:T(128)} %bitcast.1.slot, f32[512,512]{1,0:T(8,128)S(1)} %copy-done.1, f32[512,512]{1,0:T(8,128)S(1)} %copy-done.2, bf16[2,512,512]{2,1,0:T(8,128)(2,1)S(1)} %bitcast.21), custom_call_target="tpu_custom_call" | custom-call | bytes 4194304 | tf_op jit(solution)/shard_map/half/pallas_call | solution.py:137
  54.1 1.3 %collective-permute-start.2 = (bf16[512,512]{1,0:T(8,128)(2,1)}, bf16[512,512]{1,0:T(8,128)(2,1)}, u32[]{:S(2)}, u32[]{:S(2)}) collective-permute-start(bf16[512,512]{1,0:T(8,128)(2,1)} %get-tuple-element.36), channel_id=1, source_target_pairs={{4,32},{5,33},{6,48},{7,49},{20,34},{21,35},{22,50},{23,51},{8,72}... | collective-permute-start | bytes 1572872 | tf_op jit(solution)/shard_map/ppermute | solution.py:245
  55.3 0.7 collective-permute-start
  56.0 1.3 %collective-permute-start.1 = (bf16[256,512]{1,0:T(8,128)(2,1)S(1)}, bf16[256,512]{1,0:T(8,128)(2,1)}, u32[]{:S(2)}, u32[]{:S(2)}) collective-permute-start(bf16[256,512]{1,0:T(8,128)(2,1)S(1)} %get-tuple-element.34), channel_id=1, source_target_pairs={{4,33},{5,32},{6,49},{7,48},{20,35},{21,34},{22,51},{23,50},{8,73}... | collective-permute-start | bytes 786440 | tf_op jit(solution)/shard_map/ppermute | solution.py:245
  57.3 13.0 %collective-permute-done.2.refs_0_ = bf16[512,512]{1,0:T(8,128)(2,1)} collective-permute-done((bf16[512,512]{1,0:T(8,128)(2,1)}, bf16[512,512]{1,0:T(8,128)(2,1)}, u32[]{:S(2)}, u32[]{:S(2)}) %collective-permute-start.2) | collective-permute-done | bytes 524320 | tf_op jit(solution)/shard_map/ppermute | solution.py:245
  70.3 6.0 %collective-permute-start.3 = (bf16[512,512]{1,0:T(8,128)(2,1)}, bf16[512,512]{1,0:T(8,128)(2,1)}, u32[]{:S(2)}, u32[]{:S(2)}) collective-permute-start(bf16[512,512]{1,0:T(8,128)(2,1)} %collective-permute-done.2.refs_0_), channel_id=1, source_target_pairs={{72,64},{73,65},{74,80},{75,81},{88,66},{89,67},{90,82},{91,83},{1... | collective-permute-start | bytes 1572872 | tf_op jit(solution)/shard_map/ppermute | solution.py:245
  76.4 1.9 %collective-permute-start.6 = (bf16[512,512]{1,0:T(8,128)(2,1)}, bf16[512,512]{1,0:T(8,128)(2,1)}, u32[]{:S(2)}, u32[]{:S(2)}) collective-permute-start(bf16[512,512]{1,0:T(8,128)(2,1)} %get-tuple-element.36), channel_id=1, source_target_pairs={{0,0},{1,1},{2,16},{3,17},{16,2},{17,3},{18,18},{19,19},{36,36},{3... | collective-permute-start | bytes 1572872 | tf_op jit(solution)/shard_map/ppermute | solution.py:245
  78.3 5.8 %collective-permute-start.5 = (bf16[512,512]{1,0:T(8,128)(2,1)}, bf16[512,512]{1,0:T(8,128)(2,1)}, u32[]{:S(2)}, u32[]{:S(2)}) collective-permute-start(bf16[512,512]{1,0:T(8,128)(2,1)} %get-tuple-element.38), channel_id=1, source_target_pairs={{0,1},{1,0},{2,17},{3,16},{16,3},{17,2},{18,19},{19,18},{36,37},{3... | collective-permute-start | bytes 1572872 | tf_op jit(solution)/shard_map/ppermute | solution.py:245
  84.1 0.7 copy-done.4
  84.8 2.0 %collective-permute-start.4 = (bf16[256,512]{1,0:T(8,128)(2,1)}, bf16[256,512]{1,0:T(8,128)(2,1)}, u32[]{:S(2)}, u32[]{:S(2)}) collective-permute-start(bf16[256,512]{1,0:T(8,128)(2,1)} %collective-permute-done.1.refs_0_), channel_id=1, source_target_pairs={{72,64},{73,65},{74,80},{75,81},{88,66},{89,67},{90,82},{91,83},{1... | collective-permute-start | bytes 786440 | tf_op jit(solution)/shard_map/ppermute | solution.py:245
  86.9 0.1 copy.27.col_ref
  87.0 5.6 %collective-permute-done.4.refs_1_ = bf16[256,512]{1,0:T(8,128)(2,1)} collective-permute-done((bf16[256,512]{1,0:T(8,128)(2,1)}, bf16[256,512]{1,0:T(8,128)(2,1)}, u32[]{:S(2)}, u32[]{:S(2)}) %collective-permute-start.4) | collective-permute-done | bytes 262176 | tf_op jit(solution)/shard_map/ppermute | solution.py:245
  92.7 3.0 %finish.2 = (f32[2,512,512]{2,1,0:T(8,128)}, bf16[2,512,512]{2,1,0:T(8,128)(2,1)}) custom-call(s32[4]{0:T(128)S(1)} %get-tuple-element.40.ids, f32[512,512]{1,0:T(8,128)S(1)} %copy-done.1, bf16[2,512,512]{2,1,0:T(8,128)(2,1)S(1)} %bitcast.22, bf16[2,512,512]{2,1,0:T(8,128)(2,1)S(1)} %bitcast.27, f32[512,1]{1,0:T(8,128)S(1)} %copy.27.col_ref, ...), custom_call_target="tpu_custom_call" | custom-call | flops 5242880 | bytes 3670016 | tf_op jit(solution)/shard_map/finish/pallas_call | solution.py:171
  95.7 7.7 %collective-permute-done.5.refs_2_ = bf16[512,512]{1,0:T(8,128)(2,1)} collective-permute-done((bf16[512,512]{1,0:T(8,128)(2,1)}, bf16[512,512]{1,0:T(8,128)(2,1)}, u32[]{:S(2)}, u32[]{:S(2)}) %collective-permute-start.5) | collective-permute-done | bytes 524320 | tf_op jit(solution)/shard_map/ppermute | solution.py:245
  103.5 3.0 %finish.3 = (f32[2,512,512]{2,1,0:T(8,128)}, bf16[2,512,512]{2,1,0:T(8,128)(2,1)}) custom-call(s32[4]{0:T(128)S(1)} %get-tuple-element.24.ids, f32[512,512]{1,0:T(8,128)S(1)} %copy-done.3, bf16[2,512,512]{2,1,0:T(8,128)(2,1)S(1)} %bitcast.23, bf16[2,512,512]{2,1,0:T(8,128)(2,1)S(1)} %bitcast.28, ...), custom_call_target="tpu_custom_call", output_to_operand_aliasing={{0}: (11, {}), {1}: (12, {})} | custom-call | flops 5242880 | bytes 3670016 | tf_op jit(solution)/shard_map/finish/pallas_call | solution.py:171
  (26 shorter events, 0.1 us)
Async XLA Ops:
  0.6 7.6 %copy-start.10 = (s32[16]{0:T(128)S(1)}, s32[16]{0:T(128)}, u32[]{:S(2)}) copy-start(s32[16]{0:T(128)} %param.19) | copy-start | bytes 196
  0.6 7.6 %copy-start.9 = (s32[16,6]{0,1:T(8,128)S(1)}, s32[16,6]{0,1:T(8,128)}, u32[]{:S(2)}) copy-start(s32[16,6]{0,1:T(8,128)} %param.18) | copy-start | bytes 1156
  0.7 7.7 %copy-start.8 = (f32[16,16]{1,0:T(8,128)S(1)}, f32[16,16]{1,0:T(8,128)}, u32[]{:S(2)}) copy-start(f32[16,16]{1,0:T(8,128)} %param.17) | copy-start | bytes 3076
  0.7 24.8 %all-to-all-start = ((bf16[16,64,512]{2,1,0:T(8,128)(2,1)}), bf16[16,64,512]{2,1,0:T(8,128)(2,1)S(1)}, u32[]{:S(2)}, u32[]{:S(2)}) async-start(bf16[16,64,512]{2,1,0:T(8,128)(2,1)} %bitcast.24), calls=%async_computation | async-start | bytes 2097152 | tf_op jit(solution)/shard_map/all_to_all | solution.py:258
  27.4 24.3 %all-to-all-start.1 = ((bf16[16,64,512]{2,1,0:T(8,128)(2,1)}), bf16[16,64,512]{2,1,0:T(8,128)(2,1)S(1)}, u32[]{:S(2)}, u32[]{:S(2)}) async-start(bf16[16,64,512]{2,1,0:T(8,128)(2,1)} %mix.1), calls=%async_computation.1 | async-start | bytes 2097152 | tf_op jit(solution)/shard_map/all_to_all | solution.py:269
  34.5 17.2 %copy-start.1 = (f32[512,512]{1,0:T(8,128)S(1)}, f32[512,512]{1,0:T(8,128)}, u32[]{:S(2)}) copy-start(f32[512,512]{1,0:T(8,128)} %ladder.2.part_a.part_ref) | copy-start | bytes 3145732
  34.5 52.4 %copy-start.6 = (f32[512]{0:T(512)S(1)}, f32[512]{0:T(512)}, u32[]{:S(2)}) copy-start(f32[512]{0:T(512)} %param.15) | copy-start | bytes 6148
  34.5 58.1 %copy-start.7 = (f32[16]{0:T(128)S(1)}, f32[16]{0:T(128)}, u32[]{:S(2)}) copy-start(f32[16]{0:T(128)} %occ_ref.3) | copy-start | bytes 196
  50.9 41.7 %copy-start = (bf16[2,1,512,512]{3,2,1,0:T(8,128)(2,1)S(1)}, bf16[2,1,512,512]{3,2,1,0:T(8,128)(2,1)}, u32[]{:S(2)}) copy-start(bf16[2,1,512,512]{3,2,1,0:T(8,128)(2,1)} %param.10) | copy-start | bytes 3145732
  51.7 1.2 %copy-start.2 = (f32[512,512]{1,0:T(8,128)S(1)}, f32[512,512]{1,0:T(8,128)}, u32[]{:S(2)}) copy-start(f32[512,512]{1,0:T(8,128)} %ladder.3.part_b.part_ref) | copy-start | bytes 3145732
  54.1 16.3 %collective-permute-start.2 = (bf16[512,512]{1,0:T(8,128)(2,1)}, bf16[512,512]{1,0:T(8,128)(2,1)}, u32[]{:S(2)}, u32[]{:S(2)}) collective-permute-start(bf16[512,512]{1,0:T(8,128)(2,1)} %get-tuple-element.36), channel_id=1, source_target_pairs={{4,32},{5,33},{6,48},{7,49},{20,34},{21,35},{22,50},{23,51},{8,72}... | collective-permute-start | bytes 1572872 | tf_op jit(solution)/shard_map/ppermute | solution.py:245
  55.3 28.7 %collective-permute-start = (bf16[256,512]{1,0:T(8,128)(2,1)S(1)}, bf16[256,512]{1,0:T(8,128)(2,1)S(1)}, u32[]{:S(2)}, u32[]{:S(2)}) collective-permute-start(bf16[256,512]{1,0:T(8,128)(2,1)S(1)} %get-tuple-element.33), channel_id=1, source_target_pairs={{4,33},{5,32},{6,49},{7,48},{20,35},{21,34},{22,51},{23,50},{8,65}... | collective-permute-start | bytes 786440 | tf_op jit(solution)/shard_map/ppermute | solution.py:245
  56.0 28.8 %collective-permute-start.1 = (bf16[256,512]{1,0:T(8,128)(2,1)S(1)}, bf16[256,512]{1,0:T(8,128)(2,1)}, u32[]{:S(2)}, u32[]{:S(2)}) collective-permute-start(bf16[256,512]{1,0:T(8,128)(2,1)S(1)} %get-tuple-element.34), channel_id=1, source_target_pairs={{4,33},{5,32},{6,49},{7,48},{20,35},{21,34},{22,51},{23,50},{8,73}... | collective-permute-start | bytes 786440 | tf_op jit(solution)/shard_map/ppermute | solution.py:245
  70.3 22.3 %collective-permute-start.3 = (bf16[512,512]{1,0:T(8,128)(2,1)}, bf16[512,512]{1,0:T(8,128)(2,1)}, u32[]{:S(2)}, u32[]{:S(2)}) collective-permute-start(bf16[512,512]{1,0:T(8,128)(2,1)} %collective-permute-done.2.refs_0_), channel_id=1, source_target_pairs={{72,64},{73,65},{74,80},{75,81},{88,66},{89,67},{90,82},{91,83},{1... | collective-permute-start | bytes 1572872 | tf_op jit(solution)/shard_map/ppermute | solution.py:245
  76.4 16.3 %collective-permute-start.6 = (bf16[512,512]{1,0:T(8,128)(2,1)}, bf16[512,512]{1,0:T(8,128)(2,1)}, u32[]{:S(2)}, u32[]{:S(2)}) collective-permute-start(bf16[512,512]{1,0:T(8,128)(2,1)} %get-tuple-element.36), channel_id=1, source_target_pairs={{0,0},{1,1},{2,16},{3,17},{16,2},{17,3},{18,18},{19,19},{36,36},{3... | collective-permute-start | bytes 1572872 | tf_op jit(solution)/shard_map/ppermute | solution.py:245
  78.3 25.2 %collective-permute-start.5 = (bf16[512,512]{1,0:T(8,128)(2,1)}, bf16[512,512]{1,0:T(8,128)(2,1)}, u32[]{:S(2)}, u32[]{:S(2)}) collective-permute-start(bf16[512,512]{1,0:T(8,128)(2,1)} %get-tuple-element.38), channel_id=1, source_target_pairs={{0,1},{1,0},{2,17},{3,16},{16,3},{17,2},{18,19},{19,18},{36,37},{3... | collective-permute-start | bytes 1572872 | tf_op jit(solution)/shard_map/ppermute | solution.py:245
  84.1 0.7 copy-start.4
  84.8 7.8 %collective-permute-start.4 = (bf16[256,512]{1,0:T(8,128)(2,1)}, bf16[256,512]{1,0:T(8,128)(2,1)}, u32[]{:S(2)}, u32[]{:S(2)}) collective-permute-start(bf16[256,512]{1,0:T(8,128)(2,1)} %collective-permute-done.1.refs_0_), channel_id=1, source_target_pairs={{72,64},{73,65},{74,80},{75,81},{88,66},{89,67},{90,82},{91,83},{1... | collective-permute-start | bytes 786440 | tf_op jit(solution)/shard_map/ppermute | solution.py:245
  92.7 10.8 %copy-start.3 = (f32[512,512]{1,0:T(8,128)S(1)}, f32[512,512]{1,0:T(8,128)}, u32[]{:S(2)}) copy-start(f32[512,512]{1,0:T(8,128)} %ladder.3.part_b.part_ref) | copy-start | bytes 3145732
  92.7 10.8 %copy-start.5 = (bf16[256,512]{1,0:T(8,128)(2,1)S(1)}, bf16[256,512]{1,0:T(8,128)(2,1)}, u32[]{:S(2)}) copy-start(bf16[256,512]{1,0:T(8,128)(2,1)} %copy-done.4) | copy-start | bytes 786436

commit v11 on v9

--- a/solution.py
+++ b/solution.py
@@ -213,7 +213,7 @@
             + [across(m, late) for m in mirror_b],
             out_specs=[strip, strip],
         ),
-        compiler_params=params(24, dimension_semantics=("arbitrary",)),
+        compiler_params=params(52, dimension_semantics=("arbitrary",)),
         cost_estimate=pl.CostEstimate(
             flops=40 * part_a.size, bytes_accessed=28 * part_a.size, transcendentals=0
         ),
@@ -291,11 +291,11 @@
     sums = sums.reshape(rows_i, virt, virt)
     send_a, send_b, low_b, high_b = half_of(slot_a, part_a, part_b, sums)
     near_a = send(send_a, 0, middle="inward", other="mirror")
+    low_b = send(low_b, 1, middle="mirror", other="mirror")
     near_b = send(high_b, 1, middle="inward", other="mirror")
-    low_b = send(low_b, 1, middle="mirror", other="mirror")
     same_a = send(send_a, 0, diagonal="mirror")
     same_b = send(send_b, 1, diagonal="mirror")
-    near_b, low_b = lax.optimization_barrier((near_b, low_b))
+    low_b, near_b = lax.optimization_barrier((low_b, near_b))
     far_a = send(near_a, 0, middle="outward")
     far_b = send(near_b, 0, middle="outward")
     mirror_a, mirror_b = (near_a, far_a, same_a), (low_b, near_b, far_b, same_b)

time: 104 us -> 101 us (0.971)
  local copies, waits for them, and re-layouts: 4.85 us -> 2.28 us
  starting transfers between devices: 31 us -> 29.6 us
    unnamed x22 -> x16, local copies, waits for them, and re-layouts: 4.2 us -> 1.63 us
    ppermute x7, starting transfers between devices: 16.4 us -> 15 us  [send(): return lax.ppermute(array, AXES, pairs)]
  transfers between devices with their start and end apart: 9 -> 9, of which waited for: 4 -> 3; matrix products, arithmetic and copies ran while one was open for 1% -> 1% of each run, Pallas kernels for 31% -> 33%
where the time goes in v11:
time: 101 us; the launch traced here: 100 us
  Pallas kernels  41.6 us (41%)
  starting transfers between devices  29.6 us (29%)
  waiting for transfers between devices  25.8 us (26%)
  local copies, waits for them, and re-layouts  2.28 us (2%)
    pallas_call x2, Pallas kernels, ladder(): pl.pallas_call(ladder_kernel, out_shape=jax.ShapeDtypeStruct((virt, virt)...  32.7 us
    ppermute x7, waiting for transfers between devices, send(): return lax.ppermute(array, AXES, pairs)  25.8 us
    ppermute x7, starting transfers between devices, send(): return lax.ppermute(array, AXES, pairs)  15 us
    all_to_all x1, starting transfers between devices, shards(): slices = lax.all_to_all(slices, 'occj', 0, 0, tiled=True)  7.38 us
    all_to_all x1, starting transfers between devices, shards(): sums = lax.all_to_all(sums, 'occj', 0, 0, tiled=True)  7.23 us
    pallas_call x1, Pallas kernels, finish(): pl.pallas_call(finish_kernel, out_shape=[jax.ShapeDtypeStruct(amps.shape,...  5.88 us
  transfers between devices with their start and end apart: 9, of which 3 were waited for; matrix products, arithmetic and copies ran while one was open for 1% of the time, Pallas kernels for 33%

profile of v11, /device:TPU:36, one launch (start us, length us, event | category | flops | bytes accessed | tf_op | source)
XLA Modules:
  0.0 100.3 jit_solution(9036782648607220253)
XLA Ops:
  0.7 7.4 %all-to-all-start = ((bf16[16,64,512]{2,1,0:T(8,128)(2,1)}), bf16[16,64,512]{2,1,0:T(8,128)(2,1)S(1)}, u32[]{:S(2)}, u32[]{:S(2)}) async-start(bf16[16,64,512]{2,1,0:T(8,128)(2,1)} %bitcast.25), calls=%async_computation | async-start | bytes 2097152 | tf_op jit(solution)/shard_map/all_to_all | solution.py:279
  8.1 0.1 convert_reduce_fusion
  8.2 0.1 copy.21
  8.3 0.1 broadcast_in_dim.7
  8.4 0.1 reshape.78
  8.5 0.1 copy.22
  8.7 0.1 compare_select_fusion.w_ref
  8.8 0.1 stack.19.ids
  8.9 16.3 %ladder.2.part_a = f32[512,512]{1,0:T(8,128)} custom-call(s32[1]{0:T(128)} %bitcast.1.slot, bf16[2,512,512]{2,1,0:T(8,128)(2,1)} %bitcast.26, bf16[2,512,512]{2,1,0:T(8,128)(2,1)} %bitcast.31, bf16[512,2048]{1,0:T(8,128)(2,1)} %x_ref.3, bf16[2048,2048]{1,0:T(8,128)(2,1)} %core_ref.3, bf16[512,512]{1,0:T(8,128)(2,1)} %fock_ref.3), custom_call_target="tpu_custom_call" | custom-call | flops 11005853696 | bytes 12582912 | tf_op jit(solution)/shard_map/ladder/pallas_call | solution.py:92
  25.1 0.0 all-to-all-done.in_ref
  25.1 2.0 %mix.1 = bf16[16,64,512]{2,1,0:T(8,128)(2,1)} custom-call(f32[256,256]{1,0:T(8,128)S(1)} %compare_select_fusion.w_ref, bf16[16,64,512]{2,1,0:T(8,128)(2,1)S(1)} %all-to-all-done.in_ref), custom_call_target="tpu_custom_call" | custom-call | flops 1000000000 | bytes 2097152 | tf_op jit(solution)/shard_map/mix/pallas_call | solution.py:50
  27.1 7.2 %all-to-all-start.1 = ((bf16[16,64,512]{2,1,0:T(8,128)(2,1)}), bf16[16,64,512]{2,1,0:T(8,128)(2,1)S(1)}, u32[]{:S(2)}, u32[]{:S(2)}) async-start(bf16[16,64,512]{2,1,0:T(8,128)(2,1)} %mix.1), calls=%async_computation.1 | async-start | bytes 2097152 | tf_op jit(solution)/shard_map/all_to_all | solution.py:288
  34.3 0.0 copy-start.3
  34.4 16.4 %ladder.3.part_b = f32[512,512]{1,0:T(8,128)} custom-call(s32[1]{0:T(128)} %sub.13.slot, bf16[2,512,512]{2,1,0:T(8,128)(2,1)} %bitcast.27, bf16[2,512,512]{2,1,0:T(8,128)(2,1)} %bitcast.32, bf16[512,2048]{1,0:T(8,128)(2,1)} %x_ref.3, bf16[2048,2048]{1,0:T(8,128)(2,1)} %core_ref.3, bf16[512,512]{1,0:T(8,128)(2,1)} %fock_ref.3), custom_call_target="tpu_custom_call" | custom-call | flops 11005853696 | bytes 12582912 | tf_op jit(solution)/shard_map/ladder/pallas_call | solution.py:92
  50.8 0.0 all-to-all-done.1
  50.8 1.6 %copy-done.2 = f32[512,512]{1,0:T(8,128)S(1)} copy-done((f32[512,512]{1,0:T(8,128)S(1)}, f32[512,512]{1,0:T(8,128)}, u32[]{:S(2)}) %copy-start.2) | copy-done | bytes 1048600
  52.4 1.0 %half.1 = (bf16[512,512]{1,0:T(8,128)(2,1)S(1)}, bf16[512,512]{1,0:T(8,128)(2,1)}, bf16[256,512]{1,0:T(8,128)(2,1)S(1)}, bf16[256,512]{1,0:T(8,128)(2,1)S(1)}) custom-call(s32[1]{0:T(128)} %bitcast.1.slot, f32[512,512]{1,0:T(8,128)S(1)} %copy-done.1, f32[512,512]{1,0:T(8,128)S(1)} %copy-done.2, bf16[2,512,512]{2,1,0:T(8,128)(2,1)S(1)} %bitcast.21), custom_call_target="tpu_custom_call" | custom-call | bytes 4194304 | tf_op jit(solution)/shard_map/half/pallas_call | solution.py:137
  53.4 5.1 %collective-permute-start = (bf16[512,512]{1,0:T(8,128)(2,1)S(1)}, bf16[512,512]{1,0:T(8,128)(2,1)S(1)}, u32[]{:S(2)}, u32[]{:S(2)}) collective-permute-start(bf16[512,512]{1,0:T(8,128)(2,1)S(1)} %get-tuple-element.28), channel_id=1, source_target_pairs={{4,32},{5,33},{6,48},{7,49},{20,34},{21,35},{22,50},{23,51},{8,72}... | collective-permute-start | bytes 1572872 | tf_op jit(solution)/shard_map/ppermute | solution.py:268
  58.5 3.1 %collective-permute-start.3 = (bf16[256,512]{1,0:T(8,128)(2,1)S(1)}, bf16[256,512]{1,0:T(8,128)(2,1)S(1)}, u32[]{:S(2)}, u32[]{:S(2)}) collective-permute-start(bf16[256,512]{1,0:T(8,128)(2,1)S(1)} %get-tuple-element.29), channel_id=1, source_target_pairs={{4,33},{5,32},{6,49},{7,48},{20,35},{21,34},{22,51},{23,50},{8,65}... | collective-permute-start | bytes 786440 | tf_op jit(solution)/shard_map/ppermute | solution.py:268
  61.6 1.3 %collective-permute-start.4 = (bf16[256,512]{1,0:T(8,128)(2,1)S(1)}, bf16[256,512]{1,0:T(8,128)(2,1)S(1)}, u32[]{:S(2)}, u32[]{:S(2)}) collective-permute-start(bf16[256,512]{1,0:T(8,128)(2,1)S(1)} %get-tuple-element.30), channel_id=1, source_target_pairs={{4,33},{5,32},{6,49},{7,48},{20,35},{21,34},{22,51},{23,50},{8,73}... | collective-permute-start | bytes 786440 | tf_op jit(solution)/shard_map/ppermute | solution.py:268
  62.9 1.5 %collective-permute-start.2 = (bf16[512,512]{1,0:T(8,128)(2,1)S(1)}, bf16[512,512]{1,0:T(8,128)(2,1)}, u32[]{:S(2)}, u32[]{:S(2)}) collective-permute-start(bf16[512,512]{1,0:T(8,128)(2,1)S(1)} %get-tuple-element.28), channel_id=1, source_target_pairs={{0,0},{1,1},{2,16},{3,17},{16,2},{17,3},{18,18},{19,19},{36,36},{3... | collective-permute-start | bytes 1572872 | tf_op jit(solution)/shard_map/ppermute | solution.py:268
  64.4 1.5 %collective-permute-start.6 = (bf16[512,512]{1,0:T(8,128)(2,1)}, bf16[512,512]{1,0:T(8,128)(2,1)}, u32[]{:S(2)}, u32[]{:S(2)}) collective-permute-start(bf16[512,512]{1,0:T(8,128)(2,1)} %get-tuple-element.33), channel_id=1, source_target_pairs={{0,1},{1,0},{2,17},{3,16},{16,3},{17,2},{18,19},{19,18},{36,37},{3... | collective-permute-start | bytes 1572872 | tf_op jit(solution)/shard_map/ppermute | solution.py:268
  65.8 4.9 %collective-permute-done.refs_0_ = bf16[512,512]{1,0:T(8,128)(2,1)S(1)} collective-permute-done((bf16[512,512]{1,0:T(8,128)(2,1)S(1)}, bf16[512,512]{1,0:T(8,128)(2,1)S(1)}, u32[]{:S(2)}, u32[]{:S(2)}) %collective-permute-start) | collective-permute-done | bytes 524320 | tf_op jit(solution)/shard_map/ppermute | solution.py:268
  70.8 1.3 %collective-permute-start.1 = (bf16[512,512]{1,0:T(8,128)(2,1)S(1)}, bf16[512,512]{1,0:T(8,128)(2,1)}, u32[]{:S(2)}, u32[]{:S(2)}) collective-permute-start(bf16[512,512]{1,0:T(8,128)(2,1)S(1)} %collective-permute-done.refs_0_), channel_id=1, source_target_pairs={{72,64},{73,65},{74,80},{75,81},{88,66},{89,67},{90,82},{91,83},{1... | collective-permute-start | bytes 1572872 | tf_op jit(solution)/shard_map/ppermute | solution.py:268
  72.1 6.7 %collective-permute-done.3.refs_3_ = bf16[256,512]{1,0:T(8,128)(2,1)S(1)} collective-permute-done((bf16[256,512]{1,0:T(8,128)(2,1)S(1)}, bf16[256,512]{1,0:T(8,128)(2,1)S(1)}, u32[]{:S(2)}, u32[]{:S(2)}) %collective-permute-start.3) | collective-permute-done | bytes 262176 | tf_op jit(solution)/shard_map/ppermute | solution.py:268
  78.8 1.3 %collective-permute-start.5 = (bf16[256,512]{1,0:T(8,128)(2,1)S(1)}, bf16[256,512]{1,0:T(8,128)(2,1)S(1)}, u32[]{:S(2)}, u32[]{:S(2)}) collective-permute-start(bf16[256,512]{1,0:T(8,128)(2,1)S(1)} %collective-permute-done.4.refs_4_), channel_id=1, source_target_pairs={{72,64},{73,65},{74,80},{75,81},{88,66},{89,67},{90,82},{91,83},{1... | collective-permute-start | bytes 786440 | tf_op jit(solution)/shard_map/ppermute | solution.py:268
  80.1 0.1 copy.23.col_ref
  80.2 14.1 %collective-permute-done.5.refs_5_ = bf16[256,512]{1,0:T(8,128)(2,1)S(1)} collective-permute-done((bf16[256,512]{1,0:T(8,128)(2,1)S(1)}, bf16[256,512]{1,0:T(8,128)(2,1)S(1)}, u32[]{:S(2)}, u32[]{:S(2)}) %collective-permute-start.5) | collective-permute-done | bytes 262176 | tf_op jit(solution)/shard_map/ppermute | solution.py:268
  94.4 0.0 collective-permute-done.6.refs_6_
  94.4 0.0 collective-permute-done.2.refs_2_
  94.4 0.0 collective-permute-done.1.refs_1_
  94.4 5.9 %finish.1 = (f32[2,512,512]{2,1,0:T(8,128)}, bf16[2,512,512]{2,1,0:T(8,128)(2,1)}) custom-call(s32[6]{0:T(128)S(1)} %stack.19.ids, f32[512,512]{1,0:T(8,128)} %ladder.2.part_a, f32[512,512]{1,0:T(8,128)} %ladder.3.part_b, bf16[2,512,512]{2,1,0:T(8,128)(2,1)} %bitcast.22, bf16[2,512,512]{2,1,0:T(8,128)(2,1)} %bitcast.28, f32[512,1]{1,0:T(8,128)S(1)} %copy.23.col_ref, ...), custom_call_target="tpu_custom_call" | custom-call | flops 10485760 | bytes 7340032 | tf_op jit(solution)/shard_map/finish/pallas_call | solution.py:194
  (19 shorter events, 0.1 us)
Async XLA Ops:
  0.6 7.4 %copy-start.7 = (s32[16]{0:T(128)S(1)}, s32[16]{0:T(128)}, u32[]{:S(2)}) copy-start(s32[16]{0:T(128)} %param.19) | copy-start | bytes 196
  0.6 7.5 %copy-start.6 = (s32[16,6]{0,1:T(8,128)S(1)}, s32[16,6]{0,1:T(8,128)}, u32[]{:S(2)}) copy-start(s32[16,6]{0,1:T(8,128)} %param.18) | copy-start | bytes 1156
  0.7 7.6 %copy-start.5 = (f32[16,16]{1,0:T(8,128)S(1)}, f32[16,16]{1,0:T(8,128)}, u32[]{:S(2)}) copy-start(f32[16,16]{1,0:T(8,128)} %param.17) | copy-start | bytes 3076
  0.7 24.5 %all-to-all-start = ((bf16[16,64,512]{2,1,0:T(8,128)(2,1)}), bf16[16,64,512]{2,1,0:T(8,128)(2,1)S(1)}, u32[]{:S(2)}, u32[]{:S(2)}) async-start(bf16[16,64,512]{2,1,0:T(8,128)(2,1)} %bitcast.25), calls=%async_computation | async-start | bytes 2097152 | tf_op jit(solution)/shard_map/all_to_all | solution.py:279
  27.1 23.7 %all-to-all-start.1 = ((bf16[16,64,512]{2,1,0:T(8,128)(2,1)}), bf16[16,64,512]{2,1,0:T(8,128)(2,1)S(1)}, u32[]{:S(2)}, u32[]{:S(2)}) async-start(bf16[16,64,512]{2,1,0:T(8,128)(2,1)} %mix.1), calls=%async_computation.1 | async-start | bytes 2097152 | tf_op jit(solution)/shard_map/all_to_all | solution.py:288
  34.3 16.4 %copy-start.1 = (f32[512,512]{1,0:T(8,128)S(1)}, f32[512,512]{1,0:T(8,128)}, u32[]{:S(2)}) copy-start(f32[512,512]{1,0:T(8,128)} %ladder.2.part_a) | copy-start | bytes 3145732
  34.3 45.7 %copy-start.3 = (f32[512]{0:T(512)S(1)}, f32[512]{0:T(512)}, u32[]{:S(2)}) copy-start(f32[512]{0:T(512)} %param.15) | copy-start | bytes 6148
  50.8 43.6 %copy-start.4 = (f32[16]{0:T(128)S(1)}, f32[16]{0:T(128)}, u32[]{:S(2)}) copy-start(f32[16]{0:T(128)} %occ_ref.1) | copy-start | bytes 196
  50.8 43.6 %copy-start = (bf16[16,64,512]{2,1,0:T(8,128)(2,1)}, bf16[16,64,512]{2,1,0:T(8,128)(2,1)S(1)}, u32[]{:S(2)}) copy-start(bf16[16,64,512]{2,1,0:T(8,128)(2,1)S(1)} %all-to-all-done.1) | copy-start | bytes 3145732
  50.8 1.6 %copy-start.2 = (f32[512,512]{1,0:T(8,128)S(1)}, f32[512,512]{1,0:T(8,128)}, u32[]{:S(2)}) copy-start(f32[512,512]{1,0:T(8,128)} %ladder.3.part_b) | copy-start | bytes 3145732
  53.4 17.4 %collective-permute-start = (bf16[512,512]{1,0:T(8,128)(2,1)S(1)}, bf16[512,512]{1,0:T(8,128)(2,1)S(1)}, u32[]{:S(2)}, u32[]{:S(2)}) collective-permute-start(bf16[512,512]{1,0:T(8,128)(2,1)S(1)} %get-tuple-element.28), channel_id=1, source_target_pairs={{4,32},{5,33},{6,48},{7,49},{20,34},{21,35},{22,50},{23,51},{8,72}... | collective-permute-start | bytes 1572872 | tf_op jit(solution)/shard_map/ppermute | solution.py:268
  58.5 20.2 %collective-permute-start.3 = (bf16[256,512]{1,0:T(8,128)(2,1)S(1)}, bf16[256,512]{1,0:T(8,128)(2,1)S(1)}, u32[]{:S(2)}, u32[]{:S(2)}) collective-permute-start(bf16[256,512]{1,0:T(8,128)(2,1)S(1)} %get-tuple-element.29), channel_id=1, source_target_pairs={{4,33},{5,32},{6,49},{7,48},{20,35},{21,34},{22,51},{23,50},{8,65}... | collective-permute-start | bytes 786440 | tf_op jit(solution)/shard_map/ppermute | solution.py:268
  61.6 17.2 %collective-permute-start.4 = (bf16[256,512]{1,0:T(8,128)(2,1)S(1)}, bf16[256,512]{1,0:T(8,128)(2,1)S(1)}, u32[]{:S(2)}, u32[]{:S(2)}) collective-permute-start(bf16[256,512]{1,0:T(8,128)(2,1)S(1)} %get-tuple-element.30), channel_id=1, source_target_pairs={{4,33},{5,32},{6,49},{7,48},{20,35},{21,34},{22,51},{23,50},{8,73}... | collective-permute-start | bytes 786440 | tf_op jit(solution)/shard_map/ppermute | solution.py:268
  62.9 31.5 %collective-permute-start.2 = (bf16[512,512]{1,0:T(8,128)(2,1)S(1)}, bf16[512,512]{1,0:T(8,128)(2,1)}, u32[]{:S(2)}, u32[]{:S(2)}) collective-permute-start(bf16[512,512]{1,0:T(8,128)(2,1)S(1)} %get-tuple-element.28), channel_id=1, source_target_pairs={{0,0},{1,1},{2,16},{3,17},{16,2},{17,3},{18,18},{19,19},{36,36},{3... | collective-permute-start | bytes 1572872 | tf_op jit(solution)/shard_map/ppermute | solution.py:268
  64.4 30.0 %collective-permute-start.6 = (bf16[512,512]{1,0:T(8,128)(2,1)}, bf16[512,512]{1,0:T(8,128)(2,1)}, u32[]{:S(2)}, u32[]{:S(2)}) collective-permute-start(bf16[512,512]{1,0:T(8,128)(2,1)} %get-tuple-element.33), channel_id=1, source_target_pairs={{0,1},{1,0},{2,17},{3,16},{16,3},{17,2},{18,19},{19,18},{36,37},{3... | collective-permute-start | bytes 1572872 | tf_op jit(solution)/shard_map/ppermute | solution.py:268
  70.8 23.6 %collective-permute-start.1 = (bf16[512,512]{1,0:T(8,128)(2,1)S(1)}, bf16[512,512]{1,0:T(8,128)(2,1)}, u32[]{:S(2)}, u32[]{:S(2)}) collective-permute-start(bf16[512,512]{1,0:T(8,128)(2,1)S(1)} %collective-permute-done.refs_0_), channel_id=1, source_target_pairs={{72,64},{73,65},{74,80},{75,81},{88,66},{89,67},{90,82},{91,83},{1... | collective-permute-start | bytes 1572872 | tf_op jit(solution)/shard_map/ppermute | solution.py:268
  78.8 15.6 %collective-permute-start.5 = (bf16[256,512]{1,0:T(8,128)(2,1)S(1)}, bf16[256,512]{1,0:T(8,128)(2,1)S(1)}, u32[]{:S(2)}, u32[]{:S(2)}) collective-permute-start(bf16[256,512]{1,0:T(8,128)(2,1)S(1)} %collective-permute-done.4.refs_4_), channel_id=1, source_target_pairs={{72,64},{73,65},{74,80},{75,81},{88,66},{89,67},{90,82},{91,83},{1... | collective-permute-start | bytes 786440 | tf_op jit(solution)/shard_map/ppermute | solution.py:268

commit v12 on v11

--- a/solution.py
+++ b/solution.py
@@ -158,7 +158,7 @@
 
     def finish(part_ref, first, mirror):
         half = part_ref[...] - sum_ref[...].astype(F32)
-        residual = half + mirror.astype(F32).T
+        residual = half + mirror.T.astype(F32)
         denominator = col_ref[...] + row_ref[...] - occ_ref[first] - occ_ref[ids[4]]
         res_ref[...] = residual
         new_ref[...] = (amp_ref[...].astype(F32) - residual / denominator).astype(BF16)

time: 101 us -> 101 us (level)
  no operation moved by 1% of the time
where the time goes in v12:
time: 101 us; the launch traced here: 100 us
  Pallas kernels  41.5 us (41%)
  starting transfers between devices  29.6 us (29%)
  waiting for transfers between devices  25.8 us (26%)
  local copies, waits for them, and re-layouts  2.28 us (2%)
    pallas_call x2, Pallas kernels, ladder(): pl.pallas_call(ladder_kernel, out_shape=jax.ShapeDtypeStruct((virt, virt)...  32.7 us
    ppermute x7, waiting for transfers between devices, send(): return lax.ppermute(array, AXES, pairs)  25.8 us
    ppermute x7, starting transfers between devices, send(): return lax.ppermute(array, AXES, pairs)  15 us
    all_to_all x1, starting transfers between devices, shards(): slices = lax.all_to_all(slices, 'occj', 0, 0, tiled=True)  7.38 us
    all_to_all x1, starting transfers between devices, shards(): sums = lax.all_to_all(sums, 'occj', 0, 0, tiled=True)  7.23 us
    pallas_call x1, Pallas kernels, finish(): pl.pallas_call(finish_kernel, out_shape=[jax.ShapeDtypeStruct(amps.shape,...  5.87 us
  transfers between devices with their start and end apart: 9, of which 3 were waited for; matrix products, arithmetic and copies ran while one was open for 1% of the time, Pallas kernels for 33%

profile of v12, /device:TPU:36, one launch (start us, length us, event | category | flops | bytes accessed | tf_op | source)
XLA Modules:
  0.0 100.3 jit_solution(15468074968402080681)
XLA Ops:
  0.7 7.4 %all-to-all-start = ((bf16[16,64,512]{2,1,0:T(8,128)(2,1)}), bf16[16,64,512]{2,1,0:T(8,128)(2,1)S(1)}, u32[]{:S(2)}, u32[]{:S(2)}) async-start(bf16[16,64,512]{2,1,0:T(8,128)(2,1)} %bitcast.25), calls=%async_computation | async-start | bytes 2097152 | tf_op jit(solution)/shard_map/all_to_all | solution.py:279
  8.1 0.1 convert_reduce_fusion
  8.2 0.1 copy.21
  8.3 0.1 broadcast_in_dim.7
  8.4 0.1 reshape.78
  8.5 0.1 copy.22
  8.7 0.1 compare_select_fusion.w_ref
  8.8 0.1 stack.19.ids
  8.9 16.3 %ladder.2.part_a = f32[512,512]{1,0:T(8,128)} custom-call(s32[1]{0:T(128)} %bitcast.1.slot, bf16[2,512,512]{2,1,0:T(8,128)(2,1)} %bitcast.26, bf16[2,512,512]{2,1,0:T(8,128)(2,1)} %bitcast.31, bf16[512,2048]{1,0:T(8,128)(2,1)} %x_ref.3, bf16[2048,2048]{1,0:T(8,128)(2,1)} %core_ref.3, bf16[512,512]{1,0:T(8,128)(2,1)} %fock_ref.3), custom_call_target="tpu_custom_call" | custom-call | flops 11005853696 | bytes 12582912 | tf_op jit(solution)/shard_map/ladder/pallas_call | solution.py:92
  25.1 0.0 all-to-all-done.in_ref
  25.1 2.0 %mix.1 = bf16[16,64,512]{2,1,0:T(8,128)(2,1)} custom-call(f32[256,256]{1,0:T(8,128)S(1)} %compare_select_fusion.w_ref, bf16[16,64,512]{2,1,0:T(8,128)(2,1)S(1)} %all-to-all-done.in_ref), custom_call_target="tpu_custom_call" | custom-call | flops 1000000000 | bytes 2097152 | tf_op jit(solution)/shard_map/mix/pallas_call | solution.py:50
  27.1 7.2 %all-to-all-start.1 = ((bf16[16,64,512]{2,1,0:T(8,128)(2,1)}), bf16[16,64,512]{2,1,0:T(8,128)(2,1)S(1)}, u32[]{:S(2)}, u32[]{:S(2)}) async-start(bf16[16,64,512]{2,1,0:T(8,128)(2,1)} %mix.1), calls=%async_computation.1 | async-start | bytes 2097152 | tf_op jit(solution)/shard_map/all_to_all | solution.py:288
  34.3 0.0 copy-start.3
  34.4 16.4 %ladder.3.part_b = f32[512,512]{1,0:T(8,128)} custom-call(s32[1]{0:T(128)} %sub.13.slot, bf16[2,512,512]{2,1,0:T(8,128)(2,1)} %bitcast.27, bf16[2,512,512]{2,1,0:T(8,128)(2,1)} %bitcast.32, bf16[512,2048]{1,0:T(8,128)(2,1)} %x_ref.3, bf16[2048,2048]{1,0:T(8,128)(2,1)} %core_ref.3, bf16[512,512]{1,0:T(8,128)(2,1)} %fock_ref.3), custom_call_target="tpu_custom_call" | custom-call | flops 11005853696 | bytes 12582912 | tf_op jit(solution)/shard_map/ladder/pallas_call | solution.py:92
  50.8 0.0 all-to-all-done.1
  50.8 1.6 %copy-done.2 = f32[512,512]{1,0:T(8,128)S(1)} copy-done((f32[512,512]{1,0:T(8,128)S(1)}, f32[512,512]{1,0:T(8,128)}, u32[]{:S(2)}) %copy-start.2) | copy-done | bytes 1048600
  52.4 1.0 %half.1 = (bf16[512,512]{1,0:T(8,128)(2,1)S(1)}, bf16[512,512]{1,0:T(8,128)(2,1)}, bf16[256,512]{1,0:T(8,128)(2,1)S(1)}, bf16[256,512]{1,0:T(8,128)(2,1)S(1)}) custom-call(s32[1]{0:T(128)} %bitcast.1.slot, f32[512,512]{1,0:T(8,128)S(1)} %copy-done.1, f32[512,512]{1,0:T(8,128)S(1)} %copy-done.2, bf16[2,512,512]{2,1,0:T(8,128)(2,1)S(1)} %bitcast.21), custom_call_target="tpu_custom_call" | custom-call | bytes 4194304 | tf_op jit(solution)/shard_map/half/pallas_call | solution.py:137
  53.4 5.1 %collective-permute-start = (bf16[512,512]{1,0:T(8,128)(2,1)S(1)}, bf16[512,512]{1,0:T(8,128)(2,1)S(1)}, u32[]{:S(2)}, u32[]{:S(2)}) collective-permute-start(bf16[512,512]{1,0:T(8,128)(2,1)S(1)} %get-tuple-element.28), channel_id=1, source_target_pairs={{4,32},{5,33},{6,48},{7,49},{20,34},{21,35},{22,50},{23,51},{8,72}... | collective-permute-start | bytes 1572872 | tf_op jit(solution)/shard_map/ppermute | solution.py:268
  58.5 3.1 %collective-permute-start.3 = (bf16[256,512]{1,0:T(8,128)(2,1)S(1)}, bf16[256,512]{1,0:T(8,128)(2,1)S(1)}, u32[]{:S(2)}, u32[]{:S(2)}) collective-permute-start(bf16[256,512]{1,0:T(8,128)(2,1)S(1)} %get-tuple-element.29), channel_id=1, source_target_pairs={{4,33},{5,32},{6,49},{7,48},{20,35},{21,34},{22,51},{23,50},{8,65}... | collective-permute-start | bytes 786440 | tf_op jit(solution)/shard_map/ppermute | solution.py:268
  61.6 1.3 %collective-permute-start.4 = (bf16[256,512]{1,0:T(8,128)(2,1)S(1)}, bf16[256,512]{1,0:T(8,128)(2,1)S(1)}, u32[]{:S(2)}, u32[]{:S(2)}) collective-permute-start(bf16[256,512]{1,0:T(8,128)(2,1)S(1)} %get-tuple-element.30), channel_id=1, source_target_pairs={{4,33},{5,32},{6,49},{7,48},{20,35},{21,34},{22,51},{23,50},{8,73}... | collective-permute-start | bytes 786440 | tf_op jit(solution)/shard_map/ppermute | solution.py:268
  62.9 1.5 %collective-permute-start.2 = (bf16[512,512]{1,0:T(8,128)(2,1)S(1)}, bf16[512,512]{1,0:T(8,128)(2,1)}, u32[]{:S(2)}, u32[]{:S(2)}) collective-permute-start(bf16[512,512]{1,0:T(8,128)(2,1)S(1)} %get-tuple-element.28), channel_id=1, source_target_pairs={{0,0},{1,1},{2,16},{3,17},{16,2},{17,3},{18,18},{19,19},{36,36},{3... | collective-permute-start | bytes 1572872 | tf_op jit(solution)/shard_map/ppermute | solution.py:268
  64.4 1.5 %collective-permute-start.6 = (bf16[512,512]{1,0:T(8,128)(2,1)}, bf16[512,512]{1,0:T(8,128)(2,1)}, u32[]{:S(2)}, u32[]{:S(2)}) collective-permute-start(bf16[512,512]{1,0:T(8,128)(2,1)} %get-tuple-element.33), channel_id=1, source_target_pairs={{0,1},{1,0},{2,17},{3,16},{16,3},{17,2},{18,19},{19,18},{36,37},{3... | collective-permute-start | bytes 1572872 | tf_op jit(solution)/shard_map/ppermute | solution.py:268
  65.8 4.9 %collective-permute-done.refs_0_ = bf16[512,512]{1,0:T(8,128)(2,1)S(1)} collective-permute-done((bf16[512,512]{1,0:T(8,128)(2,1)S(1)}, bf16[512,512]{1,0:T(8,128)(2,1)S(1)}, u32[]{:S(2)}, u32[]{:S(2)}) %collective-permute-start) | collective-permute-done | bytes 524320 | tf_op jit(solution)/shard_map/ppermute | solution.py:268
  70.8 1.3 %collective-permute-start.1 = (bf16[512,512]{1,0:T(8,128)(2,1)S(1)}, bf16[512,512]{1,0:T(8,128)(2,1)}, u32[]{:S(2)}, u32[]{:S(2)}) collective-permute-start(bf16[512,512]{1,0:T(8,128)(2,1)S(1)} %collective-permute-done.refs_0_), channel_id=1, source_target_pairs={{72,64},{73,65},{74,80},{75,81},{88,66},{89,67},{90,82},{91,83},{1... | collective-permute-start | bytes 1572872 | tf_op jit(solution)/shard_map/ppermute | solution.py:268
  72.1 6.7 %collective-permute-done.3.refs_3_ = bf16[256,512]{1,0:T(8,128)(2,1)S(1)} collective-permute-done((bf16[256,512]{1,0:T(8,128)(2,1)S(1)}, bf16[256,512]{1,0:T(8,128)(2,1)S(1)}, u32[]{:S(2)}, u32[]{:S(2)}) %collective-permute-start.3) | collective-permute-done | bytes 262176 | tf_op jit(solution)/shard_map/ppermute | solution.py:268
  78.8 1.3 %collective-permute-start.5 = (bf16[256,512]{1,0:T(8,128)(2,1)S(1)}, bf16[256,512]{1,0:T(8,128)(2,1)S(1)}, u32[]{:S(2)}, u32[]{:S(2)}) collective-permute-start(bf16[256,512]{1,0:T(8,128)(2,1)S(1)} %collective-permute-done.4.refs_4_), channel_id=1, source_target_pairs={{72,64},{73,65},{74,80},{75,81},{88,66},{89,67},{90,82},{91,83},{1... | collective-permute-start | bytes 786440 | tf_op jit(solution)/shard_map/ppermute | solution.py:268
  80.1 0.1 copy.23.col_ref
  80.2 14.1 %collective-permute-done.5.refs_5_ = bf16[256,512]{1,0:T(8,128)(2,1)S(1)} collective-permute-done((bf16[256,512]{1,0:T(8,128)(2,1)S(1)}, bf16[256,512]{1,0:T(8,128)(2,1)S(1)}, u32[]{:S(2)}, u32[]{:S(2)}) %collective-permute-start.5) | collective-permute-done | bytes 262176 | tf_op jit(solution)/shard_map/ppermute | solution.py:268
  94.4 0.0 collective-permute-done.6.refs_6_
  94.4 0.0 collective-permute-done.2.refs_2_
  94.4 0.0 collective-permute-done.1.refs_1_
  94.4 5.9 %finish.1 = (f32[2,512,512]{2,1,0:T(8,128)}, bf16[2,512,512]{2,1,0:T(8,128)(2,1)}) custom-call(s32[6]{0:T(128)S(1)} %stack.19.ids, f32[512,512]{1,0:T(8,128)} %ladder.2.part_a, f32[512,512]{1,0:T(8,128)} %ladder.3.part_b, bf16[2,512,512]{2,1,0:T(8,128)(2,1)} %bitcast.22, bf16[2,512,512]{2,1,0:T(8,128)(2,1)} %bitcast.28, f32[512,1]{1,0:T(8,128)S(1)} %copy.23.col_ref, ...), custom_call_target="tpu_custom_call" | custom-call | flops 10485760 | bytes 7340032 | tf_op jit(solution)/shard_map/finish/pallas_call | solution.py:194
  (19 shorter events, 0.1 us)
Async XLA Ops:
  0.6 7.4 %copy-start.7 = (s32[16]{0:T(128)S(1)}, s32[16]{0:T(128)}, u32[]{:S(2)}) copy-start(s32[16]{0:T(128)} %param.19) | copy-start | bytes 196
  0.6 7.5 %copy-start.6 = (s32[16,6]{0,1:T(8,128)S(1)}, s32[16,6]{0,1:T(8,128)}, u32[]{:S(2)}) copy-start(s32[16,6]{0,1:T(8,128)} %param.18) | copy-start | bytes 1156
  0.7 7.6 %copy-start.5 = (f32[16,16]{1,0:T(8,128)S(1)}, f32[16,16]{1,0:T(8,128)}, u32[]{:S(2)}) copy-start(f32[16,16]{1,0:T(8,128)} %param.17) | copy-start | bytes 3076
  0.7 24.5 %all-to-all-start = ((bf16[16,64,512]{2,1,0:T(8,128)(2,1)}), bf16[16,64,512]{2,1,0:T(8,128)(2,1)S(1)}, u32[]{:S(2)}, u32[]{:S(2)}) async-start(bf16[16,64,512]{2,1,0:T(8,128)(2,1)} %bitcast.25), calls=%async_computation | async-start | bytes 2097152 | tf_op jit(solution)/shard_map/all_to_all | solution.py:279
  27.1 23.7 %all-to-all-start.1 = ((bf16[16,64,512]{2,1,0:T(8,128)(2,1)}), bf16[16,64,512]{2,1,0:T(8,128)(2,1)S(1)}, u32[]{:S(2)}, u32[]{:S(2)}) async-start(bf16[16,64,512]{2,1,0:T(8,128)(2,1)} %mix.1), calls=%async_computation.1 | async-start | bytes 2097152 | tf_op jit(solution)/shard_map/all_to_all | solution.py:288
  34.3 16.4 %copy-start.1 = (f32[512,512]{1,0:T(8,128)S(1)}, f32[512,512]{1,0:T(8,128)}, u32[]{:S(2)}) copy-start(f32[512,512]{1,0:T(8,128)} %ladder.2.part_a) | copy-start | bytes 3145732
  34.3 45.7 %copy-start.3 = (f32[512]{0:T(512)S(1)}, f32[512]{0:T(512)}, u32[]{:S(2)}) copy-start(f32[512]{0:T(512)} %param.15) | copy-start | bytes 6148
  50.8 43.6 %copy-start.4 = (f32[16]{0:T(128)S(1)}, f32[16]{0:T(128)}, u32[]{:S(2)}) copy-start(f32[16]{0:T(128)} %occ_ref.1) | copy-start | bytes 196
  50.8 43.6 %copy-start = (bf16[16,64,512]{2,1,0:T(8,128)(2,1)}, bf16[16,64,512]{2,1,0:T(8,128)(2,1)S(1)}, u32[]{:S(2)}) copy-start(bf16[16,64,512]{2,1,0:T(8,128)(2,1)S(1)} %all-to-all-done.1) | copy-start | bytes 3145732
  50.8 1.6 %copy-start.2 = (f32[512,512]{1,0:T(8,128)S(1)}, f32[512,512]{1,0:T(8,128)}, u32[]{:S(2)}) copy-start(f32[512,512]{1,0:T(8,128)} %ladder.3.part_b) | copy-start | bytes 3145732
  53.4 17.4 %collective-permute-start = (bf16[512,512]{1,0:T(8,128)(2,1)S(1)}, bf16[512,512]{1,0:T(8,128)(2,1)S(1)}, u32[]{:S(2)}, u32[]{:S(2)}) collective-permute-start(bf16[512,512]{1,0:T(8,128)(2,1)S(1)} %get-tuple-element.28), channel_id=1, source_target_pairs={{4,32},{5,33},{6,48},{7,49},{20,34},{21,35},{22,50},{23,51},{8,72}... | collective-permute-start | bytes 1572872 | tf_op jit(solution)/shard_map/ppermute | solution.py:268
  58.5 20.2 %collective-permute-start.3 = (bf16[256,512]{1,0:T(8,128)(2,1)S(1)}, bf16[256,512]{1,0:T(8,128)(2,1)S(1)}, u32[]{:S(2)}, u32[]{:S(2)}) collective-permute-start(bf16[256,512]{1,0:T(8,128)(2,1)S(1)} %get-tuple-element.29), channel_id=1, source_target_pairs={{4,33},{5,32},{6,49},{7,48},{20,35},{21,34},{22,51},{23,50},{8,65}... | collective-permute-start | bytes 786440 | tf_op jit(solution)/shard_map/ppermute | solution.py:268
  61.6 17.2 %collective-permute-start.4 = (bf16[256,512]{1,0:T(8,128)(2,1)S(1)}, bf16[256,512]{1,0:T(8,128)(2,1)S(1)}, u32[]{:S(2)}, u32[]{:S(2)}) collective-permute-start(bf16[256,512]{1,0:T(8,128)(2,1)S(1)} %get-tuple-element.30), channel_id=1, source_target_pairs={{4,33},{5,32},{6,49},{7,48},{20,35},{21,34},{22,51},{23,50},{8,73}... | collective-permute-start | bytes 786440 | tf_op jit(solution)/shard_map/ppermute | solution.py:268
  62.9 31.5 %collective-permute-start.2 = (bf16[512,512]{1,0:T(8,128)(2,1)S(1)}, bf16[512,512]{1,0:T(8,128)(2,1)}, u32[]{:S(2)}, u32[]{:S(2)}) collective-permute-start(bf16[512,512]{1,0:T(8,128)(2,1)S(1)} %get-tuple-element.28), channel_id=1, source_target_pairs={{0,0},{1,1},{2,16},{3,17},{16,2},{17,3},{18,18},{19,19},{36,36},{3... | collective-permute-start | bytes 1572872 | tf_op jit(solution)/shard_map/ppermute | solution.py:268
  64.4 30.0 %collective-permute-start.6 = (bf16[512,512]{1,0:T(8,128)(2,1)}, bf16[512,512]{1,0:T(8,128)(2,1)}, u32[]{:S(2)}, u32[]{:S(2)}) collective-permute-start(bf16[512,512]{1,0:T(8,128)(2,1)} %get-tuple-element.33), channel_id=1, source_target_pairs={{0,1},{1,0},{2,17},{3,16},{16,3},{17,2},{18,19},{19,18},{36,37},{3... | collective-permute-start | bytes 1572872 | tf_op jit(solution)/shard_map/ppermute | solution.py:268
  70.8 23.6 %collective-permute-start.1 = (bf16[512,512]{1,0:T(8,128)(2,1)S(1)}, bf16[512,512]{1,0:T(8,128)(2,1)}, u32[]{:S(2)}, u32[]{:S(2)}) collective-permute-start(bf16[512,512]{1,0:T(8,128)(2,1)S(1)} %collective-permute-done.refs_0_), channel_id=1, source_target_pairs={{72,64},{73,65},{74,80},{75,81},{88,66},{89,67},{90,82},{91,83},{1... | collective-permute-start | bytes 1572872 | tf_op jit(solution)/shard_map/ppermute | solution.py:268
  78.8 15.6 %collective-permute-start.5 = (bf16[256,512]{1,0:T(8,128)(2,1)S(1)}, bf16[256,512]{1,0:T(8,128)(2,1)S(1)}, u32[]{:S(2)}, u32[]{:S(2)}) collective-permute-start(bf16[256,512]{1,0:T(8,128)(2,1)S(1)} %collective-permute-done.4.refs_4_), channel_id=1, source_target_pairs={{72,64},{73,65},{74,80},{75,81},{88,66},{89,67},{90,82},{91,83},{1... | collective-permute-start | bytes 786440 | tf_op jit(solution)/shard_map/ppermute | solution.py:268

commit v13 on v12

--- a/solution.py
+++ b/solution.py
@@ -188,8 +188,12 @@
     def late(g, s):
         return jnp.maximum(g - 2, 0)
 
-    def across(m, at):
-        return pl.BlockSpec((m.shape[0], rows), lambda g, s: (0, at(g, s)))
+    def across(m, at, *kinds):
+        def block(g, s):
+            used = functools.reduce(jnp.logical_or, [s[5] == k for k in kinds])
+            return (0, jnp.where(used, at(g, s), 0))
+
+        return pl.BlockSpec((m.shape[0], rows), block)
 
     return pl.pallas_call(
         finish_kernel,
@@ -209,8 +213,9 @@
                 whole((1, virt)),
                 pl.BlockSpec(memory_space=pltpu.SMEM),
             ]
-            + [across(m, early) for m in mirror_a]
-            + [across(m, late) for m in mirror_b],
+            + [across(m, early, k) for m, k in zip(mirror_a, range(3))]
+            + [across(mirror_b[0], late, 0, 1)]
+            + [across(m, late, k) for m, k in zip(mirror_b[1:], range(3))],
             out_specs=[strip, strip],
         ),
         compiler_params=params(52, dimension_semantics=("arbitrary",)),

time: 101 us -> 101 us (level)
  no operation moved by 1% of the time
where the time goes in v13:
time: 101 us; the launch traced here: 100 us
  Pallas kernels  41.5 us (41%)
  starting transfers between devices  29.6 us (29%)
  waiting for transfers between devices  25.8 us (26%)
  local copies, waits for them, and re-layouts  2.28 us (2%)
    pallas_call x2, Pallas kernels, ladder(): pl.pallas_call(ladder_kernel, out_shape=jax.ShapeDtypeStruct((virt, virt)...  32.7 us
    ppermute x7, waiting for transfers between devices, send(): return lax.ppermute(array, AXES, pairs)  25.8 us
    ppermute x7, starting transfers between devices, send(): return lax.ppermute(array, AXES, pairs)  15 us
    all_to_all x1, starting transfers between devices, shards(): slices = lax.all_to_all(slices, 'occj', 0, 0, tiled=True)  7.38 us
    all_to_all x1, starting transfers between devices, shards(): sums = lax.all_to_all(sums, 'occj', 0, 0, tiled=True)  7.23 us
    pallas_call x1, Pallas kernels, finish(): pl.pallas_call(finish_kernel, out_shape=[jax.ShapeDtypeStruct(amps.shape,...  5.85 us
  transfers between devices with their start and end apart: 9, of which 3 were waited for; matrix products, arithmetic and copies ran while one was open for 1% of the time, Pallas kernels for 33%

profile of v13, /device:TPU:36, one launch (start us, length us, event | category | flops | bytes accessed | tf_op | source)
XLA Modules:
  0.0 100.3 jit_solution(15136419038864487982)
XLA Ops:
  0.7 7.4 %all-to-all-start = ((bf16[16,64,512]{2,1,0:T(8,128)(2,1)}), bf16[16,64,512]{2,1,0:T(8,128)(2,1)S(1)}, u32[]{:S(2)}, u32[]{:S(2)}) async-start(bf16[16,64,512]{2,1,0:T(8,128)(2,1)} %bitcast.25), calls=%async_computation | async-start | bytes 2097152 | tf_op jit(solution)/shard_map/all_to_all | solution.py:284
  8.1 0.1 convert_reduce_fusion
  8.2 0.1 copy.21
  8.3 0.1 broadcast_in_dim.7
  8.4 0.1 reshape.78
  8.5 0.1 copy.22
  8.7 0.1 compare_select_fusion.w_ref
  8.8 0.1 stack.19.ids
  8.9 16.3 %ladder.2.part_a = f32[512,512]{1,0:T(8,128)} custom-call(s32[1]{0:T(128)} %bitcast.1.slot, bf16[2,512,512]{2,1,0:T(8,128)(2,1)} %bitcast.26, bf16[2,512,512]{2,1,0:T(8,128)(2,1)} %bitcast.31, bf16[512,2048]{1,0:T(8,128)(2,1)} %x_ref.3, bf16[2048,2048]{1,0:T(8,128)(2,1)} %core_ref.3, bf16[512,512]{1,0:T(8,128)(2,1)} %fock_ref.3), custom_call_target="tpu_custom_call" | custom-call | flops 11005853696 | bytes 12582912 | tf_op jit(solution)/shard_map/ladder/pallas_call | solution.py:92
  25.1 0.0 all-to-all-done.in_ref
  25.1 2.0 %mix.1 = bf16[16,64,512]{2,1,0:T(8,128)(2,1)} custom-call(f32[256,256]{1,0:T(8,128)S(1)} %compare_select_fusion.w_ref, bf16[16,64,512]{2,1,0:T(8,128)(2,1)S(1)} %all-to-all-done.in_ref), custom_call_target="tpu_custom_call" | custom-call | flops 1000000000 | bytes 2097152 | tf_op jit(solution)/shard_map/mix/pallas_call | solution.py:50
  27.1 7.2 %all-to-all-start.1 = ((bf16[16,64,512]{2,1,0:T(8,128)(2,1)}), bf16[16,64,512]{2,1,0:T(8,128)(2,1)S(1)}, u32[]{:S(2)}, u32[]{:S(2)}) async-start(bf16[16,64,512]{2,1,0:T(8,128)(2,1)} %mix.1), calls=%async_computation.1 | async-start | bytes 2097152 | tf_op jit(solution)/shard_map/all_to_all | solution.py:293
  34.3 0.0 copy-start.3
  34.4 16.4 %ladder.3.part_b = f32[512,512]{1,0:T(8,128)} custom-call(s32[1]{0:T(128)} %sub.13.slot, bf16[2,512,512]{2,1,0:T(8,128)(2,1)} %bitcast.27, bf16[2,512,512]{2,1,0:T(8,128)(2,1)} %bitcast.32, bf16[512,2048]{1,0:T(8,128)(2,1)} %x_ref.3, bf16[2048,2048]{1,0:T(8,128)(2,1)} %core_ref.3, bf16[512,512]{1,0:T(8,128)(2,1)} %fock_ref.3), custom_call_target="tpu_custom_call" | custom-call | flops 11005853696 | bytes 12582912 | tf_op jit(solution)/shard_map/ladder/pallas_call | solution.py:92
  50.8 0.0 all-to-all-done.1
  50.8 1.6 %copy-done.2 = f32[512,512]{1,0:T(8,128)S(1)} copy-done((f32[512,512]{1,0:T(8,128)S(1)}, f32[512,512]{1,0:T(8,128)}, u32[]{:S(2)}) %copy-start.2) | copy-done | bytes 1048600
  52.4 1.0 %half.1 = (bf16[512,512]{1,0:T(8,128)(2,1)S(1)}, bf16[512,512]{1,0:T(8,128)(2,1)}, bf16[256,512]{1,0:T(8,128)(2,1)S(1)}, bf16[256,512]{1,0:T(8,128)(2,1)S(1)}) custom-call(s32[1]{0:T(128)} %bitcast.1.slot, f32[512,512]{1,0:T(8,128)S(1)} %copy-done.1, f32[512,512]{1,0:T(8,128)S(1)} %copy-done.2, bf16[2,512,512]{2,1,0:T(8,128)(2,1)S(1)} %bitcast.21), custom_call_target="tpu_custom_call" | custom-call | bytes 4194304 | tf_op jit(solution)/shard_map/half/pallas_call | solution.py:137
  53.4 5.1 %collective-permute-start = (bf16[512,512]{1,0:T(8,128)(2,1)S(1)}, bf16[512,512]{1,0:T(8,128)(2,1)S(1)}, u32[]{:S(2)}, u32[]{:S(2)}) collective-permute-start(bf16[512,512]{1,0:T(8,128)(2,1)S(1)} %get-tuple-element.28), channel_id=1, source_target_pairs={{4,32},{5,33},{6,48},{7,49},{20,34},{21,35},{22,50},{23,51},{8,72}... | collective-permute-start | bytes 1572872 | tf_op jit(solution)/shard_map/ppermute | solution.py:273
  58.5 3.1 %collective-permute-start.3 = (bf16[256,512]{1,0:T(8,128)(2,1)S(1)}, bf16[256,512]{1,0:T(8,128)(2,1)S(1)}, u32[]{:S(2)}, u32[]{:S(2)}) collective-permute-start(bf16[256,512]{1,0:T(8,128)(2,1)S(1)} %get-tuple-element.29), channel_id=1, source_target_pairs={{4,33},{5,32},{6,49},{7,48},{20,35},{21,34},{22,51},{23,50},{8,65}... | collective-permute-start | bytes 786440 | tf_op jit(solution)/shard_map/ppermute | solution.py:273
  61.6 1.3 %collective-permute-start.4 = (bf16[256,512]{1,0:T(8,128)(2,1)S(1)}, bf16[256,512]{1,0:T(8,128)(2,1)S(1)}, u32[]{:S(2)}, u32[]{:S(2)}) collective-permute-start(bf16[256,512]{1,0:T(8,128)(2,1)S(1)} %get-tuple-element.30), channel_id=1, source_target_pairs={{4,33},{5,32},{6,49},{7,48},{20,35},{21,34},{22,51},{23,50},{8,73}... | collective-permute-start | bytes 786440 | tf_op jit(solution)/shard_map/ppermute | solution.py:273
  62.9 1.5 %collective-permute-start.2 = (bf16[512,512]{1,0:T(8,128)(2,1)S(1)}, bf16[512,512]{1,0:T(8,128)(2,1)}, u32[]{:S(2)}, u32[]{:S(2)}) collective-permute-start(bf16[512,512]{1,0:T(8,128)(2,1)S(1)} %get-tuple-element.28), channel_id=1, source_target_pairs={{0,0},{1,1},{2,16},{3,17},{16,2},{17,3},{18,18},{19,19},{36,36},{3... | collective-permute-start | bytes 1572872 | tf_op jit(solution)/shard_map/ppermute | solution.py:273
  64.4 1.5 %collective-permute-start.6 = (bf16[512,512]{1,0:T(8,128)(2,1)}, bf16[512,512]{1,0:T(8,128)(2,1)}, u32[]{:S(2)}, u32[]{:S(2)}) collective-permute-start(bf16[512,512]{1,0:T(8,128)(2,1)} %get-tuple-element.33), channel_id=1, source_target_pairs={{0,1},{1,0},{2,17},{3,16},{16,3},{17,2},{18,19},{19,18},{36,37},{3... | collective-permute-start | bytes 1572872 | tf_op jit(solution)/shard_map/ppermute | solution.py:273
  65.8 4.9 %collective-permute-done.refs_0_ = bf16[512,512]{1,0:T(8,128)(2,1)S(1)} collective-permute-done((bf16[512,512]{1,0:T(8,128)(2,1)S(1)}, bf16[512,512]{1,0:T(8,128)(2,1)S(1)}, u32[]{:S(2)}, u32[]{:S(2)}) %collective-permute-start) | collective-permute-done | bytes 524320 | tf_op jit(solution)/shard_map/ppermute | solution.py:273
  70.8 1.3 %collective-permute-start.1 = (bf16[512,512]{1,0:T(8,128)(2,1)S(1)}, bf16[512,512]{1,0:T(8,128)(2,1)}, u32[]{:S(2)}, u32[]{:S(2)}) collective-permute-start(bf16[512,512]{1,0:T(8,128)(2,1)S(1)} %collective-permute-done.refs_0_), channel_id=1, source_target_pairs={{72,64},{73,65},{74,80},{75,81},{88,66},{89,67},{90,82},{91,83},{1... | collective-permute-start | bytes 1572872 | tf_op jit(solution)/shard_map/ppermute | solution.py:273
  72.1 6.7 %collective-permute-done.3.refs_3_ = bf16[256,512]{1,0:T(8,128)(2,1)S(1)} collective-permute-done((bf16[256,512]{1,0:T(8,128)(2,1)S(1)}, bf16[256,512]{1,0:T(8,128)(2,1)S(1)}, u32[]{:S(2)}, u32[]{:S(2)}) %collective-permute-start.3) | collective-permute-done | bytes 262176 | tf_op jit(solution)/shard_map/ppermute | solution.py:273
  78.8 1.3 %collective-permute-start.5 = (bf16[256,512]{1,0:T(8,128)(2,1)S(1)}, bf16[256,512]{1,0:T(8,128)(2,1)S(1)}, u32[]{:S(2)}, u32[]{:S(2)}) collective-permute-start(bf16[256,512]{1,0:T(8,128)(2,1)S(1)} %collective-permute-done.4.refs_4_), channel_id=1, source_target_pairs={{72,64},{73,65},{74,80},{75,81},{88,66},{89,67},{90,82},{91,83},{1... | collective-permute-start | bytes 786440 | tf_op jit(solution)/shard_map/ppermute | solution.py:273
  80.1 0.1 copy.23.col_ref
  80.2 14.1 %collective-permute-done.5.refs_5_ = bf16[256,512]{1,0:T(8,128)(2,1)S(1)} collective-permute-done((bf16[256,512]{1,0:T(8,128)(2,1)S(1)}, bf16[256,512]{1,0:T(8,128)(2,1)S(1)}, u32[]{:S(2)}, u32[]{:S(2)}) %collective-permute-start.5) | collective-permute-done | bytes 262176 | tf_op jit(solution)/shard_map/ppermute | solution.py:273
  94.4 0.0 collective-permute-done.6.refs_6_
  94.4 0.0 collective-permute-done.2.refs_2_
  94.4 0.0 collective-permute-done.1.refs_1_
  94.4 5.9 %finish.1 = (f32[2,512,512]{2,1,0:T(8,128)}, bf16[2,512,512]{2,1,0:T(8,128)(2,1)}) custom-call(s32[6]{0:T(128)S(1)} %stack.19.ids, f32[512,512]{1,0:T(8,128)} %ladder.2.part_a, f32[512,512]{1,0:T(8,128)} %ladder.3.part_b, bf16[2,512,512]{2,1,0:T(8,128)(2,1)} %bitcast.22, bf16[2,512,512]{2,1,0:T(8,128)(2,1)} %bitcast.28, f32[512,1]{1,0:T(8,128)S(1)} %copy.23.col_ref, ...), custom_call_target="tpu_custom_call" | custom-call | flops 10485760 | bytes 7340032 | tf_op jit(solution)/shard_map/finish/pallas_call | solution.py:198
  (19 shorter events, 0.1 us)
Async XLA Ops:
  0.6 7.4 %copy-start.7 = (s32[16]{0:T(128)S(1)}, s32[16]{0:T(128)}, u32[]{:S(2)}) copy-start(s32[16]{0:T(128)} %param.19) | copy-start | bytes 196
  0.6 7.5 %copy-start.6 = (s32[16,6]{0,1:T(8,128)S(1)}, s32[16,6]{0,1:T(8,128)}, u32[]{:S(2)}) copy-start(s32[16,6]{0,1:T(8,128)} %param.18) | copy-start | bytes 1156
  0.7 7.6 %copy-start.5 = (f32[16,16]{1,0:T(8,128)S(1)}, f32[16,16]{1,0:T(8,128)}, u32[]{:S(2)}) copy-start(f32[16,16]{1,0:T(8,128)} %param.17) | copy-start | bytes 3076
  0.7 24.5 %all-to-all-start = ((bf16[16,64,512]{2,1,0:T(8,128)(2,1)}), bf16[16,64,512]{2,1,0:T(8,128)(2,1)S(1)}, u32[]{:S(2)}, u32[]{:S(2)}) async-start(bf16[16,64,512]{2,1,0:T(8,128)(2,1)} %bitcast.25), calls=%async_computation | async-start | bytes 2097152 | tf_op jit(solution)/shard_map/all_to_all | solution.py:284
  27.1 23.7 %all-to-all-start.1 = ((bf16[16,64,512]{2,1,0:T(8,128)(2,1)}), bf16[16,64,512]{2,1,0:T(8,128)(2,1)S(1)}, u32[]{:S(2)}, u32[]{:S(2)}) async-start(bf16[16,64,512]{2,1,0:T(8,128)(2,1)} %mix.1), calls=%async_computation.1 | async-start | bytes 2097152 | tf_op jit(solution)/shard_map/all_to_all | solution.py:293
  34.3 16.4 %copy-start.1 = (f32[512,512]{1,0:T(8,128)S(1)}, f32[512,512]{1,0:T(8,128)}, u32[]{:S(2)}) copy-start(f32[512,512]{1,0:T(8,128)} %ladder.2.part_a) | copy-start | bytes 3145732
  34.3 45.7 %copy-start.3 = (f32[512]{0:T(512)S(1)}, f32[512]{0:T(512)}, u32[]{:S(2)}) copy-start(f32[512]{0:T(512)} %param.15) | copy-start | bytes 6148
  50.8 43.6 %copy-start.4 = (f32[16]{0:T(128)S(1)}, f32[16]{0:T(128)}, u32[]{:S(2)}) copy-start(f32[16]{0:T(128)} %occ_ref.1) | copy-start | bytes 196
  50.8 43.6 %copy-start = (bf16[16,64,512]{2,1,0:T(8,128)(2,1)}, bf16[16,64,512]{2,1,0:T(8,128)(2,1)S(1)}, u32[]{:S(2)}) copy-start(bf16[16,64,512]{2,1,0:T(8,128)(2,1)S(1)} %all-to-all-done.1) | copy-start | bytes 3145732
  50.8 1.6 %copy-start.2 = (f32[512,512]{1,0:T(8,128)S(1)}, f32[512,512]{1,0:T(8,128)}, u32[]{:S(2)}) copy-start(f32[512,512]{1,0:T(8,128)} %ladder.3.part_b) | copy-start | bytes 3145732
  53.4 17.4 %collective-permute-start = (bf16[512,512]{1,0:T(8,128)(2,1)S(1)}, bf16[512,512]{1,0:T(8,128)(2,1)S(1)}, u32[]{:S(2)}, u32[]{:S(2)}) collective-permute-start(bf16[512,512]{1,0:T(8,128)(2,1)S(1)} %get-tuple-element.28), channel_id=1, source_target_pairs={{4,32},{5,33},{6,48},{7,49},{20,34},{21,35},{22,50},{23,51},{8,72}... | collective-permute-start | bytes 1572872 | tf_op jit(solution)/shard_map/ppermute | solution.py:273
  58.5 20.2 %collective-permute-start.3 = (bf16[256,512]{1,0:T(8,128)(2,1)S(1)}, bf16[256,512]{1,0:T(8,128)(2,1)S(1)}, u32[]{:S(2)}, u32[]{:S(2)}) collective-permute-start(bf16[256,512]{1,0:T(8,128)(2,1)S(1)} %get-tuple-element.29), channel_id=1, source_target_pairs={{4,33},{5,32},{6,49},{7,48},{20,35},{21,34},{22,51},{23,50},{8,65}... | collective-permute-start | bytes 786440 | tf_op jit(solution)/shard_map/ppermute | solution.py:273
  61.6 17.2 %collective-permute-start.4 = (bf16[256,512]{1,0:T(8,128)(2,1)S(1)}, bf16[256,512]{1,0:T(8,128)(2,1)S(1)}, u32[]{:S(2)}, u32[]{:S(2)}) collective-permute-start(bf16[256,512]{1,0:T(8,128)(2,1)S(1)} %get-tuple-element.30), channel_id=1, source_target_pairs={{4,33},{5,32},{6,49},{7,48},{20,35},{21,34},{22,51},{23,50},{8,73}... | collective-permute-start | bytes 786440 | tf_op jit(solution)/shard_map/ppermute | solution.py:273
  62.9 31.5 %collective-permute-start.2 = (bf16[512,512]{1,0:T(8,128)(2,1)S(1)}, bf16[512,512]{1,0:T(8,128)(2,1)}, u32[]{:S(2)}, u32[]{:S(2)}) collective-permute-start(bf16[512,512]{1,0:T(8,128)(2,1)S(1)} %get-tuple-element.28), channel_id=1, source_target_pairs={{0,0},{1,1},{2,16},{3,17},{16,2},{17,3},{18,18},{19,19},{36,36},{3... | collective-permute-start | bytes 1572872 | tf_op jit(solution)/shard_map/ppermute | solution.py:273
  64.4 30.0 %collective-permute-start.6 = (bf16[512,512]{1,0:T(8,128)(2,1)}, bf16[512,512]{1,0:T(8,128)(2,1)}, u32[]{:S(2)}, u32[]{:S(2)}) collective-permute-start(bf16[512,512]{1,0:T(8,128)(2,1)} %get-tuple-element.33), channel_id=1, source_target_pairs={{0,1},{1,0},{2,17},{3,16},{16,3},{17,2},{18,19},{19,18},{36,37},{3... | collective-permute-start | bytes 1572872 | tf_op jit(solution)/shard_map/ppermute | solution.py:273
  70.8 23.6 %collective-permute-start.1 = (bf16[512,512]{1,0:T(8,128)(2,1)S(1)}, bf16[512,512]{1,0:T(8,128)(2,1)}, u32[]{:S(2)}, u32[]{:S(2)}) collective-permute-start(bf16[512,512]{1,0:T(8,128)(2,1)S(1)} %collective-permute-done.refs_0_), channel_id=1, source_target_pairs={{72,64},{73,65},{74,80},{75,81},{88,66},{89,67},{90,82},{91,83},{1... | collective-permute-start | bytes 1572872 | tf_op jit(solution)/shard_map/ppermute | solution.py:273
  78.8 15.6 %collective-permute-start.5 = (bf16[256,512]{1,0:T(8,128)(2,1)S(1)}, bf16[256,512]{1,0:T(8,128)(2,1)S(1)}, u32[]{:S(2)}, u32[]{:S(2)}) collective-permute-start(bf16[256,512]{1,0:T(8,128)(2,1)S(1)} %collective-permute-done.4.refs_4_), channel_id=1, source_target_pairs={{72,64},{73,65},{74,80},{75,81},{88,66},{89,67},{90,82},{91,83},{1... | collective-permute-start | bytes 786440 | tf_op jit(solution)/shard_map/ppermute | solution.py:273

commit v14 on v13

--- a/solution.py
+++ b/solution.py
@@ -143,7 +143,7 @@
             in_specs=[strip, strip, pl.BlockSpec((2, rows, virt), lambda r, s: (0, r, 0))],
             out_specs=[strip, strip, whole((rows, virt)), whole((rows, virt))],
         ),
-        compiler_params=params(16),
+        compiler_params=params(52),
         cost_estimate=pl.CostEstimate(
             flops=0, bytes_accessed=16 * part_a.size, transcendentals=0
         ),

time: 101 us -> 102 us (level)
  transfers between devices with their start and end apart: 9 -> 9, of which waited for: 3 -> 3; matrix products, arithmetic and copies ran while one was open for 1% -> 1% of each run, Pallas kernels for 33% -> 32%
where the time goes in v14:
time: 102 us; the launch traced here: 101 us
  Pallas kernels  42.3 us (41%)
  starting transfers between devices  28.8 us (28%)
  waiting for transfers between devices  26.6 us (26%)
  local copies, waits for them, and re-layouts  2.42 us (2%)
    pallas_call x2, Pallas kernels, ladder(): pl.pallas_call(ladder_kernel, out_shape=jax.ShapeDtypeStruct((virt, virt)...  32.6 us
    ppermute x7, waiting for transfers between devices, send(): return lax.ppermute(array, AXES, pairs)  26.6 us
    ppermute x7, starting transfers between devices, send(): return lax.ppermute(array, AXES, pairs)  14.2 us
    all_to_all x1, starting transfers between devices, shards(): slices = lax.all_to_all(slices, 'occj', 0, 0, tiled=True)  7.38 us
    all_to_all x1, starting transfers between devices, shards(): sums = lax.all_to_all(sums, 'occj', 0, 0, tiled=True)  7.23 us
    pallas_call x1, Pallas kernels, finish(): pl.pallas_call(finish_kernel, out_shape=[jax.ShapeDtypeStruct(amps.shape,...  5.83 us
  transfers between devices with their start and end apart: 9, of which 3 were waited for; matrix products, arithmetic and copies ran while one was open for 1% of the time, Pallas kernels for 32%

profile of v14, /device:TPU:36, one launch (start us, length us, event | category | flops | bytes accessed | tf_op | source)
XLA Modules:
  0.0 101.2 jit_solution(11724108699651986267)
XLA Ops:
  0.7 7.4 %all-to-all-start = ((bf16[16,64,512]{2,1,0:T(8,128)(2,1)}), bf16[16,64,512]{2,1,0:T(8,128)(2,1)S(1)}, u32[]{:S(2)}, u32[]{:S(2)}) async-start(bf16[16,64,512]{2,1,0:T(8,128)(2,1)} %bitcast.25), calls=%async_computation | async-start | bytes 2097152 | tf_op jit(solution)/shard_map/all_to_all | solution.py:284
  8.1 0.1 convert_reduce_fusion
  8.2 0.1 copy.21
  8.3 0.1 broadcast_in_dim.7
  8.4 0.1 reshape.78
  8.5 0.1 copy.22
  8.7 0.1 compare_select_fusion.w_ref
  8.8 0.1 stack.19.ids
  8.9 16.3 %ladder.2.part_a = f32[512,512]{1,0:T(8,128)} custom-call(s32[1]{0:T(128)} %bitcast.1.slot, bf16[2,512,512]{2,1,0:T(8,128)(2,1)} %bitcast.26, bf16[2,512,512]{2,1,0:T(8,128)(2,1)} %bitcast.31, bf16[512,2048]{1,0:T(8,128)(2,1)} %x_ref.3, bf16[2048,2048]{1,0:T(8,128)(2,1)} %core_ref.3, bf16[512,512]{1,0:T(8,128)(2,1)} %fock_ref.3), custom_call_target="tpu_custom_call" | custom-call | flops 11005853696 | bytes 12582912 | tf_op jit(solution)/shard_map/ladder/pallas_call | solution.py:92
  25.2 0.0 all-to-all-done.in_ref
  25.2 2.0 %mix.1 = bf16[16,64,512]{2,1,0:T(8,128)(2,1)} custom-call(f32[256,256]{1,0:T(8,128)S(1)} %compare_select_fusion.w_ref, bf16[16,64,512]{2,1,0:T(8,128)(2,1)S(1)} %all-to-all-done.in_ref), custom_call_target="tpu_custom_call" | custom-call | flops 1000000000 | bytes 2097152 | tf_op jit(solution)/shard_map/mix/pallas_call | solution.py:50
  27.1 7.2 %all-to-all-start.1 = ((bf16[16,64,512]{2,1,0:T(8,128)(2,1)}), bf16[16,64,512]{2,1,0:T(8,128)(2,1)S(1)}, u32[]{:S(2)}, u32[]{:S(2)}) async-start(bf16[16,64,512]{2,1,0:T(8,128)(2,1)} %mix.1), calls=%async_computation.1 | async-start | bytes 2097152 | tf_op jit(solution)/shard_map/all_to_all | solution.py:293
  34.3 16.3 %ladder.3.part_b = f32[512,512]{1,0:T(8,128)} custom-call(s32[1]{0:T(128)} %sub.13.slot, bf16[2,512,512]{2,1,0:T(8,128)(2,1)} %bitcast.27, bf16[2,512,512]{2,1,0:T(8,128)(2,1)} %bitcast.32, bf16[512,2048]{1,0:T(8,128)(2,1)} %x_ref.3, bf16[2048,2048]{1,0:T(8,128)(2,1)} %core_ref.3, bf16[512,512]{1,0:T(8,128)(2,1)} %fock_ref.3), custom_call_target="tpu_custom_call" | custom-call | flops 11005853696 | bytes 12582912 | tf_op jit(solution)/shard_map/ladder/pallas_call | solution.py:92
  50.7 0.0 all-to-all-done.1
  50.7 1.0 copy-done.2
  51.6 2.0 %half.1 = (bf16[512,512]{1,0:T(8,128)(2,1)S(1)}, bf16[512,512]{1,0:T(8,128)(2,1)S(1)}, bf16[256,512]{1,0:T(8,128)(2,1)S(1)}, bf16[256,512]{1,0:T(8,128)(2,1)S(1)}) custom-call(s32[1]{0:T(128)} %bitcast.1.slot, f32[512,512]{1,0:T(8,128)} %ladder.2.part_a, f32[512,512]{1,0:T(8,128)} %ladder.3.part_b, bf16[2,512,512]{2,1,0:T(8,128)(2,1)} %bitcast.23), custom_call_target="tpu_custom_call" | custom-call | bytes 4194304 | tf_op jit(solution)/shard_map/half/pallas_call | solution.py:137
  53.6 5.1 %collective-permute-start = (bf16[512,512]{1,0:T(8,128)(2,1)S(1)}, bf16[512,512]{1,0:T(8,128)(2,1)S(1)}, u32[]{:S(2)}, u32[]{:S(2)}) collective-permute-start(bf16[512,512]{1,0:T(8,128)(2,1)S(1)} %get-tuple-element.28), channel_id=1, source_target_pairs={{4,32},{5,33},{6,48},{7,49},{20,34},{21,35},{22,50},{23,51},{8,72}... | collective-permute-start | bytes 1572872 | tf_op jit(solution)/shard_map/ppermute | solution.py:273
  58.7 3.1 %collective-permute-start.3 = (bf16[256,512]{1,0:T(8,128)(2,1)S(1)}, bf16[256,512]{1,0:T(8,128)(2,1)S(1)}, u32[]{:S(2)}, u32[]{:S(2)}) collective-permute-start(bf16[256,512]{1,0:T(8,128)(2,1)S(1)} %get-tuple-element.29), channel_id=1, source_target_pairs={{4,33},{5,32},{6,49},{7,48},{20,35},{21,34},{22,51},{23,50},{8,65}... | collective-permute-start | bytes 786440 | tf_op jit(solution)/shard_map/ppermute | solution.py:273
  61.8 1.3 %collective-permute-start.4 = (bf16[256,512]{1,0:T(8,128)(2,1)S(1)}, bf16[256,512]{1,0:T(8,128)(2,1)S(1)}, u32[]{:S(2)}, u32[]{:S(2)}) collective-permute-start(bf16[256,512]{1,0:T(8,128)(2,1)S(1)} %get-tuple-element.30), channel_id=1, source_target_pairs={{4,33},{5,32},{6,49},{7,48},{20,35},{21,34},{22,51},{23,50},{8,73}... | collective-permute-start | bytes 786440 | tf_op jit(solution)/shard_map/ppermute | solution.py:273
  63.1 0.7 collective-permute-start.2
  63.8 1.5 %collective-permute-start.6 = (bf16[512,512]{1,0:T(8,128)(2,1)S(1)}, bf16[512,512]{1,0:T(8,128)(2,1)}, u32[]{:S(2)}, u32[]{:S(2)}) collective-permute-start(bf16[512,512]{1,0:T(8,128)(2,1)S(1)} %get-tuple-element.33), channel_id=1, source_target_pairs={{0,1},{1,0},{2,17},{3,16},{16,3},{17,2},{18,19},{19,18},{36,37},{3... | collective-permute-start | bytes 1572872 | tf_op jit(solution)/shard_map/ppermute | solution.py:273
  65.3 5.7 %collective-permute-done.refs_0_ = bf16[512,512]{1,0:T(8,128)(2,1)S(1)} collective-permute-done((bf16[512,512]{1,0:T(8,128)(2,1)S(1)}, bf16[512,512]{1,0:T(8,128)(2,1)S(1)}, u32[]{:S(2)}, u32[]{:S(2)}) %collective-permute-start) | collective-permute-done | bytes 524320 | tf_op jit(solution)/shard_map/ppermute | solution.py:273
  71.0 1.3 %collective-permute-start.1 = (bf16[512,512]{1,0:T(8,128)(2,1)S(1)}, bf16[512,512]{1,0:T(8,128)(2,1)}, u32[]{:S(2)}, u32[]{:S(2)}) collective-permute-start(bf16[512,512]{1,0:T(8,128)(2,1)S(1)} %collective-permute-done.refs_0_), channel_id=1, source_target_pairs={{72,64},{73,65},{74,80},{75,81},{88,66},{89,67},{90,82},{91,83},{1... | collective-permute-start | bytes 1572872 | tf_op jit(solution)/shard_map/ppermute | solution.py:273
  72.3 6.7 %collective-permute-done.3.refs_3_ = bf16[256,512]{1,0:T(8,128)(2,1)S(1)} collective-permute-done((bf16[256,512]{1,0:T(8,128)(2,1)S(1)}, bf16[256,512]{1,0:T(8,128)(2,1)S(1)}, u32[]{:S(2)}, u32[]{:S(2)}) %collective-permute-start.3) | collective-permute-done | bytes 262176 | tf_op jit(solution)/shard_map/ppermute | solution.py:273
  79.0 0.0 collective-permute-done.4.refs_4_
  79.0 1.3 %collective-permute-start.5 = (bf16[256,512]{1,0:T(8,128)(2,1)S(1)}, bf16[256,512]{1,0:T(8,128)(2,1)S(1)}, u32[]{:S(2)}, u32[]{:S(2)}) collective-permute-start(bf16[256,512]{1,0:T(8,128)(2,1)S(1)} %collective-permute-done.4.refs_4_), channel_id=1, source_target_pairs={{72,64},{73,65},{74,80},{75,81},{88,66},{89,67},{90,82},{91,83},{1... | collective-permute-start | bytes 786440 | tf_op jit(solution)/shard_map/ppermute | solution.py:273
  80.3 0.1 copy.23.col_ref
  80.4 14.1 %collective-permute-done.5.refs_5_ = bf16[256,512]{1,0:T(8,128)(2,1)S(1)} collective-permute-done((bf16[256,512]{1,0:T(8,128)(2,1)S(1)}, bf16[256,512]{1,0:T(8,128)(2,1)S(1)}, u32[]{:S(2)}, u32[]{:S(2)}) %collective-permute-start.5) | collective-permute-done | bytes 262176 | tf_op jit(solution)/shard_map/ppermute | solution.py:273
  94.6 0.0 collective-permute-done.6.refs_6_
  94.6 0.0 collective-permute-done.1.refs_1_
  94.6 0.8 copy-done.3
  95.4 5.8 %finish.1 = (f32[2,512,512]{2,1,0:T(8,128)}, bf16[2,512,512]{2,1,0:T(8,128)(2,1)}) custom-call(s32[6]{0:T(128)S(1)} %stack.19.ids, f32[512,512]{1,0:T(8,128)} %ladder.2.part_a, f32[512,512]{1,0:T(8,128)} %ladder.3.part_b, bf16[2,512,512]{2,1,0:T(8,128)(2,1)} %bitcast.24, bf16[2,512,512]{2,1,0:T(8,128)(2,1)} %bitcast.28, f32[512,1]{1,0:T(8,128)S(1)} %copy.23.col_ref, ...), custom_call_target="tpu_custom_call" | custom-call | flops 10485760 | bytes 7340032 | tf_op jit(solution)/shard_map/finish/pallas_call | solution.py:198
  (17 shorter events, 0.1 us)
Async XLA Ops:
  0.6 7.4 %copy-start.6 = (s32[16]{0:T(128)S(1)}, s32[16]{0:T(128)}, u32[]{:S(2)}) copy-start(s32[16]{0:T(128)} %param.19) | copy-start | bytes 196
  0.6 7.5 %copy-start.5 = (s32[16,6]{0,1:T(8,128)S(1)}, s32[16,6]{0,1:T(8,128)}, u32[]{:S(2)}) copy-start(s32[16,6]{0,1:T(8,128)} %param.18) | copy-start | bytes 1156
  0.7 7.6 %copy-start.4 = (f32[16,16]{1,0:T(8,128)S(1)}, f32[16,16]{1,0:T(8,128)}, u32[]{:S(2)}) copy-start(f32[16,16]{1,0:T(8,128)} %param.17) | copy-start | bytes 3076
  0.7 24.5 %all-to-all-start = ((bf16[16,64,512]{2,1,0:T(8,128)(2,1)}), bf16[16,64,512]{2,1,0:T(8,128)(2,1)S(1)}, u32[]{:S(2)}, u32[]{:S(2)}) async-start(bf16[16,64,512]{2,1,0:T(8,128)(2,1)} %bitcast.25), calls=%async_computation | async-start | bytes 2097152 | tf_op jit(solution)/shard_map/all_to_all | solution.py:284
  27.1 23.6 %all-to-all-start.1 = ((bf16[16,64,512]{2,1,0:T(8,128)(2,1)}), bf16[16,64,512]{2,1,0:T(8,128)(2,1)S(1)}, u32[]{:S(2)}, u32[]{:S(2)}) async-start(bf16[16,64,512]{2,1,0:T(8,128)(2,1)} %mix.1), calls=%async_computation.1 | async-start | bytes 2097152 | tf_op jit(solution)/shard_map/all_to_all | solution.py:293
  50.7 29.6 %copy-start = (f32[512]{0:T(512)S(1)}, f32[512]{0:T(512)}, u32[]{:S(2)}) copy-start(f32[512]{0:T(512)} %param.15) | copy-start | bytes 6148
  50.7 44.7 %copy-start.1 = (f32[16]{0:T(128)S(1)}, f32[16]{0:T(128)}, u32[]{:S(2)}) copy-start(f32[16]{0:T(128)} %occ_ref.1) | copy-start | bytes 196
  50.7 1.0 copy-start.2
  53.6 17.4 %collective-permute-start = (bf16[512,512]{1,0:T(8,128)(2,1)S(1)}, bf16[512,512]{1,0:T(8,128)(2,1)S(1)}, u32[]{:S(2)}, u32[]{:S(2)}) collective-permute-start(bf16[512,512]{1,0:T(8,128)(2,1)S(1)} %get-tuple-element.28), channel_id=1, source_target_pairs={{4,32},{5,33},{6,48},{7,49},{20,34},{21,35},{22,50},{23,51},{8,72}... | collective-permute-start | bytes 1572872 | tf_op jit(solution)/shard_map/ppermute | solution.py:273
  58.7 20.2 %collective-permute-start.3 = (bf16[256,512]{1,0:T(8,128)(2,1)S(1)}, bf16[256,512]{1,0:T(8,128)(2,1)S(1)}, u32[]{:S(2)}, u32[]{:S(2)}) collective-permute-start(bf16[256,512]{1,0:T(8,128)(2,1)S(1)} %get-tuple-element.29), channel_id=1, source_target_pairs={{4,33},{5,32},{6,49},{7,48},{20,35},{21,34},{22,51},{23,50},{8,65}... | collective-permute-start | bytes 786440 | tf_op jit(solution)/shard_map/ppermute | solution.py:273
  61.8 17.2 %collective-permute-start.4 = (bf16[256,512]{1,0:T(8,128)(2,1)S(1)}, bf16[256,512]{1,0:T(8,128)(2,1)S(1)}, u32[]{:S(2)}, u32[]{:S(2)}) collective-permute-start(bf16[256,512]{1,0:T(8,128)(2,1)S(1)} %get-tuple-element.30), channel_id=1, source_target_pairs={{4,33},{5,32},{6,49},{7,48},{20,35},{21,34},{22,51},{23,50},{8,73}... | collective-permute-start | bytes 786440 | tf_op jit(solution)/shard_map/ppermute | solution.py:273
  63.1 31.5 %collective-permute-start.2 = (bf16[512,512]{1,0:T(8,128)(2,1)S(1)}, bf16[512,512]{1,0:T(8,128)(2,1)S(1)}, u32[]{:S(2)}, u32[]{:S(2)}) collective-permute-start(bf16[512,512]{1,0:T(8,128)(2,1)S(1)} %get-tuple-element.28), channel_id=1, source_target_pairs={{0,0},{1,1},{2,16},{3,17},{16,2},{17,3},{18,18},{19,19},{36,36},{3... | collective-permute-start | bytes 1572872 | tf_op jit(solution)/shard_map/ppermute | solution.py:273
  63.8 30.8 %collective-permute-start.6 = (bf16[512,512]{1,0:T(8,128)(2,1)S(1)}, bf16[512,512]{1,0:T(8,128)(2,1)}, u32[]{:S(2)}, u32[]{:S(2)}) collective-permute-start(bf16[512,512]{1,0:T(8,128)(2,1)S(1)} %get-tuple-element.33), channel_id=1, source_target_pairs={{0,1},{1,0},{2,17},{3,16},{16,3},{17,2},{18,19},{19,18},{36,37},{3... | collective-permute-start | bytes 1572872 | tf_op jit(solution)/shard_map/ppermute | solution.py:273
  71.0 23.6 %collective-permute-start.1 = (bf16[512,512]{1,0:T(8,128)(2,1)S(1)}, bf16[512,512]{1,0:T(8,128)(2,1)}, u32[]{:S(2)}, u32[]{:S(2)}) collective-permute-start(bf16[512,512]{1,0:T(8,128)(2,1)S(1)} %collective-permute-done.refs_0_), channel_id=1, source_target_pairs={{72,64},{73,65},{74,80},{75,81},{88,66},{89,67},{90,82},{91,83},{1... | collective-permute-start | bytes 1572872 | tf_op jit(solution)/shard_map/ppermute | solution.py:273
  79.0 15.6 %collective-permute-start.5 = (bf16[256,512]{1,0:T(8,128)(2,1)S(1)}, bf16[256,512]{1,0:T(8,128)(2,1)S(1)}, u32[]{:S(2)}, u32[]{:S(2)}) collective-permute-start(bf16[256,512]{1,0:T(8,128)(2,1)S(1)} %collective-permute-done.4.refs_4_), channel_id=1, source_target_pairs={{72,64},{73,65},{74,80},{75,81},{88,66},{89,67},{90,82},{91,83},{1... | collective-permute-start | bytes 786440 | tf_op jit(solution)/shard_map/ppermute | solution.py:273
  94.6 0.8 copy-start.3
